TPU v7x, 32 devices: a whole 2x2x4 slice. The times are simulated.
32 devices in a mesh: grp: 2 (over x), col: 16 (over z, y, core).
Axes of the slice: x: 2, y: 2, z: 4, core: 2. Of those that a mesh axis runs over, the one named last changes fastest.
Arguments:
- mode_rows: float32 [16384, 256], P(('grp', 'col')), parts along dimension 0, may hold values from -8 to 8, as said below
- coeffs: bfloat16 [512, 256], P(('grp', 'col')), parts along dimension 0, may hold values from -18 to 18, as said below
- diffusivity: float32 [32, 64], P(('grp', 'col')), parts along dimension 0, may hold values from 0.02 to 0.24
- counts: int32 [32], P(('grp', 'col')), parts along dimension 0, may hold values from 32 to 64
- emis_idx: int32 [512], P('grp'), parts along dimension 0, may hold values from 0 to 15
- emis_table: float32 [16, 8], replicated, may hold values from 0.2 to 1.5
- reactants: int32 [12, 2], replicated, may hold values from 0 to 7
- stoich: int32 [12, 8], replicated, may hold values from -1 to 1
- rate_consts: float32 [12], replicated, may hold values from 0.02 to 0.2
- loss_rates: float32 [8], replicated, may hold values from 0.2 to 2
Outputs:
- modes_out: float32 [16384, 256], P(('grp', 'col')), parts along dimension 0
- coeffs_out: bfloat16 [512, 256], P(('grp', 'col')), parts along dimension 0
There are 2 independent parts, one for each index of `grp`. A program takes and returns all parts, laid end to end along the dimension named above; an argument that names none is the same for every part. Nothing has to cross between parts.
Inputs may be any that keep to these rules, and one draw needn't show every extreme that they name: `mode_rows`: modes of order one. `coeffs`: coefficients of order one.
All inputs are finite; a program needn't handle non-finite values.
Results may differ from a plain program's by a relative error of at most 0.0014.
The roundings to bfloat16 on the way count: a program that leaves them out, or rounds other values in their place, can miss the bound.
Values may be sent and summed in bfloat16 or wider, within the bound.
No kernel may reach another device: no remote copies, remote signals or barrier semaphores. Data moves between devices by JAX's collectives and lax.ppermute only.
A program may use at most 64 MiB of HBM per device.

v0:
```python
import math

import jax
import jax.numpy as jnp
from jax import lax
from jax.sharding import PartitionSpec as P

S = 8
LEV = 64
R = 256
NEMIS = 16
NSUB = 2


TIME_STEP = 0.1
RATE_STEP = 0.3
RIDGE_SHARE = 0.05
PRECISE = lax.Precision.HIGHEST


def diffuse(mode_block, diffusivity, counts):
    ncols = counts.shape[0]
    rank = mode_block.shape[1]
    blocked = mode_block.reshape(ncols, S, LEV, rank)
    level_index = jnp.arange(LEV, dtype=jnp.int32)
    face_coef = jnp.where(
        level_index[None, :] + 1 < counts[:, None], diffusivity, jnp.zeros_like(diffusivity)
    )
    upper_cells = jnp.concatenate([blocked[:, :, 1:], jnp.zeros_like(blocked[:, :, :1])], axis=2)
    face_flux = face_coef[:, None, :, None] * (upper_cells - blocked)
    lower_flux = jnp.concatenate(
        [jnp.zeros_like(face_flux[:, :, :1]), face_flux[:, :, :-1]], axis=2
    )
    return (blocked + face_flux - lower_flux).reshape(mode_block.shape)


def species_pick(table_column):
    return (table_column[:, None] == jnp.arange(S, dtype=jnp.int32)[None, :]).astype(jnp.float32)


def reaction(
    field_block,
    pick_first,
    pick_second,
    stoich_wide,
    rate_consts,
    loss_rates,
    emis_block,
    active,
    profile,
):
    first_amount = jnp.einsum("rs,bcsl->bcrl", pick_first, field_block, precision=PRECISE)
    second_amount = jnp.einsum("rs,bcsl->bcrl", pick_second, field_block, precision=PRECISE)
    reaction_speed = rate_consts[None, None, :, None] * first_amount * second_amount
    produced = jnp.einsum("rs,bcrl->bcsl", stoich_wide, reaction_speed, precision=PRECISE)
    tendency_raw = (
        produced
        - loss_rates[None, None, :, None] * field_block
        + emis_block[:, None, :, None] * profile[None, None, None, :]
    )
    return tendency_raw * active[None, :, None, :]


def on_device(
    mode_rows,
    coeffs,
    diffusivity,
    counts,
    emis_idx,
    emis_table,
    reactants,
    stoich,
    rate_consts,
    loss_rates,
):
    rows_dev = mode_rows.shape[0]
    mem_dev = coeffs.shape[0]
    col_count = lax.axis_size("col")
    total_rows = rows_dev * col_count
    members = mem_dev * col_count
    columns_dev = counts.shape[0]
    level_index = jnp.arange(LEV, dtype=jnp.int32)
    active = (level_index[None, :] < counts[:, None]).astype(jnp.float32)
    profile = jnp.exp(-4.0 * level_index.astype(jnp.float32) / LEV)
    chosen = (emis_idx[:, None] == jnp.arange(NEMIS, dtype=jnp.int32)[None, :]).astype(jnp.float32)
    member_emis = jnp.sum(chosen[:, :, None] * emis_table[None, :, :], axis=1)
    pick_first = species_pick(reactants[:, 0])
    pick_second = species_pick(reactants[:, 1])
    stoich_wide = stoich.astype(jnp.float32)
    rank_root = math.sqrt(R)
    inv_root = 1.0 / rank_root
    block_rows = math.gcd(members, 128)
    block_count = members // block_rows
    modes = mode_rows
    for substep in range(NSUB):
        diffused = diffuse(modes, diffusivity, counts)
        mode_bf = diffused.astype(jnp.bfloat16)
        rate_scale = rank_root / total_rows
        coef_gathered = lax.all_gather(coeffs, "col", axis=0, tiled=True)

        def member_block(pulled, block_inputs):
            coef_block, emis_block = block_inputs
            field_block = (
                lax.dot_general(
                    coef_block,
                    mode_bf,
                    (((1,), (1,)), ((), ())),
                    preferred_element_type=jnp.float32,
                )
                * inv_root
            )
            tendency = reaction(
                field_block.reshape(block_rows, columns_dev, S, LEV),
                pick_first,
                pick_second,
                stoich_wide,
                rate_consts,
                loss_rates,
                emis_block,
                active,
                profile,
            )
            tendency = tendency.reshape(block_rows, rows_dev).astype(jnp.bfloat16)
            pulled = pulled + lax.dot_general(
                tendency, coef_block, (((0,), (0,)), ((), ())), preferred_element_type=jnp.float32
            )
            part_rate = jnp.dot(tendency, mode_bf, preferred_element_type=jnp.float32)
            return (pulled, part_rate)

        pulled, rate_blocks = lax.scan(
            member_block,
            jnp.zeros((rows_dev, R), jnp.float32),
            (
                coef_gathered.reshape(block_count, block_rows, R),
                member_emis.reshape(block_count, block_rows, S),
            ),
        )
        pulled, rate_term = (pulled, rate_blocks.reshape(members, R))
        rate_mine = lax.psum_scatter(rate_term, "col", scatter_dimension=0, tiled=True) * rate_scale
        coef_wide = coeffs.astype(jnp.float32)
        gram_part = jnp.dot(coef_wide.T, coef_wide, precision=PRECISE)
        proj_part = lax.dot_general(
            mode_bf.astype(jnp.float32), pulled, (((0,), (0,)), ((), ())), precision=PRECISE
        )
        gram_matrix, proj_matrix = lax.psum((gram_part, proj_part), "col")
        proj_matrix = proj_matrix / total_rows
        gram_matrix = gram_matrix + RIDGE_SHARE * members * jnp.eye(R, dtype=jnp.float32)
        remainder = pulled - jnp.dot(diffused, proj_matrix, precision=PRECISE)
        factor = jnp.linalg.cholesky(gram_matrix)
        solved = jax.scipy.linalg.cho_solve((factor, True), remainder.T).T
        modes = diffused + TIME_STEP * rank_root * solved
        coeffs = (coef_wide + RATE_STEP * rate_mine).astype(jnp.bfloat16)
    return (modes, coeffs)


def solution(mesh):
    placed = (
        P(("grp", "col"), None),
        P(("grp", "col"), None),
        P(("grp", "col"), None),
        P(("grp", "col")),
        P("grp"),
        P(),
        P(),
        P(),
        P(),
        P(),
    )
    return jax.shard_map(
        on_device,
        mesh=mesh,
        in_specs=placed,
        out_specs=(P(("grp", "col"), None), P(("grp", "col"), None)),
        check_vma=False,
    )
```

profile of v0, /device:TPU:0, one launch (start us, length us, event | category | flops | bytes accessed | tf_op | source)
XLA Modules:
  0.0 393.3 jit_solution(5223242467514382098)
XLA Ops:
  7.2 23.7 %all_gather.6 = bf16[256,256]{1,0:T(8,128)(2,1)S(1)} all-gather(bf16[16,256]{1,0:T(8,128)(2,1)} %param.18), channel_id=1, replica_groups=mesh['grp'=2,'col'=16] {'col'}, dimensions={0}, use_global_device_ids=true | all-gather | bytes 139264 | tf_op jit(solution)/shard_map/all_gather | solution.py:99
  30.9 0.9 fusion.102
  31.9 1.2 slice.80
  33.7 0.6 copy-done.14
  34.7 0.7 copy-done.13
  35.3 0.7 copy-done.12
  36.0 0.7 copy-done.10
  36.8 0.6 copy-done.11
  37.5 0.6 copy-done.8
  38.2 7.1 %while.30 = (s32[]{:T(128)}, f32[512,256]{1,0:T(8,128)S(1)}, f32[2,128,256]{2,1,0:T(8,128)S(1)}, f32[12]{0:T(128)S(1)}, bf16[2,128,256]{2,1,0:T(8,128)(2,1)S(1)}...) while((s32[]{:T(128)}, f32[512,256]{1,0:T(8,128)S(1)}, ...), condition=%wide.region_7.9_spmd.clone, body=%wide.region_6.8_spmd.clone.sunk | while | flops 129892992 | bytes 5650131 | solution.py:130
  38.5 0.7 convolution_bitcast_fusion.10
  39.2 0.7 fusion.186
  39.9 0.7 fusion.187
  42.1 0.7 convolution_bitcast_fusion.10
  42.7 0.7 fusion.186
  43.5 0.7 fusion.187
  44.1 0.5 fusion.188
  45.3 1.2 fusion.103
  46.5 0.7 reduce-scatter.3.cloned.1.call-update
  47.2 0.6 all-reduce.10.cloned.1.call-start
  48.0 86.0 %all-reduce.12.cloned.1.call-done = (f32[256,256]{1,0:T(8,128)}, f32[256,256]{0,1:T(8,128)}) async-done(((f32[256,256]{1,0:T(8,128)}, f32[256,256]{0,1:T(8,128)}), (f32[256,256]{1,0:T(8,128)}, f32[256,256]{0,1:T(8,128)})) %all-reduce.12.cloned.1.call-update) | async-done | bytes 524304 | tf_op jit(solution)/shard_map/psum | solution.py:145
  134.0 1.0 select_add_fusion.1
  135.1 0.8 copy-done.1
  136.0 11.7 %cholesky.130 = f32[128,128]{1,0:T(8,128)S(1)} custom-call(f32[128,128]{1,0:T(8,128)S(1)} %cholesky.194), custom_call_target="Cholesky" | custom-call | tf_op jit(solution)/shard_map/jit(cholesky)/cholesky | solution.py:149
  147.7 9.8 %custom-call.17 = f32[1,128,128]{1,2,0:T(8,128)S(1)} custom-call(f32[1,128,128]{2,1,0:T(8,128)S(1)} %get-tuple-element.369), custom_call_target="InvertDiagBlocksLowerTriangular" | custom-call | tf_op jit(solution)/shard_map/jit(cholesky)/cholesky | solution.py:149
  158.1 11.7 %cholesky.147 = f32[128,128]{1,0:T(8,128)S(1)} custom-call(f32[128,128]{1,0:T(8,128)S(1)} %convolution_subtract_fusion.7), custom_call_target="Cholesky" | custom-call | tf_op jit(solution)/shard_map/jit(cholesky)/cholesky | solution.py:149
  169.8 0.6 compare_reduce_fusion.2
  171.8 4.0 %while.32 = (s32[]{:T(128)}, f32[256,256]{1,0:T(8,128)S(1)}, s32[2,2]{1,0:T(2,128)S(1)}, f32[2,128,128]{2,1,0:T(8,128)S(1)}, s32[]{:T(128)}) while((s32[]{:T(128)}, f32[256,256]{1,0:T(8,128)S(1)}, s32[2,2]{1,0:T(2,128)S(1)}, f32[2,128,128]{2,1,0:T(8,128)S(1)}, s32[]{:T(128)}) %tuple.90), condition=%wide.while_cond, body=%wide.while_body.sunk | while | flops 2 | bytes 131181 | solution.py:150
  172.0 0.6 fusion.206
  172.6 1.3 bitcast_dynamic-update-slice_fusion.4
  173.9 0.6 fusion.206
  174.5 1.3 bitcast_dynamic-update-slice_fusion.4
  175.8 19.7 %custom-call.18 = f32[2,128,128]{1,2,0:T(8,128)S(1)} custom-call(f32[2,128,128]{2,1,0:T(8,128)S(1)} %get-tuple-element.258), custom_call_target="InvertDiagBlocksLowerTriangular" | custom-call | tf_op jit(solution)/shard_map/jit(_cho_solve)/triangular_solve | solution.py:150
  195.5 0.6 fusion.65
  196.5 0.6 convolution_subtract_fusion.5
  199.4 0.7 add_convert_fusion.1
  200.2 21.3 %all_gather.7 = bf16[256,256]{1,0:T(8,128)(2,1)S(1)} all-gather(bf16[16,256]{1,0:T(8,128)(2,1)S(1)} %add_convert_fusion.1), channel_id=1, replica_groups=mesh['grp'=2,'col'=16] {'col'}, dimensions={0}, use_global_device_ids=true | all-gather | bytes 139264 | tf_op jit(solution)/shard_map/all_gather | solution.py:99
  221.4 0.9 fusion.104
  222.4 7.1 %while.31 = (s32[]{:T(128)}, f32[512,256]{1,0:T(8,128)S(1)}, f32[2,128,256]{2,1,0:T(8,128)S(1)}, f32[12]{0:T(128)S(1)}, bf16[2,128,256]{2,1,0:T(8,128)(2,1)S(1)}...) while((s32[]{:T(128)}, f32[512,256]{1,0:T(8,128)S(1)}, ...), condition=%wide.region_12.15_spmd.clone, body=%wide.region_11.14_spmd.clone.sunk | while | flops 129892992 | bytes 5650131 | solution.py:130
  222.8 0.7 convolution_bitcast_fusion.11
  223.4 0.7 fusion.202
  224.2 0.7 fusion.203
  226.3 0.7 convolution_bitcast_fusion.11
  227.0 0.7 fusion.202
  227.7 0.7 fusion.203
  229.5 1.2 fusion.105
  231.3 86.9 %all-reduce.10.cloned.1.call-done = (f32[256,256]{1,0:T(8,128)}, f32[256,256]{0,1:T(8,128)}) async-done(((f32[256,256]{1,0:T(8,128)}, f32[256,256]{0,1:T(8,128)}), (f32[256,256]{1,0:T(8,128)}, f32[256,256]{0,1:T(8,128)})) %all-reduce.10.cloned.1.call-update) | async-done | bytes 524304 | tf_op jit(solution)/shard_map/psum | solution.py:145
  318.2 1.0 select_add_fusion
  319.3 0.8 copy-done.2
  320.2 11.7 %cholesky.164 = f32[128,128]{1,0:T(8,128)S(1)} custom-call(f32[128,128]{1,0:T(8,128)S(1)} %cholesky.197), custom_call_target="Cholesky" | custom-call | tf_op jit(solution)/shard_map/jit(cholesky)/cholesky | solution.py:149
  332.0 9.8 %custom-call.19 = f32[1,128,128]{1,2,0:T(8,128)S(1)} custom-call(f32[1,128,128]{2,1,0:T(8,128)S(1)} %get-tuple-element.365), custom_call_target="InvertDiagBlocksLowerTriangular" | custom-call | tf_op jit(solution)/shard_map/jit(cholesky)/cholesky | solution.py:149
  342.3 11.7 %cholesky.181 = f32[128,128]{1,0:T(8,128)S(1)} custom-call(f32[128,128]{1,0:T(8,128)S(1)} %convolution_subtract_fusion.6), custom_call_target="Cholesky" | custom-call | tf_op jit(solution)/shard_map/jit(cholesky)/cholesky | solution.py:149
  354.0 0.7 compare_reduce_fusion
  354.7 0.6 compare_reduce_fusion.1
  356.8 4.4 %while.33 = (s32[]{:T(128)}, f32[256,256]{1,0:T(8,128)S(1)}, s32[2,2]{1,0:T(2,128)S(1)}, f32[2,128,128]{2,1,0:T(8,128)S(1)}, s32[]{:T(128)}) while((s32[]{:T(128)}, f32[256,256]{1,0:T(8,128)S(1)}, s32[2,2]{1,0:T(2,128)S(1)}, f32[2,128,128]{2,1,0:T(8,128)S(1)}, s32[]{:T(128)}) %tuple.120), condition=%wide.while_cond.clone, body=%wide.while_body.clone.sunk | while | flops 2 | bytes 131181 | solution.py:150
  357.1 0.6 fusion.207
  357.7 1.4 bitcast_dynamic-update-slice_fusion.5
  359.1 0.6 fusion.207
  359.7 1.4 bitcast_dynamic-update-slice_fusion.5
  361.2 19.7 %custom-call.20 = f32[2,128,128]{1,2,0:T(8,128)S(1)} custom-call(f32[2,128,128]{2,1,0:T(8,128)S(1)} %get-tuple-element.259), custom_call_target="InvertDiagBlocksLowerTriangular" | custom-call | tf_op jit(solution)/shard_map/jit(_cho_solve)/triangular_solve | solution.py:150
  380.8 0.6 fusion.64
  381.9 0.6 convolution_subtract_fusion.3
  384.2 1.0 copy.72
  385.2 1.3 add_convert_fusion
  (119 shorter events, 13.0 us)
Async XLA Ops:
  7.2 126.8 %all-reduce.12.cloned.1.call-start = ((), (), s32[]{:S(2)}) async-start(), calls=%async_computation.5 | async-start | bytes 1048576 | tf_op jit(solution)/shard_map/psum | solution.py:145
  7.2 23.7 %copy-start.7 = (bf16[16,256]{1,0:T(8,128)(2,1)S(1)}, bf16[16,256]{1,0:T(8,128)(2,1)}, u32[]{:S(2)}) copy-start(bf16[16,256]{1,0:T(8,128)(2,1)} %param.18) | copy-start | bytes 24580
  31.9 2.5 copy-start
  33.7 0.7 copy-start.14
  34.6 0.7 copy-start.13
  35.3 0.7 copy-start.12
  36.0 0.7 copy-start.10
  36.7 0.7 copy-start.11
  37.5 0.7 copy-start.8
  37.5 0.7 copy-start.9
  45.2 1.2 copy-start.3
  46.5 153.0 %reduce-scatter.3.cloned.1.call-start = ((), (), s32[]{:S(2)}) async-start(), calls=%async_computation.2 | async-start | bytes 278528 | tf_op jit(solution)/shard_map/reduce_scatter | solution.py:139
  47.2 271.0 %all-reduce.10.cloned.1.call-start = ((), (), s32[]{:S(2)}) async-start(), calls=%async_computation.4 | async-start | bytes 1048576 | tf_op jit(solution)/shard_map/psum | solution.py:145
  135.0 1.0 copy-start.1
  171.8 23.7 %copy-start.5 = (f32[256,256]{1,0:T(8,128)S(1)}, f32[256,256]{1,0:T(8,128)}, u32[]{:S(2)}) copy-start(f32[256,256]{1,0:T(8,128)} %get-tuple-element.356) | copy-start | bytes 786436
  229.5 1.2 copy-start.4
  230.7 154.5 %reduce-scatter.5.cloned.1.call-start = ((), (), s32[]{:S(2)}) async-start(), calls=%async_computation.3 | async-start | bytes 278528 | tf_op jit(solution)/shard_map/reduce_scatter | solution.py:139
  319.2 1.0 copy-start.2
  356.8 24.1 %copy-start.6 = (f32[256,256]{1,0:T(8,128)S(1)}, f32[256,256]{1,0:T(8,128)}, u32[]{:S(2)}) copy-start(f32[256,256]{1,0:T(8,128)} %get-tuple-element.354) | copy-start | bytes 786436
Sparse Core Ops, SparseCore 0:
  46.6 87.3 all-reduce.11
  137.5 56.2 reduce-scatter.2
  230.8 87.3 all-reduce.9
  321.6 56.2 reduce-scatter.4
where the time goes:
time: 398 us; the launch traced here: 393 us
  waiting for transfers between devices  174 us (44%)
  other arithmetic  116 us (29%)
  blocking collectives  44.9 us (11%)
  matrix products  22 us (6%)
  between operations  17.8 us (4%)
  local copies, waits for them, and re-layouts  17.3 us (4%)
    psum x2, waiting for transfers between devices, on_device(): gram_matrix, proj_matrix = lax.psum((gram_part, proj_part), 'col')  173 us
    another operation x13, other arithmetic, on_device(): factor = jnp.linalg.cholesky(gram_matrix)  68.6 us
    all_gather x2, blocking collectives, on_device(): coef_gathered = lax.all_gather(coeffs, 'col', axis=0, tiled=True)  44.9 us
    another operation x5, other arithmetic, on_device(): solved = jax.scipy.linalg.cho_solve((factor, True), remainder.T).T  39.4 us
  transfers between devices with their start and end apart: 4, of which 2 were waited for; matrix products, arithmetic and copies ran while one was open for 32% of the time, Pallas kernels for 0%

commit v1 on v0

v1 whole, which is shorter than its diff:
```python
import functools
import math

import jax
import jax.numpy as jnp
from jax import lax
from jax.experimental import pallas as pl
from jax.experimental.pallas import tpu as pltpu
from jax.sharding import PartitionSpec as P

S = 8
LEV = 64
R = 256
NREAC = 12
NEMIS = 16
NSUB = 2

TIME_STEP = 0.1
RATE_STEP = 0.3
RIDGE_SHARE = 0.05

F32 = jnp.float32
BF16 = jnp.bfloat16

NN = (((1,), (0,)), ((), ()))
NT = (((1,), (1,)), ((), ()))
TN = (((0,), (0,)), ((), ()))


def mm(a, b, dims=NN):
    return lax.dot_general(a, b, dims, preferred_element_type=F32)


def split(x):
    high = x.astype(BF16)
    return high, (x - high.astype(F32)).astype(BF16)


def mm3(a, b, dims=NN):
    return mm(a[0], b[0], dims) + (mm(a[0], b[1], dims) + mm(a[1], b[0], dims))


def diffuse_rows(modes, face_ref, counts_ref, columns):
    level = lax.broadcasted_iota(jnp.int32, (LEV, R), 0)
    faces = []
    for c in range(columns):
        face = jnp.broadcast_to(face_ref[:, c : c + 1], (LEV, R))
        faces += [jnp.where(level + 1 < counts_ref[c], face, 0.0)] * S
    face = jnp.concatenate(faces, axis=0)
    rows = modes.shape[0]
    flux = face * (pltpu.roll(modes, rows - 1, 0) - modes)
    return modes + flux - pltpu.roll(flux, 1, 0)


def react(
    diffused, coef_ref, emis_ref, counts_ref, pair_ref, stoich_ref, speed_ref, loss_ref,
    field_ref, tend_ref, rate_ref, columns,
):
    mode_bf = diffused.astype(BF16)
    members = coef_ref.shape[0]
    block = math.gcd(members, 256)
    step = 16
    steps = LEV // step
    for b in range(members // block):
        lanes = slice(b * block, (b + 1) * block)
        field_ref[...] = mm(mode_bf, coef_ref[lanes, :], NT) * (1.0 / math.sqrt(R))

        def part(i, _):
            c = i // steps
            low = (i - c * steps) * step
            base = c * (S * LEV) + low
            level = lax.broadcasted_iota(jnp.int32, (step, block), 0) + low
            profile = jnp.exp(level.astype(F32) * (-4.0 / LEV))
            live = level < counts_ref[c]

            def amount(s):
                return field_ref[pl.ds(pl.multiple_of(base + s * LEV, step), step), :]

            total = []
            for s in range(S):
                total.append(emis_ref[s : s + 1, lanes] * profile - loss_ref[s] * amount(s))
            for r in range(NREAC):
                speed = speed_ref[r] * amount(pair_ref[r, 0]) * amount(pair_ref[r, 1])
                for s in range(S):
                    total[s] = total[s] + stoich_ref[r, s].astype(F32) * speed
            for s in range(S):
                tend_ref[pl.ds(pl.multiple_of(base + s * LEV, step), step), lanes] = jnp.where(
                    live, total[s], 0.0
                ).astype(BF16)
            return 0

        lax.fori_loop(0, columns * steps, part, 0)
        rate_ref[lanes, :] = mm(tend_ref[:, lanes], mode_bf, TN)


def first_kernel(
    columns,
    counts_ref, pair_ref, stoich_ref, speed_ref, loss_ref, table_ref,
    modes_ref, face_ref, coef_ref, idx_ref,
    diff_ref, tend_ref, rate_ref, emis_ref,
    field_ref,
):
    index = idx_ref[...]
    for s in range(S):
        row = jnp.zeros(index.shape, F32)
        for k in range(NEMIS):
            row = jnp.where(index == k, table_ref[k, s], row)
        emis_ref[s : s + 1, :] = row
    diffused = diffuse_rows(modes_ref[...], face_ref, counts_ref, columns)
    diff_ref[...] = diffused
    react(
        diffused, coef_ref, emis_ref, counts_ref, pair_ref, stoich_ref, speed_ref, loss_ref,
        field_ref, tend_ref, rate_ref, columns,
    )


def advance(diffused, pull, solve_ref, rate):
    transfer = mm3(split(rate), split(solve_ref[...]), TN)
    moved = mm3(split(diffused), split(transfer))
    return diffused + (TIME_STEP * math.sqrt(R)) * (pull - moved)


def middle_kernel(
    columns, total_rows,
    counts_ref, pair_ref, stoich_ref, speed_ref, loss_ref,
    diff_in_ref, pull_ref, solve_ref, sum_ref, coef_ref, face_ref, emis_ref,
    diff_ref, tend_ref, rate_ref, coef_out_ref,
    field_ref,
):
    raw = sum_ref[...]
    coef_out_ref[...] = (
        coef_ref[...].astype(F32) + RATE_STEP * (raw * (math.sqrt(R) / total_rows))
    ).astype(BF16)
    modes = advance(diff_in_ref[...], pull_ref[...], solve_ref, raw * (1.0 / total_rows))
    diffused = diffuse_rows(modes, face_ref, counts_ref, columns)
    diff_ref[...] = diffused
    react(
        diffused, coef_out_ref, emis_ref, counts_ref, pair_ref, stoich_ref, speed_ref, loss_ref,
        field_ref, tend_ref, rate_ref, columns,
    )


def last_kernel(
    total_rows,
    place_ref,
    diff_in_ref, pull_ref, solve_ref, sum_ref, coef_ref,
    modes_ref, coef_out_ref,
):
    mine = coef_out_ref.shape[0]
    own = pl.ds(pl.multiple_of(place_ref[0] * mine, mine), mine)
    coef_out_ref[...] = (
        coef_ref[own, :].astype(F32)
        + RATE_STEP * (sum_ref[own, :] * (math.sqrt(R) / total_rows))
    ).astype(BF16)
    modes_ref[...] = advance(
        diff_in_ref[...], pull_ref[...], solve_ref, sum_ref[...] * (1.0 / total_rows)
    )


def solve_kernel(
    ridge, coef_ref, tend_ref, solve_ref, pull_ref, gram_high_ref, gram_low_ref, inv_ref
):
    coef = coef_ref[...]
    eye = (
        lax.broadcasted_iota(jnp.int32, (R, R), 0) == lax.broadcasted_iota(jnp.int32, (R, R), 1)
    ).astype(F32)
    gram = mm(coef, coef, TN) + ridge * eye
    top = jnp.max(jnp.sum(jnp.abs(gram), axis=0, keepdims=True))
    high, low = split(gram)
    gram_high_ref[...] = high
    gram_low_ref[...] = low
    scale = 2.0 / (top + ridge)
    inv_ref[...] = scale * eye
    gap = (top - ridge) / (top + ridge)

    def refine(gap):
        square = gap * gap
        factor = 2.0 / (2.0 - square)
        inv = inv_ref[...]
        halves = split(inv)
        rest = eye - mm3((gram_high_ref[...], gram_low_ref[...]), halves)
        inv_ref[...] = factor * (inv + mm3(halves, split(rest)))
        return square / (2.0 - square)

    lax.while_loop(lambda gap: gap > 1e-5, refine, gap)
    high, low = split(inv_ref[...])
    solve = mm(coef, high) + mm(coef, low)
    solve_ref[...] = solve
    high, low = split(solve)
    pull_ref[...] = mm(tend_ref[...], high) + mm(tend_ref[...], low)


VMEM_LIMIT = 48 * 1024 * 1024


def whole(n):
    return [pl.BlockSpec(memory_space=pltpu.VMEM)] * n


def scalars(n):
    return [pl.BlockSpec(memory_space=pltpu.SMEM)] * n


def call(kernel, n_scalar, outs, scratch, *args):
    return pl.pallas_call(
        kernel,
        in_specs=scalars(n_scalar) + whole(len(args) - n_scalar),
        out_specs=whole(len(outs)),
        out_shape=[jax.ShapeDtypeStruct(shape, dtype) for shape, dtype in outs],
        scratch_shapes=[pltpu.VMEM(shape, dtype) for shape, dtype in scratch],
        compiler_params=pltpu.CompilerParams(vmem_limit_bytes=VMEM_LIMIT),
    )(*args)


def sum_over(x, n):
    if n & (n - 1) or n < 2:
        return lax.psum(x, "col")

    def swap(value, mask):
        return lax.ppermute(value, "col", [(i, i ^ mask) for i in range(n)])

    half = x.shape[0] // 2
    side = lax.axis_index("col") & 1
    keep = lax.dynamic_slice_in_dim(x, side * half, half, 0)
    give = lax.dynamic_slice_in_dim(x, (1 - side) * half, half, 0)
    part = keep + swap(give, 1)
    mask = 2
    while mask < n:
        part = part + swap(part, mask if mask * 2 < n or mask < 8 else mask | (mask >> 1))
        mask *= 2
    other = swap(part, 1)
    return jnp.where(
        side == 0, jnp.concatenate([part, other], 0), jnp.concatenate([other, part], 0)
    )


def on_device(
    mode_rows,
    coeffs,
    diffusivity,
    counts,
    emis_idx,
    emis_table,
    reactants,
    stoich,
    rate_consts,
    loss_rates,
):
    n = lax.axis_size("col")
    rows = mode_rows.shape[0]
    total_rows = rows * n
    mine = coeffs.shape[0]
    members = mine * n
    columns = counts.shape[0]
    ridge = RIDGE_SHARE * members
    block = math.gcd(members, 256)
    place = lax.axis_index("col").astype(jnp.int32).reshape(1)
    face = diffusivity.T
    coef = lax.all_to_all(jnp.tile(coeffs, (n, 1)), "col", 0, 0, tiled=True)

    rows_f32 = ((rows, R), F32)
    tend_out = ((rows, members), BF16)
    rate_out = ((members, R), F32)
    field_tmp = ((rows, block), F32)
    chem = (counts, reactants, stoich, rate_consts, loss_rates)

    def solve(coef, tend):
        return call(
            functools.partial(solve_kernel, ridge), 0,
            [rate_out, rows_f32], [((R, R), BF16), ((R, R), BF16), ((R, R), F32)],
            coef, tend,
        )

    diff, tend, rate, emis = call(
        functools.partial(first_kernel, columns), 6,
        [rows_f32, tend_out, rate_out, ((S, members), F32)], [field_tmp],
        *chem, emis_table, mode_rows, face, coef, emis_idx.reshape(1, members),
    )
    for _ in range(NSUB - 1):
        total = sum_over(rate, n)
        solved, pull = solve(coef, tend)
        diff, tend, rate, coef = call(
            functools.partial(middle_kernel, columns, total_rows), 5,
            [rows_f32, tend_out, rate_out, ((members, R), BF16)], [field_tmp],
            *chem, diff, pull, solved, total, coef, face, emis,
        )
    total = sum_over(rate, n)
    solved, pull = solve(coef, tend)
    modes, coef_out = call(
        functools.partial(last_kernel, total_rows), 1,
        [rows_f32, ((mine, R), BF16)], [],
        place, diff, pull, solved, total, coef,
    )
    return (modes, coef_out)


def solution(mesh):
    placed = (
        P(("grp", "col"), None),
        P(("grp", "col"), None),
        P(("grp", "col"), None),
        P(("grp", "col")),
        P("grp"),
        P(),
        P(),
        P(),
        P(),
        P(),
    )
    return jax.shard_map(
        on_device,
        mesh=mesh,
        in_specs=placed,
        out_specs=(P(("grp", "col"), None), P(("grp", "col"), None)),
        check_vma=False,
    )
```

time: 398 us -> 78.1 us (0.20); the launches traced: 393 us -> 77.7 us
  waiting for transfers between devices: 174 us -> 40.1 us
  other arithmetic: 116 us -> 0.18 us
  blocking collectives: 44.9 us -> 0 us
  matrix products: 22 us -> 0 us
  Pallas kernels: 0 us -> 19.9 us
  between operations: 17.8 us -> 1.48 us
  local copies, waits for them, and re-layouts: 17.3 us -> 5.31 us
  starting transfers between devices: 0.9 us -> 10.6 us
    psum x2 -> x0, waiting for transfers between devices: 173 us -> none  [on_device(): gram_matrix, proj_matrix = lax.psum((gram_part, proj_part), 'col')]
    another operation x18 -> x0, other arithmetic: 108 us -> none  [the longest x13 68.6 us: on_device(): factor = jnp.linalg.cholesky(gram_matrix)]
    all_gather x2 -> x0, blocking collectives: 44.9 us -> none  [on_device(): coef_gathered = lax.all_gather(coeffs, 'col', axis=0, tiled=True)]
    ppermute x0 -> x10, waiting for transfers between devices: none -> 35.1 us  [swap(): return lax.ppermute(value, 'col', [(i, i ^ mask) for i in range(n)])]
    pallas_call x0 -> x5, Pallas kernels: none -> 19.9 us  [call(): pl.pallas_call(kernel, in_specs=scalars(n_scalar) + whole(len(args) - n_s...]
    dot_general x30 -> x0, matrix products: 15.9 us -> none  [the longest x4 2.74 us: reaction(): jnp.einsum('rs,bcsl->bcrl', pick_first, field_block, precision=PRECISE)]
    all_to_all x0 -> x1, starting transfers between devices: none -> 7.39 us  [on_device(): coef = lax.all_to_all(jnp.tile(coeffs, (n, 1)), 'col', 0, 0, tiled=True)]
    another operation x21 -> x1, local copies, waits for them, and re-layouts: 8.03 us -> 1.36 us  [on_device(): coef = lax.all_to_all(jnp.tile(coeffs, (n, 1)), 'col', 0, 0, tiled=True)]
  transfers between devices with their start and end apart: 4 -> 11, of which waited for: 2 -> 9; matrix products, arithmetic and copies ran while one was open for 32% -> 0% of each run, Pallas kernels for 0% -> 17%
where the time goes in v1:
time: 78.1 us; the launch traced here: 77.7 us
  waiting for transfers between devices  40.1 us (51%)
  Pallas kernels  19.9 us (25%)
  starting transfers between devices  10.6 us (14%)
  local copies, waits for them, and re-layouts  5.31 us (7%)
  between operations  1.48 us (2%)
    ppermute x10, waiting for transfers between devices, swap(): return lax.ppermute(value, 'col', [(i, i ^ mask) for i in range(n)])  35.1 us
    pallas_call x5, Pallas kernels, call(): pl.pallas_call(kernel, in_specs=scalars(n_scalar) + whole(len(args) - n_s...  19.9 us
    all_to_all x1, starting transfers between devices, on_device(): coef = lax.all_to_all(jnp.tile(coeffs, (n, 1)), 'col', 0, 0, tiled=True)  7.39 us
    all_to_all x1, waiting for transfers between devices, on_device(): coef = lax.all_to_all(jnp.tile(coeffs, (n, 1)), 'col', 0, 0, tiled=True)  5.04 us
    unnamed x19, local copies, waits for them, and re-layouts  3.82 us
    ppermute x10, starting transfers between devices, swap(): return lax.ppermute(value, 'col', [(i, i ^ mask) for i in range(n)])  3.26 us
  transfers between devices with their start and end apart: 11, of which 9 were waited for; matrix products, arithmetic and copies ran while one was open for 0% of the time, Pallas kernels for 17%

profile of v1, /device:TPU:0, one launch (start us, length us, event | category | flops | bytes accessed | tf_op | source)
XLA Modules:
  0.0 77.7 jit_solution(13856607804218277429)
XLA Ops:
  0.6 1.4 %tile.2 = bf16[16,16,256]{2,1,0:T(8,128)(2,1)} broadcast(bf16[16,256]{1,0:T(8,128)(2,1)} %param.11), dimensions={1,2} | broadcast | bytes 139264 | tf_op jit(solution)/shard_map/tile | solution.py:259
  2.0 7.4 %all-to-all-start = ((bf16[16,16,256]{2,1,0:T(8,128)(2,1)}), bf16[16,16,256]{2,1,0:T(8,128)(2,1)S(1)}, u32[]{:S(2)}, u32[]{:S(2)}) async-start(bf16[16,16,256]{2,1,0:T(8,128)(2,1)} %tile.2), calls=%async_computation | async-start | bytes 262144 | tf_op jit(solution)/shard_map/all_to_all | solution.py:259
  9.4 0.0 copy-start.6
  10.1 0.0 copy-done.6
  10.1 0.0 copy-start.4
  10.1 0.1 copy.16.pair_ref
  10.2 0.6 copy-done.4
  10.8 0.0 copy-start.5
  10.8 0.1 copy.17.stoich_ref
  10.8 0.6 copy-done.5
  11.4 0.1 copy.14.table_ref
  11.5 0.0 copy-start.7
  11.5 0.7 copy-done.7
  12.2 0.0 copy-start.3
  12.2 0.1 copy.15.face_ref
  12.3 5.0 %all-to-all-done = bf16[16,16,256]{2,1,0:T(8,128)(2,1)S(1)} async-done(((bf16[16,16,256]{2,1,0:T(8,128)(2,1)}), bf16[16,16,256]{2,1,0:T(8,128)(2,1)S(1)}, u32[]{:S(2)}, u32[]{:S(2)}) %all-to-all-start) | async-done | bytes 131104 | tf_op jit(solution)/shard_map/all_to_all | solution.py:259
  17.3 0.0 copy-start.1
  17.3 0.0 copy-start.2
  17.3 0.0 copy-done.3
  17.3 0.6 copy-done.1
  18.0 0.0 copy-done.2
  18.0 0.0 copy-start
  18.0 1.0 %copy-done = f32[512,256]{1,0:T(8,128)S(1)} copy-done((f32[512,256]{1,0:T(8,128)S(1)}, f32[512,256]{1,0:T(8,128)}, u32[]{:S(2)}) %copy-start) | copy-done | bytes 524312
  19.0 2.3 %shard_map.113 = (f32[512,256]{1,0:T(8,128)S(1)}, bf16[512,256]{1,0:T(8,128)(2,1)S(1)}, f32[256,256]{1,0:T(8,128)S(1)}, f32[8,256]{1,0:T(8,128)S(1)}) custom-call(s32[1]{0:T(128)S(6)} %copy.19.counts_ref, s32[12,2]{1,0:T(8,128)S(1)} %copy.16.pair_ref, s32[12,8]{1,0:T(8,128)S(1)} %copy.17.stoich_ref, f32[12]{0:T(128)S(1)} %copy-done.1, f32[8]{0:T(128)S(1)} %copy-done.2, ...), custom_call_target="tpu_custom_call" | custom-call | tf_op jit(solution)/shard_map/pallas_call | solution.py:205
  21.4 0.1 collective-permute-start
  21.4 1.3 %collective-permute-done = f32[128,256]{1,0:T(8,128)S(1)} collective-permute-done((f32[128,256]{1,0:T(8,128)S(1)}, f32[128,256]{1,0:T(8,128)S(1)}, u32[]{:S(2)}, u32[]{:S(2)}) %collective-permute-start) | collective-permute-done | bytes 131104 | tf_op jit(solution)/shard_map/ppermute | solution.py:220
  22.8 0.1 collective-permute-start.1
  22.9 5.5 %collective-permute-done.1 = f32[128,256]{1,0:T(8,128)S(1)} collective-permute-done((f32[128,256]{1,0:T(8,128)S(1)}, f32[128,256]{1,0:T(8,128)S(1)}, u32[]{:S(2)}, u32[]{:S(2)}) %collective-permute-start.1) | collective-permute-done | bytes 131104 | tf_op jit(solution)/shard_map/ppermute | solution.py:220
  28.4 0.1 collective-permute-start.2
  28.5 5.0 %collective-permute-done.2 = f32[128,256]{1,0:T(8,128)S(1)} collective-permute-done((f32[128,256]{1,0:T(8,128)S(1)}, f32[128,256]{1,0:T(8,128)S(1)}, u32[]{:S(2)}, u32[]{:S(2)}) %collective-permute-start.2) | collective-permute-done | bytes 131104 | tf_op jit(solution)/shard_map/ppermute | solution.py:220
  33.5 0.8 %collective-permute-start.3 = (f32[128,256]{1,0:T(8,128)S(1)}, f32[128,256]{1,0:T(8,128)S(1)}, u32[]{:S(2)}, u32[]{:S(2)}) collective-permute-start(f32[128,256]{1,0:T(8,128)S(1)} %add.36), channel_id=1, source_target_pairs={{0,12},{1,13},{2,14},{3,15},{4,8},{5,9},{6,10},{7,11},{8,4},{9,5},... | collective-permute-start | bytes 393224 | tf_op jit(solution)/shard_map/ppermute | solution.py:220
  34.3 6.0 %collective-permute-done.3 = f32[128,256]{1,0:T(8,128)S(1)} collective-permute-done((f32[128,256]{1,0:T(8,128)S(1)}, f32[128,256]{1,0:T(8,128)S(1)}, u32[]{:S(2)}, u32[]{:S(2)}) %collective-permute-start.3) | collective-permute-done | bytes 131104 | tf_op jit(solution)/shard_map/ppermute | solution.py:220
  40.4 0.1 collective-permute-start.4
  40.4 6.5 %shard_map.114 = (f32[256,256]{1,0:T(8,128)S(1)}, f32[512,256]{1,0:T(8,128)S(1)}) custom-call(bf16[256,256]{1,0:T(8,128)(2,1)S(1)} %bitcast.5, bf16[512,256]{1,0:T(8,128)(2,1)S(1)} %get-tuple-element.15.tend_ref), custom_call_target="tpu_custom_call" | custom-call | tf_op jit(solution)/shard_map/pallas_call | solution.py:205
  46.9 0.0 collective-permute-done.4
  47.0 3.0 %shard_map.115 = (f32[512,256]{1,0:T(8,128)S(1)}, bf16[512,256]{1,0:T(8,128)(2,1)S(1)}, f32[256,256]{1,0:T(8,128)S(1)}, bf16[256,256]{1,0:T(8,128)(2,1)S(1)}) custom-call(s32[1]{0:T(128)S(6)} %copy.19.counts_ref, s32[12,2]{1,0:T(8,128)S(1)} %copy.16.pair_ref, s32[12,8]{1,0:T(8,128)S(1)} %copy.17.stoich_ref, f32[12]{0:T(128)S(1)} %copy-done.1, ...), custom_call_target="tpu_custom_call" | custom-call | tf_op jit(solution)/shard_map/pallas_call | solution.py:205
  50.0 0.6 collective-permute-start.5
  50.6 1.0 %collective-permute-done.5 = f32[128,256]{1,0:T(8,128)S(1)} collective-permute-done((f32[128,256]{1,0:T(8,128)S(1)}, f32[128,256]{1,0:T(8,128)S(1)}, u32[]{:S(2)}, u32[]{:S(2)}) %collective-permute-start.5) | collective-permute-done | bytes 131104 | tf_op jit(solution)/shard_map/ppermute | solution.py:220
  51.6 0.5 collective-permute-start.6
  52.1 5.3 %collective-permute-done.6 = f32[128,256]{1,0:T(8,128)S(1)} collective-permute-done((f32[128,256]{1,0:T(8,128)S(1)}, f32[128,256]{1,0:T(8,128)S(1)}, u32[]{:S(2)}, u32[]{:S(2)}) %collective-permute-start.6) | collective-permute-done | bytes 131104 | tf_op jit(solution)/shard_map/ppermute | solution.py:220
  57.4 0.1 collective-permute-start.7
  57.5 5.0 %collective-permute-done.7 = f32[128,256]{1,0:T(8,128)S(1)} collective-permute-done((f32[128,256]{1,0:T(8,128)S(1)}, f32[128,256]{1,0:T(8,128)S(1)}, u32[]{:S(2)}, u32[]{:S(2)}) %collective-permute-start.7) | collective-permute-done | bytes 131104 | tf_op jit(solution)/shard_map/ppermute | solution.py:220
  62.5 0.9 %collective-permute-start.8 = (f32[128,256]{1,0:T(8,128)S(1)}, f32[128,256]{1,0:T(8,128)S(1)}, u32[]{:S(2)}, u32[]{:S(2)}) collective-permute-start(f32[128,256]{1,0:T(8,128)S(1)} %add.40), channel_id=1, source_target_pairs={{0,12},{1,13},{2,14},{3,15},{4,8},{5,9},{6,10},{7,11},{8,4},{9,5},... | collective-permute-start | bytes 393224 | tf_op jit(solution)/shard_map/ppermute | solution.py:220
  63.4 6.0 %collective-permute-done.8 = f32[128,256]{1,0:T(8,128)S(1)} collective-permute-done((f32[128,256]{1,0:T(8,128)S(1)}, f32[128,256]{1,0:T(8,128)S(1)}, u32[]{:S(2)}, u32[]{:S(2)}) %collective-permute-start.8) | collective-permute-done | bytes 131104 | tf_op jit(solution)/shard_map/ppermute | solution.py:220
  69.4 0.1 collective-permute-start.9
  69.5 6.5 %shard_map.116 = (f32[256,256]{1,0:T(8,128)S(1)}, f32[512,256]{1,0:T(8,128)S(1)}) custom-call(bf16[256,256]{1,0:T(8,128)(2,1)S(1)} %get-tuple-element.21.coef_ref, bf16[512,256]{1,0:T(8,128)(2,1)S(1)} %get-tuple-element.22.tend_ref), custom_call_target="tpu_custom_call" | custom-call | tf_op jit(solution)/shard_map/pallas_call | solution.py:205
  76.0 0.0 collective-permute-done.9
  76.1 1.6 %shard_map.117 = (f32[512,256]{1,0:T(8,128)}, bf16[16,256]{1,0:T(8,128)(2,1)}) custom-call(s32[1]{0:T(128)} %bitcast.place_ref, f32[512,256]{1,0:T(8,128)S(1)} %get-tuple-element.20.diff_in_ref, f32[512,256]{1,0:T(8,128)S(1)} %get-tuple-element.23.pull_ref, f32[256,256]{1,0:T(8,128)S(1)} %get-tuple-element.24.solve_ref, ...), custom_call_target="tpu_custom_call" | custom-call | tf_op jit(solution)/shard_map/pallas_call | solution.py:205
  (12 shorter events, 0.2 us)
Async XLA Ops:
  2.0 15.3 %all-to-all-start = ((bf16[16,16,256]{2,1,0:T(8,128)(2,1)}), bf16[16,16,256]{2,1,0:T(8,128)(2,1)S(1)}, u32[]{:S(2)}, u32[]{:S(2)}) async-start(bf16[16,16,256]{2,1,0:T(8,128)(2,1)} %tile.2), calls=%async_computation | async-start | bytes 262144 | tf_op jit(solution)/shard_map/all_to_all | solution.py:259
  9.4 0.7 copy-start.6
  10.1 0.7 copy-start.4
  10.8 0.7 copy-start.5
  11.5 0.7 copy-start.7
  12.2 5.1 %copy-start.3 = (s32[256]{0:T(256)S(1)}, s32[256]{0:T(256)}, u32[]{:S(2)}) copy-start(s32[256]{0:T(256)} %param.14) | copy-start | bytes 3076
  17.3 0.7 copy-start.1
  17.3 0.7 copy-start.2
  18.0 1.0 %copy-start = (f32[512,256]{1,0:T(8,128)S(1)}, f32[512,256]{1,0:T(8,128)}, u32[]{:S(2)}) copy-start(f32[512,256]{1,0:T(8,128)} %modes_ref.1) | copy-start | bytes 1572868
  21.4 1.4 %collective-permute-start = (f32[128,256]{1,0:T(8,128)S(1)}, f32[128,256]{1,0:T(8,128)S(1)}, u32[]{:S(2)}, u32[]{:S(2)}) collective-permute-start(f32[128,256]{1,0:T(8,128)S(1)} %constant_dynamic-slice_fusion.1), channel_id=1, source_target_pairs={{0,1},{1,0},{2,3},{3,2},{4,5},{5,4},{6,7},{7,6},{8,9},{9,8},{10,11... | collective-permute-start | bytes 393224 | tf_op jit(solution)/shard_map/ppermute | solution.py:220
  22.8 5.6 %collective-permute-start.1 = (f32[128,256]{1,0:T(8,128)S(1)}, f32[128,256]{1,0:T(8,128)S(1)}, u32[]{:S(2)}, u32[]{:S(2)}) collective-permute-start(f32[128,256]{1,0:T(8,128)S(1)} %dynamic-slice_add_fusion.1), channel_id=1, source_target_pairs={{0,2},{1,3},{2,0},{3,1},{4,6},{5,7},{6,4},{7,5},{8,10},{9,11},{10,... | collective-permute-start | bytes 393224 | tf_op jit(solution)/shard_map/ppermute | solution.py:220
  28.4 5.0 %collective-permute-start.2 = (f32[128,256]{1,0:T(8,128)S(1)}, f32[128,256]{1,0:T(8,128)S(1)}, u32[]{:S(2)}, u32[]{:S(2)}) collective-permute-start(f32[128,256]{1,0:T(8,128)S(1)} %add.35), channel_id=1, source_target_pairs={{0,4},{1,5},{2,6},{3,7},{4,0},{5,1},{6,2},{7,3},{8,12},{9,13},{10,... | collective-permute-start | bytes 393224 | tf_op jit(solution)/shard_map/ppermute | solution.py:220
  33.5 6.8 %collective-permute-start.3 = (f32[128,256]{1,0:T(8,128)S(1)}, f32[128,256]{1,0:T(8,128)S(1)}, u32[]{:S(2)}, u32[]{:S(2)}) collective-permute-start(f32[128,256]{1,0:T(8,128)S(1)} %add.36), channel_id=1, source_target_pairs={{0,12},{1,13},{2,14},{3,15},{4,8},{5,9},{6,10},{7,11},{8,4},{9,5},... | collective-permute-start | bytes 393224 | tf_op jit(solution)/shard_map/ppermute | solution.py:220
  40.4 6.6 %collective-permute-start.4 = (f32[128,256]{1,0:T(8,128)S(1)}, f32[128,256]{1,0:T(8,128)S(1)}, u32[]{:S(2)}, u32[]{:S(2)}) collective-permute-start(f32[128,256]{1,0:T(8,128)S(1)} %add.37), channel_id=1, source_target_pairs={{0,1},{1,0},{2,3},{3,2},{4,5},{5,4},{6,7},{7,6},{8,9},{9,8},{10,11... | collective-permute-start | bytes 393224 | tf_op jit(solution)/shard_map/ppermute | solution.py:220
  50.0 1.5 %collective-permute-start.5 = (f32[128,256]{1,0:T(8,128)S(1)}, f32[128,256]{1,0:T(8,128)S(1)}, u32[]{:S(2)}, u32[]{:S(2)}) collective-permute-start(f32[128,256]{1,0:T(8,128)S(1)} %constant_dynamic-slice_fusion), channel_id=1, source_target_pairs={{0,1},{1,0},{2,3},{3,2},{4,5},{5,4},{6,7},{7,6},{8,9},{9,8},{10,11... | collective-permute-start | bytes 393224 | tf_op jit(solution)/shard_map/ppermute | solution.py:220
  51.6 5.8 %collective-permute-start.6 = (f32[128,256]{1,0:T(8,128)S(1)}, f32[128,256]{1,0:T(8,128)S(1)}, u32[]{:S(2)}, u32[]{:S(2)}) collective-permute-start(f32[128,256]{1,0:T(8,128)S(1)} %dynamic-slice_add_fusion), channel_id=1, source_target_pairs={{0,2},{1,3},{2,0},{3,1},{4,6},{5,7},{6,4},{7,5},{8,10},{9,11},{10,... | collective-permute-start | bytes 393224 | tf_op jit(solution)/shard_map/ppermute | solution.py:220
  57.4 5.0 %collective-permute-start.7 = (f32[128,256]{1,0:T(8,128)S(1)}, f32[128,256]{1,0:T(8,128)S(1)}, u32[]{:S(2)}, u32[]{:S(2)}) collective-permute-start(f32[128,256]{1,0:T(8,128)S(1)} %add.39), channel_id=1, source_target_pairs={{0,4},{1,5},{2,6},{3,7},{4,0},{5,1},{6,2},{7,3},{8,12},{9,13},{10,... | collective-permute-start | bytes 393224 | tf_op jit(solution)/shard_map/ppermute | solution.py:220
  62.5 6.9 %collective-permute-start.8 = (f32[128,256]{1,0:T(8,128)S(1)}, f32[128,256]{1,0:T(8,128)S(1)}, u32[]{:S(2)}, u32[]{:S(2)}) collective-permute-start(f32[128,256]{1,0:T(8,128)S(1)} %add.40), channel_id=1, source_target_pairs={{0,12},{1,13},{2,14},{3,15},{4,8},{5,9},{6,10},{7,11},{8,4},{9,5},... | collective-permute-start | bytes 393224 | tf_op jit(solution)/shard_map/ppermute | solution.py:220
  69.4 6.6 %collective-permute-start.9 = (f32[128,256]{1,0:T(8,128)S(1)}, f32[128,256]{1,0:T(8,128)S(1)}, u32[]{:S(2)}, u32[]{:S(2)}) collective-permute-start(f32[128,256]{1,0:T(8,128)S(1)} %add.41), channel_id=1, source_target_pairs={{0,1},{1,0},{2,3},{3,2},{4,5},{5,4},{6,7},{7,6},{8,9},{9,8},{10,11... | collective-permute-start | bytes 393224 | tf_op jit(solution)/shard_map/ppermute | solution.py:220

commit v2 on v1

--- a/solution.py
+++ b/solution.py
@@ -40,12 +40,10 @@
     return mm(a[0], b[0], dims) + (mm(a[0], b[1], dims) + mm(a[1], b[0], dims))
 
 
-def diffuse_rows(modes, face_ref, counts_ref, columns):
-    level = lax.broadcasted_iota(jnp.int32, (LEV, R), 0)
+def diffuse_rows(modes, face_ref):
     faces = []
-    for c in range(columns):
-        face = jnp.broadcast_to(face_ref[:, c : c + 1], (LEV, R))
-        faces += [jnp.where(level + 1 < counts_ref[c], face, 0.0)] * S
+    for c in range(face_ref.shape[0] // LEV):
+        faces += [face_ref[c * LEV : (c + 1) * LEV, :]] * S
     face = jnp.concatenate(faces, axis=0)
     rows = modes.shape[0]
     flux = face * (pltpu.roll(modes, rows - 1, 0) - modes)
@@ -80,9 +78,9 @@
             for s in range(S):
                 total.append(emis_ref[s : s + 1, lanes] * profile - loss_ref[s] * amount(s))
             for r in range(NREAC):
-                speed = speed_ref[r] * amount(pair_ref[r, 0]) * amount(pair_ref[r, 1])
+                speed = speed_ref[r] * amount(pair_ref[0, r]) * amount(pair_ref[1, r])
                 for s in range(S):
-                    total[s] = total[s] + stoich_ref[r, s].astype(F32) * speed
+                    total[s] = total[s] + stoich_ref[s, r].astype(F32) * speed
             for s in range(S):
                 tend_ref[pl.ds(pl.multiple_of(base + s * LEV, step), step), lanes] = jnp.where(
                     live, total[s], 0.0
@@ -93,23 +91,36 @@
         rate_ref[lanes, :] = mm(tend_ref[:, lanes], mode_bf, TN)
 
 
-def first_kernel(
+def setup_kernel(
     columns,
-    counts_ref, pair_ref, stoich_ref, speed_ref, loss_ref, table_ref,
-    modes_ref, face_ref, coef_ref, idx_ref,
-    diff_ref, tend_ref, rate_ref, emis_ref,
-    field_ref,
+    counts_ref, table_ref,
+    modes_ref, level_face_ref, idx_ref,
+    diff_ref, emis_ref, face_ref,
 ):
     index = idx_ref[...]
     for s in range(S):
         row = jnp.zeros(index.shape, F32)
         for k in range(NEMIS):
-            row = jnp.where(index == k, table_ref[k, s], row)
+            row = jnp.where(index == k, table_ref[s, k], row)
         emis_ref[s : s + 1, :] = row
-    diffused = diffuse_rows(modes_ref[...], face_ref, counts_ref, columns)
-    diff_ref[...] = diffused
+    down = lax.broadcasted_iota(jnp.int32, (LEV, LEV), 0)
+    across = lax.broadcasted_iota(jnp.int32, (LEV, LEV), 1)
+    for c in range(columns):
+        inner = (down == across) & (down + 1 < counts_ref[c])
+        face = jnp.sum(jnp.where(inner, level_face_ref[c : c + 1, :], 0.0), axis=1, keepdims=True)
+        face_ref[c * LEV : (c + 1) * LEV, :] = jnp.broadcast_to(face, (LEV, R))
+    diff_ref[...] = diffuse_rows(modes_ref[...], face_ref)
+
+
+def first_kernel(
+    columns,
+    counts_ref, pair_ref, stoich_ref, speed_ref, loss_ref,
+    diff_ref, coef_ref, emis_ref,
+    tend_ref, rate_ref,
+    field_ref,
+):
     react(
-        diffused, coef_ref, emis_ref, counts_ref, pair_ref, stoich_ref, speed_ref, loss_ref,
+        diff_ref[...], coef_ref, emis_ref, counts_ref, pair_ref, stoich_ref, speed_ref, loss_ref,
         field_ref, tend_ref, rate_ref, columns,
     )
 
@@ -132,7 +143,7 @@
         coef_ref[...].astype(F32) + RATE_STEP * (raw * (math.sqrt(R) / total_rows))
     ).astype(BF16)
     modes = advance(diff_in_ref[...], pull_ref[...], solve_ref, raw * (1.0 / total_rows))
-    diffused = diffuse_rows(modes, face_ref, counts_ref, columns)
+    diffused = diffuse_rows(modes, face_ref)
     diff_ref[...] = diffused
     react(
         diffused, coef_out_ref, emis_ref, counts_ref, pair_ref, stoich_ref, speed_ref, loss_ref,
@@ -157,32 +168,54 @@
     )
 
 
-def solve_kernel(
-    ridge, coef_ref, tend_ref, solve_ref, pull_ref, gram_high_ref, gram_low_ref, inv_ref
-):
-    coef = coef_ref[...]
-    eye = (
+def identity():
+    return (
         lax.broadcasted_iota(jnp.int32, (R, R), 0) == lax.broadcasted_iota(jnp.int32, (R, R), 1)
     ).astype(F32)
+
+
+def refine(eye, high_ref, low_ref, inv_ref, gap):
+    square = gap * gap
+    factor = 2.0 / (2.0 - square)
+    inv = inv_ref[...]
+    halves = split(inv)
+    rest = eye - mm3((high_ref[...], low_ref[...]), halves)
+    inv_ref[...] = factor * (inv + mm3(halves, split(rest)))
+    return square / (2.0 - square)
+
+
+def inverse_start(ridge, steps, coef_ref, high_ref, low_ref, inv_ref, gap_ref):
+    coef = coef_ref[...]
+    eye = identity()
     gram = mm(coef, coef, TN) + ridge * eye
     top = jnp.max(jnp.sum(jnp.abs(gram), axis=0, keepdims=True))
-    high, low = split(gram)
-    gram_high_ref[...] = high
-    gram_low_ref[...] = low
-    scale = 2.0 / (top + ridge)
-    inv_ref[...] = scale * eye
+    high_ref[...], low_ref[...] = split(gram)
+    inv_ref[...] = (2.0 / (top + ridge)) * eye
     gap = (top - ridge) / (top + ridge)
-
-    def refine(gap):
-        square = gap * gap
-        factor = 2.0 / (2.0 - square)
-        inv = inv_ref[...]
-        halves = split(inv)
-        rest = eye - mm3((gram_high_ref[...], gram_low_ref[...]), halves)
-        inv_ref[...] = factor * (inv + mm3(halves, split(rest)))
-        return square / (2.0 - square)
-
-    lax.while_loop(lambda gap: gap > 1e-5, refine, gap)
+    gap_ref[0] = lax.fori_loop(
+        0, steps, lambda i, gap: refine(eye, high_ref, low_ref, inv_ref, gap), gap
+    )
+
+
+def inverse_more(steps, gap_in_ref, high_ref, low_ref, inv_in_ref, inv_ref, gap_ref):
+    eye = identity()
+    inv_ref[...] = inv_in_ref[...]
+    gap_ref[0] = lax.fori_loop(
+        0, steps, lambda i, gap: refine(eye, high_ref, low_ref, inv_ref, gap), gap_in_ref[0]
+    )
+
+
+def inverse_end(
+    gap_in_ref, high_ref, low_ref, inv_in_ref, coef_ref, tend_ref, solve_ref, pull_ref, inv_ref
+):
+    eye = identity()
+    inv_ref[...] = inv_in_ref[...]
+    lax.while_loop(
+        lambda gap: gap > 1e-5,
+        lambda gap: refine(eye, high_ref, low_ref, inv_ref, gap),
+        gap_in_ref[0],
+    )
+    coef = coef_ref[...]
     high, low = split(inv_ref[...])
     solve = mm(coef, high) + mm(coef, low)
     solve_ref[...] = solve
@@ -201,20 +234,31 @@
     return [pl.BlockSpec(memory_space=pltpu.SMEM)] * n
 
 
+SCALAR = "scalar"
+
+
 def call(kernel, n_scalar, outs, scratch, *args):
+    out_specs = []
+    for out in outs:
+        out_specs += scalars(1) if out is SCALAR else whole(1)
     return pl.pallas_call(
         kernel,
         in_specs=scalars(n_scalar) + whole(len(args) - n_scalar),
-        out_specs=whole(len(outs)),
-        out_shape=[jax.ShapeDtypeStruct(shape, dtype) for shape, dtype in outs],
+        out_specs=out_specs,
+        out_shape=[
+            jax.ShapeDtypeStruct(*(((1,), F32) if out is SCALAR else out)) for out in outs
+        ],
         scratch_shapes=[pltpu.VMEM(shape, dtype) for shape, dtype in scratch],
         compiler_params=pltpu.CompilerParams(vmem_limit_bytes=VMEM_LIMIT),
     )(*args)
 
 
-def sum_over(x, n):
-    if n & (n - 1) or n < 2:
-        return lax.psum(x, "col")
+def sum_over(x, n, work):
+    state = ()
+    if n & (n - 1) or n < 4:
+        for piece in work:
+            state = piece(state)
+        return lax.psum(x, "col"), state
 
     def swap(value, mask):
         return lax.ppermute(value, "col", [(i, i ^ mask) for i in range(n)])
@@ -225,13 +269,22 @@
     give = lax.dynamic_slice_in_dim(x, (1 - side) * half, half, 0)
     part = keep + swap(give, 1)
     mask = 2
+    work = list(work)
     while mask < n:
-        part = part + swap(part, mask if mask * 2 < n or mask < 8 else mask | (mask >> 1))
+        last = mask * 2 >= n
+        other = swap(part, mask if not last or mask < 8 else mask | (mask >> 1))
+        while work:
+            state = work.pop(0)(state, part)
+            other, state = lax.optimization_barrier((other, state))
+            if not last:
+                break
+        part = part + other
         mask *= 2
     other = swap(part, 1)
-    return jnp.where(
+    total = jnp.where(
         side == 0, jnp.concatenate([part, other], 0), jnp.concatenate([other, part], 0)
     )
+    return total, state
 
 
 def on_device(
@@ -255,37 +308,60 @@
     ridge = RIDGE_SHARE * members
     block = math.gcd(members, 256)
     place = lax.axis_index("col").astype(jnp.int32).reshape(1)
-    face = diffusivity.T
     coef = lax.all_to_all(jnp.tile(coeffs, (n, 1)), "col", 0, 0, tiled=True)
 
     rows_f32 = ((rows, R), F32)
     tend_out = ((rows, members), BF16)
     rate_out = ((members, R), F32)
     field_tmp = ((rows, block), F32)
-    chem = (counts, reactants, stoich, rate_consts, loss_rates)
-
-    def solve(coef, tend):
-        return call(
-            functools.partial(solve_kernel, ridge), 0,
-            [rate_out, rows_f32], [((R, R), BF16), ((R, R), BF16), ((R, R), F32)],
-            coef, tend,
-        )
-
-    diff, tend, rate, emis = call(
-        functools.partial(first_kernel, columns), 6,
-        [rows_f32, tend_out, rate_out, ((S, members), F32)], [field_tmp],
-        *chem, emis_table, mode_rows, face, coef, emis_idx.reshape(1, members),
+    square = ((R, R), F32)
+    square_bf = ((R, R), BF16)
+    chem = (counts, reactants.T, stoich.T, rate_consts, loss_rates)
+
+    def summed(rate, coef, tend):
+        def tied(part, *values):
+            return lax.optimization_barrier((part, values))[1]
+
+        def start(state, part):
+            (first,) = tied(part, coef)
+            return call(
+                functools.partial(inverse_start, ridge, 3), 0,
+                [square_bf, square_bf, square, SCALAR], [], first,
+            )
+
+        def more(state, part):
+            high, low, inv, gap = tied(part, *state)
+            inv, gap = call(
+                functools.partial(inverse_more, 3), 1, [square, SCALAR], [], gap, high, low, inv
+            )
+            return high, low, inv, gap
+
+        def end(state, part):
+            high, low, inv, gap = tied(part, *state)
+            return call(
+                inverse_end, 1, [rate_out, rows_f32], [square], gap, high, low, inv, coef, tend
+            )
+
+        return sum_over(rate, n, (start, more, end))
+
+    diff, emis, face = call(
+        functools.partial(setup_kernel, columns), 2,
+        [rows_f32, ((S, members), F32), ((columns * LEV, R), F32)], [],
+        counts, emis_table.T, mode_rows, diffusivity, emis_idx.reshape(1, members),
+    )
+    tend, rate = call(
+        functools.partial(first_kernel, columns), 5,
+        [tend_out, rate_out], [field_tmp],
+        *chem, diff, coef, emis,
     )
     for _ in range(NSUB - 1):
-        total = sum_over(rate, n)
-        solved, pull = solve(coef, tend)
+        total, (solved, pull) = summed(rate, coef, tend)
         diff, tend, rate, coef = call(
             functools.partial(middle_kernel, columns, total_rows), 5,
             [rows_f32, tend_out, rate_out, ((members, R), BF16)], [field_tmp],
             *chem, diff, pull, solved, total, coef, face, emis,
         )
-    total = sum_over(rate, n)
-    solved, pull = solve(coef, tend)
+    total, (solved, pull) = summed(rate, coef, tend)
     modes, coef_out = call(
         functools.partial(last_kernel, total_rows), 1,
         [rows_f32, ((mine, R), BF16)], [],

time: 78.1 us -> 65.8 us (0.84)
  waiting for transfers between devices: 40.1 us -> 25.4 us
  Pallas kernels: 19.9 us -> 24.2 us
  local copies, waits for them, and re-layouts: 5.31 us -> 3.8 us
    ppermute x10, waiting for transfers between devices: 35.1 us -> 20.8 us  [swap(): return lax.ppermute(value, 'col', [(i, i ^ mask) for i in range(n)])]
    pallas_call x5 -> x10, Pallas kernels: 19.9 us -> 24.2 us  [call(): pl.pallas_call(kernel, in_specs=scalars(n_scalar) + whole(len(args) - n_s...]
    unnamed x19 -> x16, local copies, waits for them, and re-layouts: 3.82 us -> 2.4 us
  transfers between devices with their start and end apart: 11 -> 11, of which waited for: 9 -> 11; matrix products, arithmetic and copies ran while one was open for 0% -> 0% of each run, Pallas kernels for 17% -> 27%
where the time goes in v2:
time: 65.8 us; the launch traced here: 65.3 us
  waiting for transfers between devices  25.4 us (39%)
  Pallas kernels  24.2 us (37%)
  starting transfers between devices  10.3 us (16%)
  local copies, waits for them, and re-layouts  3.8 us (6%)
  between operations  1.51 us (2%)
    pallas_call x10, Pallas kernels, call(): pl.pallas_call(kernel, in_specs=scalars(n_scalar) + whole(len(args) - n_s...  24.2 us
    ppermute x10, waiting for transfers between devices, swap(): return lax.ppermute(value, 'col', [(i, i ^ mask) for i in range(n)])  20.8 us
    all_to_all x1, starting transfers between devices, on_device(): coef = lax.all_to_all(jnp.tile(coeffs, (n, 1)), 'col', 0, 0, tiled=True)  7.39 us
    all_to_all x1, waiting for transfers between devices, on_device(): coef = lax.all_to_all(jnp.tile(coeffs, (n, 1)), 'col', 0, 0, tiled=True)  4.59 us
    ppermute x10, starting transfers between devices, swap(): return lax.ppermute(value, 'col', [(i, i ^ mask) for i in range(n)])  2.9 us
    unnamed x16, local copies, waits for them, and re-layouts  2.4 us
    another operation x1, local copies, waits for them, and re-layouts, on_device(): coef = lax.all_to_all(jnp.tile(coeffs, (n, 1)), 'col', 0, 0, tiled=True)  1.36 us
  transfers between devices with their start and end apart: 11, of which 11 were waited for; matrix products, arithmetic and copies ran while one was open for 0% of the time, Pallas kernels for 27%

profile of v2, /device:TPU:0, one launch (start us, length us, event | category | flops | bytes accessed | tf_op | source)
XLA Modules:
  0.0 65.3 jit_solution(9601130882540894781)
XLA Ops:
  0.6 1.4 %tile.2 = bf16[16,16,256]{2,1,0:T(8,128)(2,1)} broadcast(bf16[16,256]{1,0:T(8,128)(2,1)} %param.11), dimensions={1,2} | broadcast | bytes 139264 | tf_op jit(solution)/shard_map/tile | solution.py:311
  2.0 7.4 %all-to-all-start = ((bf16[16,16,256]{2,1,0:T(8,128)(2,1)}), bf16[16,16,256]{2,1,0:T(8,128)(2,1)S(1)}, u32[]{:S(2)}, u32[]{:S(2)}) async-start(bf16[16,16,256]{2,1,0:T(8,128)(2,1)} %tile.2), calls=%async_computation | async-start | bytes 262144 | tf_op jit(solution)/shard_map/all_to_all | solution.py:311
  9.4 0.0 copy-start.2
  10.1 0.0 copy-start.6
  10.1 0.0 copy-start.7
  10.1 0.0 copy-done.2
  10.1 0.6 copy-done.6
  10.7 0.0 copy-done.7
  10.7 0.0 copy-start
  10.7 1.0 %copy-done = f32[512,256]{1,0:T(8,128)S(1)} copy-done((f32[512,256]{1,0:T(8,128)S(1)}, f32[512,256]{1,0:T(8,128)}, u32[]{:S(2)}) %copy-start) | copy-done | bytes 524312
  11.8 0.0 copy-start.5
  11.8 0.9 %shard_map.113 = (f32[512,256]{1,0:T(8,128)S(1)}, f32[8,256]{1,0:T(8,128)S(1)}, f32[64,256]{1,0:T(8,128)S(1)}) custom-call(s32[1]{0:T(128)S(6)} %copy.12.counts_ref, f32[8,16]{1,0:T(8,128)S(1)} %bitcast.12, f32[512,256]{1,0:T(8,128)S(1)} %copy-done, f32[1,64]{1,0:T(1,128)S(1)} %copy-done.7, s32[1,256]{1,0:T(1,128)S(1)} %bitcast.15), custom_call_target="tpu_custom_call" | custom-call | tf_op jit(solution)/shard_map/pallas_call | solution.py:244
  12.7 4.6 %all-to-all-done = bf16[16,16,256]{2,1,0:T(8,128)(2,1)S(1)} async-done(((bf16[16,16,256]{2,1,0:T(8,128)(2,1)}), bf16[16,16,256]{2,1,0:T(8,128)(2,1)S(1)}, u32[]{:S(2)}, u32[]{:S(2)}) %all-to-all-start) | async-done | bytes 131104 | tf_op jit(solution)/shard_map/all_to_all | solution.py:311
  17.3 0.0 copy-start.1
  17.3 0.0 copy-start.3
  17.3 0.0 copy-start.4
  17.3 0.0 copy-done.5
  17.3 0.7 %copy-done.1 = s32[12,8]{0,1:T(8,128)S(1)} copy-done((s32[12,8]{0,1:T(8,128)S(1)}, s32[12,8]{0,1:T(8,128)}, u32[]{:S(2)}) %copy-start.1) | copy-done | bytes 408
  18.0 0.0 copy-done.3
  18.0 0.0 copy-done.4
  18.0 2.0 %shard_map.114 = (bf16[512,256]{1,0:T(8,128)(2,1)S(1)}, f32[256,256]{1,0:T(8,128)S(1)}) custom-call(s32[1]{0:T(128)S(6)} %copy.12.counts_ref, s32[2,12]{1,0:T(2,128)S(1)} %bitcast.13, s32[8,12]{1,0:T(8,128)S(1)} %bitcast.10, f32[12]{0:T(128)S(1)} %copy-done.4, f32[8]{0:T(128)S(1)} %copy-done.5, f32[512,256]{1,0:T(8,128)S(1)} %get-tuple-element.71.diff_ref.diff_in_ref, ...), custom_call_target="tpu_custom_call" | custom-call | tf_op jit(solution)/shard_map/pallas_call | solution.py:244
  20.0 0.1 collective-permute-start
  20.1 1.3 %collective-permute-done = f32[128,256]{1,0:T(8,128)S(1)} collective-permute-done((f32[128,256]{1,0:T(8,128)S(1)}, f32[128,256]{1,0:T(8,128)S(1)}, u32[]{:S(2)}, u32[]{:S(2)}) %collective-permute-start) | collective-permute-done | bytes 131104 | tf_op jit(solution)/shard_map/ppermute | solution.py:264
  21.4 0.1 collective-permute-start.1
  21.5 2.7 %shard_map.115 = (bf16[256,256]{1,0:T(8,128)(2,1)S(1)}, bf16[256,256]{1,0:T(8,128)(2,1)S(1)}, f32[256,256]{1,0:T(8,128)S(1)}, f32[1]{0:T(128)}) custom-call(bf16[256,256]{1,0:T(8,128)(2,1)S(1)} %bitcast.7), custom_call_target="tpu_custom_call" | custom-call | tf_op jit(solution)/shard_map/pallas_call | solution.py:244
  24.3 2.8 %collective-permute-done.1 = f32[128,256]{1,0:T(8,128)S(1)} collective-permute-done((f32[128,256]{1,0:T(8,128)S(1)}, f32[128,256]{1,0:T(8,128)S(1)}, u32[]{:S(2)}, u32[]{:S(2)}) %collective-permute-start.1) | collective-permute-done | bytes 131104 | tf_op jit(solution)/shard_map/ppermute | solution.py:264
  27.1 0.1 collective-permute-start.2
  27.2 3.0 %shard_map.116 = (f32[256,256]{1,0:T(8,128)S(1)}, f32[1]{0:T(128)}) custom-call(f32[1]{0:T(128)} %get-tuple-element.86.gap_in_ref, bf16[256,256]{1,0:T(8,128)(2,1)S(1)} %get-tuple-element.96.high_ref, bf16[256,256]{1,0:T(8,128)(2,1)S(1)} %get-tuple-element.97.low_ref, f32[256,256]{1,0:T(8,128)S(1)} %get-tuple-element.87.inv_in_ref), custom_call_target="tpu_custom_call" | custom-call | tf_op jit(solution)/shard_map/pallas_call | solution.py:244
  30.2 1.9 %collective-permute-done.2 = f32[128,256]{1,0:T(8,128)S(1)} collective-permute-done((f32[128,256]{1,0:T(8,128)S(1)}, f32[128,256]{1,0:T(8,128)S(1)}, u32[]{:S(2)}, u32[]{:S(2)}) %collective-permute-start.2) | collective-permute-done | bytes 131104 | tf_op jit(solution)/shard_map/ppermute | solution.py:264
  32.1 0.8 %collective-permute-start.3 = (f32[128,256]{1,0:T(8,128)S(1)}, f32[128,256]{1,0:T(8,128)S(1)}, u32[]{:S(2)}, u32[]{:S(2)}) collective-permute-start(f32[128,256]{1,0:T(8,128)S(1)} %add.36), channel_id=1, source_target_pairs={{0,12},{1,13},{2,14},{3,15},{4,8},{5,9},{6,10},{7,11},{8,4},{9,5},... | collective-permute-start | bytes 393224 | tf_op jit(solution)/shard_map/ppermute | solution.py:264
  33.0 2.7 %shard_map.117 = (f32[256,256]{1,0:T(8,128)S(1)}, f32[512,256]{1,0:T(8,128)S(1)}) custom-call(f32[1]{0:T(128)} %get-tuple-element.95.gap_in_ref, bf16[256,256]{1,0:T(8,128)(2,1)S(1)} %get-tuple-element.96.high_ref, bf16[256,256]{1,0:T(8,128)(2,1)S(1)} %get-tuple-element.97.low_ref, f32[256,256]{1,0:T(8,128)S(1)} %get-tuple-element.98.inv_in_ref, ...), custom_call_target="tpu_custom_call" | custom-call | tf_op jit(solution)/shard_map/pallas_call | solution.py:244
  35.6 3.4 %collective-permute-done.3 = f32[128,256]{1,0:T(8,128)S(1)} collective-permute-done((f32[128,256]{1,0:T(8,128)S(1)}, f32[128,256]{1,0:T(8,128)S(1)}, u32[]{:S(2)}, u32[]{:S(2)}) %collective-permute-start.3) | collective-permute-done | bytes 131104 | tf_op jit(solution)/shard_map/ppermute | solution.py:264
  39.0 0.1 collective-permute-start.4
  39.1 1.3 %collective-permute-done.4 = f32[128,256]{1,0:T(8,128)S(1)} collective-permute-done((f32[128,256]{1,0:T(8,128)S(1)}, f32[128,256]{1,0:T(8,128)S(1)}, u32[]{:S(2)}, u32[]{:S(2)}) %collective-permute-start.4) | collective-permute-done | bytes 131104 | tf_op jit(solution)/shard_map/ppermute | solution.py:264
  40.4 2.8 %shard_map.118 = (f32[512,256]{1,0:T(8,128)S(1)}, bf16[512,256]{1,0:T(8,128)(2,1)S(1)}, f32[256,256]{1,0:T(8,128)S(1)}, bf16[256,256]{1,0:T(8,128)(2,1)S(1)}) custom-call(s32[1]{0:T(128)S(6)} %copy.12.counts_ref, s32[2,12]{1,0:T(2,128)S(1)} %bitcast.14, s32[8,12]{1,0:T(8,128)S(1)} %bitcast.11, f32[12]{0:T(128)S(1)} %copy-done.4, f32[8]{0:T(128)S(1)} %copy-done.5, ...), custom_call_target="tpu_custom_call" | custom-call | tf_op jit(solution)/shard_map/pallas_call | solution.py:244
  43.3 0.2 collective-permute-start.5
  43.5 1.2 %collective-permute-done.5 = f32[128,256]{1,0:T(8,128)S(1)} collective-permute-done((f32[128,256]{1,0:T(8,128)S(1)}, f32[128,256]{1,0:T(8,128)S(1)}, u32[]{:S(2)}, u32[]{:S(2)}) %collective-permute-start.5) | collective-permute-done | bytes 131104 | tf_op jit(solution)/shard_map/ppermute | solution.py:264
  44.7 0.5 collective-permute-start.6
  45.3 2.8 %shard_map.119 = (bf16[256,256]{1,0:T(8,128)(2,1)S(1)}, bf16[256,256]{1,0:T(8,128)(2,1)S(1)}, f32[256,256]{1,0:T(8,128)S(1)}, f32[1]{0:T(128)}) custom-call(bf16[256,256]{1,0:T(8,128)(2,1)S(1)} %get-tuple-element.109.coef_ref), custom_call_target="tpu_custom_call" | custom-call | tf_op jit(solution)/shard_map/pallas_call | solution.py:244
  48.0 2.3 %collective-permute-done.6 = f32[128,256]{1,0:T(8,128)S(1)} collective-permute-done((f32[128,256]{1,0:T(8,128)S(1)}, f32[128,256]{1,0:T(8,128)S(1)}, u32[]{:S(2)}, u32[]{:S(2)}) %collective-permute-start.6) | collective-permute-done | bytes 131104 | tf_op jit(solution)/shard_map/ppermute | solution.py:264
  50.4 0.1 collective-permute-start.7
  50.5 3.0 %shard_map.120 = (f32[256,256]{1,0:T(8,128)S(1)}, f32[1]{0:T(128)}) custom-call(f32[1]{0:T(128)} %get-tuple-element.121.gap_in_ref, bf16[256,256]{1,0:T(8,128)(2,1)S(1)} %get-tuple-element.131.high_ref, bf16[256,256]{1,0:T(8,128)(2,1)S(1)} %get-tuple-element.132.low_ref, f32[256,256]{1,0:T(8,128)S(1)} %get-tuple-element.122.inv_in_ref), custom_call_target="tpu_custom_call" | custom-call | tf_op jit(solution)/shard_map/pallas_call | solution.py:244
  53.5 1.9 %collective-permute-done.7 = f32[128,256]{1,0:T(8,128)S(1)} collective-permute-done((f32[128,256]{1,0:T(8,128)S(1)}, f32[128,256]{1,0:T(8,128)S(1)}, u32[]{:S(2)}, u32[]{:S(2)}) %collective-permute-start.7) | collective-permute-done | bytes 131104 | tf_op jit(solution)/shard_map/ppermute | solution.py:264
  55.4 0.9 %collective-permute-start.8 = (f32[128,256]{1,0:T(8,128)S(1)}, f32[128,256]{1,0:T(8,128)S(1)}, u32[]{:S(2)}, u32[]{:S(2)}) collective-permute-start(f32[128,256]{1,0:T(8,128)S(1)} %add.40), channel_id=1, source_target_pairs={{0,12},{1,13},{2,14},{3,15},{4,8},{5,9},{6,10},{7,11},{8,4},{9,5},... | collective-permute-start | bytes 393224 | tf_op jit(solution)/shard_map/ppermute | solution.py:264
  56.3 2.7 %shard_map.121 = (f32[256,256]{1,0:T(8,128)S(1)}, f32[512,256]{1,0:T(8,128)S(1)}) custom-call(f32[1]{0:T(128)} %get-tuple-element.130.gap_in_ref, bf16[256,256]{1,0:T(8,128)(2,1)S(1)} %get-tuple-element.131.high_ref, bf16[256,256]{1,0:T(8,128)(2,1)S(1)} %get-tuple-element.132.low_ref, f32[256,256]{1,0:T(8,128)S(1)} %get-tuple-element.133.inv_in_ref, ...), custom_call_target="tpu_custom_call" | custom-call | tf_op jit(solution)/shard_map/pallas_call | solution.py:244
  59.0 3.3 %collective-permute-done.8 = f32[128,256]{1,0:T(8,128)S(1)} collective-permute-done((f32[128,256]{1,0:T(8,128)S(1)}, f32[128,256]{1,0:T(8,128)S(1)}, u32[]{:S(2)}, u32[]{:S(2)}) %collective-permute-start.8) | collective-permute-done | bytes 131104 | tf_op jit(solution)/shard_map/ppermute | solution.py:264
  62.3 0.1 collective-permute-start.9
  62.4 1.3 %collective-permute-done.9 = f32[128,256]{1,0:T(8,128)S(1)} collective-permute-done((f32[128,256]{1,0:T(8,128)S(1)}, f32[128,256]{1,0:T(8,128)S(1)}, u32[]{:S(2)}, u32[]{:S(2)}) %collective-permute-start.9) | collective-permute-done | bytes 131104 | tf_op jit(solution)/shard_map/ppermute | solution.py:264
  63.7 1.6 %shard_map.122 = (f32[512,256]{1,0:T(8,128)}, bf16[16,256]{1,0:T(8,128)(2,1)}) custom-call(s32[1]{0:T(128)} %bitcast.place_ref, f32[512,256]{1,0:T(8,128)S(1)} %get-tuple-element.106.diff_in_ref, f32[512,256]{1,0:T(8,128)S(1)} %get-tuple-element.137.pull_ref, f32[256,256]{1,0:T(8,128)S(1)} %get-tuple-element.138.solve_ref, ...), custom_call_target="tpu_custom_call" | custom-call | tf_op jit(solution)/shard_map/pallas_call | solution.py:244
  (12 shorter events, 0.2 us)
Async XLA Ops:
  2.0 15.3 %all-to-all-start = ((bf16[16,16,256]{2,1,0:T(8,128)(2,1)}), bf16[16,16,256]{2,1,0:T(8,128)(2,1)S(1)}, u32[]{:S(2)}, u32[]{:S(2)}) async-start(bf16[16,16,256]{2,1,0:T(8,128)(2,1)} %tile.2), calls=%async_computation | async-start | bytes 262144 | tf_op jit(solution)/shard_map/all_to_all | solution.py:311
  9.4 0.7 %copy-start.2 = (f32[16,8]{0,1:T(8,128)S(1)}, f32[16,8]{0,1:T(8,128)}, u32[]{:S(2)}) copy-start(f32[16,8]{0,1:T(8,128)} %param.15) | copy-start | bytes 1540
  10.1 0.7 %copy-start.6 = (s32[256]{0:T(256)S(1)}, s32[256]{0:T(256)}, u32[]{:S(2)}) copy-start(s32[256]{0:T(256)} %param.14) | copy-start | bytes 3076
  10.1 0.7 %copy-start.7 = (f32[1,64]{1,0:T(1,128)S(1)}, f32[1,64]{1,0:T(1,128)}, u32[]{:S(2)}) copy-start(f32[1,64]{1,0:T(1,128)} %level_face_ref.1) | copy-start | bytes 772
  10.7 1.0 %copy-start = (f32[512,256]{1,0:T(8,128)S(1)}, f32[512,256]{1,0:T(8,128)}, u32[]{:S(2)}) copy-start(f32[512,256]{1,0:T(8,128)} %modes_ref.1) | copy-start | bytes 1572868
  11.8 5.5 %copy-start.5 = (f32[8]{0:T(128)S(1)}, f32[8]{0:T(128)}, u32[]{:S(2)}) copy-start(f32[8]{0:T(128)} %loss_ref.3) | copy-start | bytes 100
  17.3 0.7 %copy-start.1 = (s32[12,8]{0,1:T(8,128)S(1)}, s32[12,8]{0,1:T(8,128)}, u32[]{:S(2)}) copy-start(s32[12,8]{0,1:T(8,128)} %param.17) | copy-start | bytes 1156
  17.3 0.7 %copy-start.3 = (s32[12,2]{0,1:T(2,128)S(1)}, s32[12,2]{0,1:T(2,128)}, u32[]{:S(2)}) copy-start(s32[12,2]{0,1:T(2,128)} %param.16) | copy-start | bytes 292
  17.3 0.7 %copy-start.4 = (f32[12]{0:T(128)S(1)}, f32[12]{0:T(128)}, u32[]{:S(2)}) copy-start(f32[12]{0:T(128)} %speed_ref.3) | copy-start | bytes 148
  20.0 1.4 %collective-permute-start = (f32[128,256]{1,0:T(8,128)S(1)}, f32[128,256]{1,0:T(8,128)S(1)}, u32[]{:S(2)}, u32[]{:S(2)}) collective-permute-start(f32[128,256]{1,0:T(8,128)S(1)} %constant_dynamic-slice_fusion.1), channel_id=1, source_target_pairs={{0,1},{1,0},{2,3},{3,2},{4,5},{5,4},{6,7},{7,6},{8,9},{9,8},{10,11... | collective-permute-start | bytes 393224 | tf_op jit(solution)/shard_map/ppermute | solution.py:264
  21.4 5.6 %collective-permute-start.1 = (f32[128,256]{1,0:T(8,128)S(1)}, f32[128,256]{1,0:T(8,128)S(1)}, u32[]{:S(2)}, u32[]{:S(2)}) collective-permute-start(f32[128,256]{1,0:T(8,128)S(1)} %dynamic-slice_add_fusion.1), channel_id=1, source_target_pairs={{0,2},{1,3},{2,0},{3,1},{4,6},{5,7},{6,4},{7,5},{8,10},{9,11},{10,... | collective-permute-start | bytes 393224 | tf_op jit(solution)/shard_map/ppermute | solution.py:264
  27.1 5.0 %collective-permute-start.2 = (f32[128,256]{1,0:T(8,128)S(1)}, f32[128,256]{1,0:T(8,128)S(1)}, u32[]{:S(2)}, u32[]{:S(2)}) collective-permute-start(f32[128,256]{1,0:T(8,128)S(1)} %add.35), channel_id=1, source_target_pairs={{0,4},{1,5},{2,6},{3,7},{4,0},{5,1},{6,2},{7,3},{8,12},{9,13},{10,... | collective-permute-start | bytes 393224 | tf_op jit(solution)/shard_map/ppermute | solution.py:264
  32.1 6.8 %collective-permute-start.3 = (f32[128,256]{1,0:T(8,128)S(1)}, f32[128,256]{1,0:T(8,128)S(1)}, u32[]{:S(2)}, u32[]{:S(2)}) collective-permute-start(f32[128,256]{1,0:T(8,128)S(1)} %add.36), channel_id=1, source_target_pairs={{0,12},{1,13},{2,14},{3,15},{4,8},{5,9},{6,10},{7,11},{8,4},{9,5},... | collective-permute-start | bytes 393224 | tf_op jit(solution)/shard_map/ppermute | solution.py:264
  39.0 1.4 %collective-permute-start.4 = (f32[128,256]{1,0:T(8,128)S(1)}, f32[128,256]{1,0:T(8,128)S(1)}, u32[]{:S(2)}, u32[]{:S(2)}) collective-permute-start(f32[128,256]{1,0:T(8,128)S(1)} %add.37), channel_id=1, source_target_pairs={{0,1},{1,0},{2,3},{3,2},{4,5},{5,4},{6,7},{7,6},{8,9},{9,8},{10,11... | collective-permute-start | bytes 393224 | tf_op jit(solution)/shard_map/ppermute | solution.py:264
  43.3 1.4 %collective-permute-start.5 = (f32[128,256]{1,0:T(8,128)S(1)}, f32[128,256]{1,0:T(8,128)S(1)}, u32[]{:S(2)}, u32[]{:S(2)}) collective-permute-start(f32[128,256]{1,0:T(8,128)S(1)} %constant_dynamic-slice_fusion), channel_id=1, source_target_pairs={{0,1},{1,0},{2,3},{3,2},{4,5},{5,4},{6,7},{7,6},{8,9},{9,8},{10,11... | collective-permute-start | bytes 393224 | tf_op jit(solution)/shard_map/ppermute | solution.py:264
  44.7 5.6 %collective-permute-start.6 = (f32[128,256]{1,0:T(8,128)S(1)}, f32[128,256]{1,0:T(8,128)S(1)}, u32[]{:S(2)}, u32[]{:S(2)}) collective-permute-start(f32[128,256]{1,0:T(8,128)S(1)} %dynamic-slice_add_fusion), channel_id=1, source_target_pairs={{0,2},{1,3},{2,0},{3,1},{4,6},{5,7},{6,4},{7,5},{8,10},{9,11},{10,... | collective-permute-start | bytes 393224 | tf_op jit(solution)/shard_map/ppermute | solution.py:264
  50.4 5.0 %collective-permute-start.7 = (f32[128,256]{1,0:T(8,128)S(1)}, f32[128,256]{1,0:T(8,128)S(1)}, u32[]{:S(2)}, u32[]{:S(2)}) collective-permute-start(f32[128,256]{1,0:T(8,128)S(1)} %add.39), channel_id=1, source_target_pairs={{0,4},{1,5},{2,6},{3,7},{4,0},{5,1},{6,2},{7,3},{8,12},{9,13},{10,... | collective-permute-start | bytes 393224 | tf_op jit(solution)/shard_map/ppermute | solution.py:264
  55.4 6.8 %collective-permute-start.8 = (f32[128,256]{1,0:T(8,128)S(1)}, f32[128,256]{1,0:T(8,128)S(1)}, u32[]{:S(2)}, u32[]{:S(2)}) collective-permute-start(f32[128,256]{1,0:T(8,128)S(1)} %add.40), channel_id=1, source_target_pairs={{0,12},{1,13},{2,14},{3,15},{4,8},{5,9},{6,10},{7,11},{8,4},{9,5},... | collective-permute-start | bytes 393224 | tf_op jit(solution)/shard_map/ppermute | solution.py:264
  62.3 1.4 %collective-permute-start.9 = (f32[128,256]{1,0:T(8,128)S(1)}, f32[128,256]{1,0:T(8,128)S(1)}, u32[]{:S(2)}, u32[]{:S(2)}) collective-permute-start(f32[128,256]{1,0:T(8,128)S(1)} %add.41), channel_id=1, source_target_pairs={{0,1},{1,0},{2,3},{3,2},{4,5},{5,4},{6,7},{7,6},{8,9},{9,8},{10,11... | collective-permute-start | bytes 393224 | tf_op jit(solution)/shard_map/ppermute | solution.py:264

commit v3 on v2

v3 whole, which is shorter than its diff:
```python
import functools
import math

import jax
import jax.numpy as jnp
from jax import lax
from jax.experimental import pallas as pl
from jax.experimental.pallas import tpu as pltpu
from jax.sharding import PartitionSpec as P

S = 8
LEV = 64
R = 256
NREAC = 12
NEMIS = 16
NSUB = 2

TIME_STEP = 0.1
RATE_STEP = 0.3
RIDGE_SHARE = 0.05

F32 = jnp.float32
BF16 = jnp.bfloat16

NN = (((1,), (0,)), ((), ()))
NT = (((1,), (1,)), ((), ()))
TN = (((0,), (0,)), ((), ()))


def mm(a, b, dims=NN):
    return lax.dot_general(a, b, dims, preferred_element_type=F32)


def split(x):
    high = x.astype(BF16)
    return high, (x - high.astype(F32)).astype(BF16)


def mm3(a, b, dims=NN):
    return mm(a[0], b[0], dims) + (mm(a[0], b[1], dims) + mm(a[1], b[0], dims))


def diffuse_rows(modes, face_ref):
    faces = []
    for c in range(face_ref.shape[0] // LEV):
        faces += [face_ref[c * LEV : (c + 1) * LEV, :]] * S
    face = jnp.concatenate(faces, axis=0)
    rows = modes.shape[0]
    flux = face * (pltpu.roll(modes, rows - 1, 0) - modes)
    return modes + flux - pltpu.roll(flux, 1, 0)


def react(
    diffused, coef_ref, emis_ref, counts_ref, pair_ref, weight_ref,
    field_ref, tend_ref, rate_ref, top_ref, columns,
):
    mode_bf = diffused.astype(BF16)
    members = coef_ref.shape[0]
    block = math.gcd(members, 256)
    step = 16
    steps = LEV // step
    largest = jnp.full((1, R), 2.0**-120, F32)
    for b in range(members // block):
        lanes = slice(b * block, (b + 1) * block)
        field_ref[...] = mm(mode_bf, coef_ref[lanes, :], NT) * (1.0 / math.sqrt(R))

        def part(i, _):
            c = i // steps
            low = (i - c * steps) * step
            base = c * (S * LEV) + low
            level = lax.broadcasted_iota(jnp.int32, (step, block), 0) + low
            profile = jnp.exp(level.astype(F32) * (-4.0 / LEV))
            live = level < counts_ref[c]

            def amount(s):
                return field_ref[pl.ds(pl.multiple_of(base + s * LEV, step), step), :]

            total = []
            for s in range(S):
                total.append(emis_ref[s : s + 1, lanes] * profile - weight_ref[s, NREAC] * amount(s))
            for r in range(NREAC):
                speed = amount(pair_ref[0, r]) * amount(pair_ref[1, r])
                for s in range(S):
                    total[s] = total[s] + weight_ref[s, r] * speed
            for s in range(S):
                tend_ref[pl.ds(pl.multiple_of(base + s * LEV, step), step), lanes] = jnp.where(
                    live, total[s], 0.0
                ).astype(BF16)
            return 0

        lax.fori_loop(0, columns * steps, part, 0)
        rate = mm(tend_ref[:, lanes], mode_bf, TN)
        rate_ref[lanes, :] = rate
        largest = jnp.maximum(largest, jnp.max(jnp.abs(rate), axis=0, keepdims=True))
    power = jnp.maximum(jnp.floor(jnp.log(largest) * (1.0 / math.log(2.0))) + 2.0, -100.0)
    top_ref[...] = jnp.broadcast_to(power, top_ref.shape)


def setup_kernel(
    columns,
    counts_ref, table_ref,
    modes_ref, level_face_ref, idx_ref,
    diff_ref, emis_ref, face_ref,
):
    index = idx_ref[...]
    for s in range(S):
        row = jnp.zeros(index.shape, F32)
        for k in range(NEMIS):
            row = jnp.where(index == k, table_ref[s, k], row)
        emis_ref[s : s + 1, :] = row
    down = lax.broadcasted_iota(jnp.int32, (LEV, LEV), 0)
    across = lax.broadcasted_iota(jnp.int32, (LEV, LEV), 1)
    for c in range(columns):
        inner = (down == across) & (down + 1 < counts_ref[c])
        face = jnp.sum(jnp.where(inner, level_face_ref[c : c + 1, :], 0.0), axis=1, keepdims=True)
        face_ref[c * LEV : (c + 1) * LEV, :] = jnp.broadcast_to(face, (LEV, R))
    diff_ref[...] = diffuse_rows(modes_ref[...], face_ref)


def first_kernel(
    columns, plan,
    counts_ref, pair_ref, weight_ref,
    diff_ref, emis_ref, *refs,
):
    if plan:
        chip_ref, mine_ref, theirs_ref, tend_ref, rate_ref, top_ref, coef_ref, field_ref = refs
        rows = chip_ref.shape[0]
        place = lax.axis_index("col")
        chip, side = place // 2, place % 2
        for j, pair in enumerate(plan):
            for ref, mask in (
                (mine_ref, jnp.where(side == 0, pair[0], pair[1])),
                (theirs_ref, jnp.where(side == 0, pair[1], pair[0])),
            ):
                spot = pl.multiple_of((chip ^ mask) * rows, rows)
                coef_ref[pl.ds(spot, rows), :] = ref[j * rows : (j + 1) * rows, :]
        coef_ref[pl.ds(pl.multiple_of(chip * rows, rows), rows), :] = chip_ref[...]
    else:
        coef_ref, tend_ref, rate_ref, top_ref, field_ref = refs
    react(
        diff_ref[...], coef_ref, emis_ref, counts_ref, pair_ref, weight_ref,
        field_ref, tend_ref, rate_ref, top_ref, columns,
    )


def advance(diffused, pull, solve_ref, rate):
    transfer = mm3(split(rate), split(solve_ref[...]), TN)
    moved = mm3(split(diffused), split(transfer))
    return diffused + (TIME_STEP * math.sqrt(R)) * (pull - moved)


def middle_kernel(
    columns, total_rows,
    counts_ref, pair_ref, weight_ref,
    diff_in_ref, pull_ref, solve_ref, sum_ref, coef_ref, face_ref, emis_ref,
    diff_ref, tend_ref, rate_ref, top_ref, coef_out_ref,
    field_ref,
):
    raw = sum_ref[...]
    coef_out_ref[...] = (
        coef_ref[...].astype(F32) + RATE_STEP * (raw * (math.sqrt(R) / total_rows))
    ).astype(BF16)
    modes = advance(diff_in_ref[...], pull_ref[...], solve_ref, raw * (1.0 / total_rows))
    diffused = diffuse_rows(modes, face_ref)
    diff_ref[...] = diffused
    react(
        diffused, coef_out_ref, emis_ref, counts_ref, pair_ref, weight_ref,
        field_ref, tend_ref, rate_ref, top_ref, columns,
    )


def last_kernel(
    total_rows,
    diff_in_ref, pull_ref, solve_ref, sum_ref, coef_ref,
    modes_ref, coef_out_ref,
):
    mine = coef_out_ref.shape[0]
    own = pl.ds(pl.multiple_of(lax.axis_index("col") * mine, mine), mine)
    coef_out_ref[...] = (
        coef_ref[own, :].astype(F32)
        + RATE_STEP * (sum_ref[own, :] * (math.sqrt(R) / total_rows))
    ).astype(BF16)
    modes_ref[...] = advance(
        diff_in_ref[...], pull_ref[...], solve_ref, sum_ref[...] * (1.0 / total_rows)
    )


def identity():
    return (
        lax.broadcasted_iota(jnp.int32, (R, R), 0) == lax.broadcasted_iota(jnp.int32, (R, R), 1)
    ).astype(F32)


def refine(eye, high_ref, low_ref, inv_ref, gap):
    square = gap * gap
    factor = 2.0 / (2.0 - square)
    inv = inv_ref[...]
    halves = split(inv)
    rest = eye - mm3((high_ref[...], low_ref[...]), halves)
    inv_ref[...] = factor * (inv + mm3(halves, split(rest)))
    return square / (2.0 - square)


def inverse_start(ridge, steps, coef_ref, high_ref, low_ref, inv_ref, gap_ref):
    coef = coef_ref[...]
    eye = identity()
    gram = mm(coef, coef, TN) + ridge * eye
    top = jnp.max(jnp.sum(jnp.abs(gram), axis=0, keepdims=True))
    high_ref[...], low_ref[...] = split(gram)
    scale = 2.0 / (top + ridge)
    gap = (top - ridge) / (top + ridge)
    square = gap * gap
    factor = 2.0 / (2.0 - square)
    inv_ref[...] = (factor * scale) * (2.0 * eye - scale * gram)
    gap = lax.fori_loop(
        0, steps, lambda i, gap: refine(eye, high_ref, low_ref, inv_ref, gap),
        square / (2.0 - square),
    )
    gap_ref[...] = jnp.full(gap_ref.shape, gap, F32)


def inverse_end(
    gap_in_ref, high_ref, low_ref, inv_in_ref, coef_ref, tend_ref, solve_ref, pull_ref, inv_ref
):
    eye = identity()
    inv_ref[...] = inv_in_ref[...]
    lax.while_loop(
        lambda gap: gap > 1e-5,
        lambda gap: refine(eye, high_ref, low_ref, inv_ref, gap),
        jnp.max(gap_in_ref[...]),
    )
    coef = coef_ref[...]
    high, low = split(inv_ref[...])
    solve = mm(coef, high) + mm(coef, low)
    solve_ref[...] = solve
    high, low = split(solve)
    pull_ref[...] = mm(tend_ref[...], high) + mm(tend_ref[...], low)


VMEM_LIMIT = 48 * 1024 * 1024


def whole(n):
    return [pl.BlockSpec(memory_space=pltpu.VMEM)] * n


def scalars(n):
    return [pl.BlockSpec(memory_space=pltpu.SMEM)] * n


def call(kernel, n_scalar, outs, scratch, *args):
    return pl.pallas_call(
        kernel,
        in_specs=scalars(n_scalar) + whole(len(args) - n_scalar),
        out_specs=whole(len(outs)),
        out_shape=[jax.ShapeDtypeStruct(shape, dtype) for shape, dtype in outs],
        scratch_shapes=[pltpu.VMEM(shape, dtype) for shape, dtype in scratch],
        compiler_params=pltpu.CompilerParams(vmem_limit_bytes=VMEM_LIMIT),
    )(*args)


def tied(value, first):
    return lax.optimization_barrier((first, value))[1]


def swap(value, n, masks):
    return lax.ppermute(value, "col", [(i, i ^ masks[i % 2]) for i in range(n) if masks[i % 2]])


EXTRA = 8
LIFT = 15.0


def encode(part, power):
    scaled = (part * jnp.exp2(LIFT - power)).astype(jnp.float16)
    powers = jnp.broadcast_to(power, (EXTRA, R)).astype(jnp.float16)
    return lax.optimization_barrier(jnp.concatenate([scaled, powers], 0))


def decode(message):
    rows = message.shape[0] - EXTRA
    power = message[rows : rows + 1].astype(F32)
    return message[:rows].astype(F32) * jnp.exp2(power - LIFT), power


def sum_over(x, top, n, work):
    state = ()
    work = list(work)
    if n & (n - 1) or n < 4:
        while work:
            state = work.pop(0)(state, x)
        return lax.psum(x, "col"), state
    half = x.shape[0] // 2
    side = lax.axis_index("col") & 1
    keep = lax.dynamic_slice_in_dim(x, side * half, half, 0)
    give = lax.dynamic_slice_in_dim(x, (1 - side) * half, half, 0)
    got = swap(jnp.concatenate([give, top], 0), n, (1, 1))
    part = keep + got[:half]
    power = jnp.maximum(top[:1], got[half : half + 1]) + 1.0
    mask = 2
    while mask < n:
        masks = [mask, mask * 2, mask * 3] if mask * 2 < n else [mask]
        message = encode(part, power)
        others = [swap(message, n, (m, m)) for m in masks]
        mask *= 4 if len(masks) == 3 else 2
        while work:
            state = work.pop(0)(state, message)
            others, state = lax.optimization_barrier((others, state))
            if mask < n:
                break
        part, power = decode(message)
        for other in others:
            more, high = decode(other)
            part = part + more
            power = jnp.maximum(power, high)
        power = power + float(len(masks))
    other = swap(part, n, (1, 1))
    total = jnp.where(
        side == 0, jnp.concatenate([part, other], 0), jnp.concatenate([other, part], 0)
    )
    return total, state


def on_device(
    mode_rows,
    coeffs,
    diffusivity,
    counts,
    emis_idx,
    emis_table,
    reactants,
    stoich,
    rate_consts,
    loss_rates,
):
    n = lax.axis_size("col")
    rows = mode_rows.shape[0]
    total_rows = rows * n
    mine = coeffs.shape[0]
    members = mine * n
    columns = counts.shape[0]
    ridge = RIDGE_SHARE * members
    block = math.gcd(members, 256)
    rows_f32 = ((rows, R), F32)
    tend_out = ((rows, members), BF16)
    rate_out = ((members, R), F32)
    top_out = ((EXTRA, R), F32)
    coef_out = ((members, R), BF16)
    field_tmp = ((rows, block), F32)
    square = ((R, R), F32)
    square_bf = ((R, R), BF16)
    weights = stoich.astype(F32).T * rate_consts[None, :]
    chem = (counts, reactants.T, jnp.concatenate([weights, loss_rates[:, None]], 1))

    def setup(modes):
        return call(
            functools.partial(setup_kernel, columns), 2,
            [rows_f32, ((S, members), F32), ((columns * LEV, R), F32)], [],
            counts, emis_table.T, modes, diffusivity, emis_idx.reshape(1, members),
        )

    if n == 16:
        plan = ((1, 4), (2, 5), (3, 6), (0, 7))
        other = swap(coeffs, n, (1, 1))
        side = lax.axis_index("col") & 1
        chip = jnp.where(
            side == 0, jnp.concatenate([coeffs, other], 0), jnp.concatenate([other, coeffs], 0)
        )
        fetched = [swap(chip, n, (2 * a, 2 * b)) for a, b in plan]
        diff, emis, face = setup(tied(mode_rows, chip))
        fetched, diff = lax.optimization_barrier((fetched, diff))
        mine_rows = jnp.concatenate(fetched, 0)
        gathered = (chip, mine_rows, swap(mine_rows, n, (1, 1)))
        tend, rate, top, coef = call(
            functools.partial(first_kernel, columns, plan), 3,
            [tend_out, rate_out, top_out, coef_out], [field_tmp],
            *chem, diff, emis, *gathered,
        )
    else:
        coef = lax.all_to_all(jnp.tile(coeffs, (n, 1)), "col", 0, 0, tiled=True)
        diff, emis, face = setup(mode_rows)
        tend, rate, top = call(
            functools.partial(first_kernel, columns, ()), 3,
            [tend_out, rate_out, top_out], [field_tmp],
            *chem, diff, emis, coef,
        )

    def summed(rate, top, coef, tend):
        def start(state, ready):
            return call(
                functools.partial(inverse_start, ridge, 3), 0,
                [square_bf, square_bf, square, top_out], [], tied(coef, ready),
            )

        def end(state, ready):
            high, low, inv, gap = tied(state, ready)
            return call(
                inverse_end, 0, [rate_out, rows_f32], [square], gap, high, low, inv, coef, tend
            )

        return sum_over(rate, top, n, (start, end))

    for _ in range(NSUB - 1):
        total, (solved, pull) = summed(rate, top, coef, tend)
        diff, tend, rate, top, coef = call(
            functools.partial(middle_kernel, columns, total_rows), 3,
            [rows_f32, tend_out, rate_out, top_out, coef_out], [field_tmp],
            *chem, diff, pull, solved, total, coef, face, emis,
        )
    total, (solved, pull) = summed(rate, top, coef, tend)
    return tuple(
        call(
            functools.partial(last_kernel, total_rows), 0,
            [rows_f32, ((mine, R), BF16)], [],
            diff, pull, solved, total, coef,
        )
    )


def solution(mesh):
    placed = (
        P(("grp", "col"), None),
        P(("grp", "col"), None),
        P(("grp", "col"), None),
        P(("grp", "col")),
        P("grp"),
        P(),
        P(),
        P(),
        P(),
        P(),
    )
    return jax.shard_map(
        on_device,
        mesh=mesh,
        in_specs=placed,
        out_specs=(P(("grp", "col"), None), P(("grp", "col"), None)),
        check_vma=False,
    )
```

time: 65.8 us -> 57.1 us (0.87)
  waiting for transfers between devices: 25.4 us -> 10.2 us
  starting transfers between devices: 10.3 us -> 21.9 us
  Pallas kernels: 24.2 us -> 19.3 us
    ppermute x10 -> x18, starting transfers between devices: 2.9 us -> 21.9 us  [swap(): lax.ppermute(value, 'col', [(i, i ^ masks[i % 2]) for i in range(n) if ma...]
    ppermute x10 -> x18, waiting for transfers between devices: 20.8 us -> 10.2 us  [swap(): lax.ppermute(value, 'col', [(i, i ^ masks[i % 2]) for i in range(n) if ma...]
    all_to_all x1 -> x0, starting transfers between devices: 7.39 us -> none  [on_device(): coef = lax.all_to_all(jnp.tile(coeffs, (n, 1)), 'col', 0, 0, tiled=True)]
    pallas_call x10 -> x8, Pallas kernels: 24.2 us -> 19.3 us  [call(): pl.pallas_call(kernel, in_specs=scalars(n_scalar) + whole(len(args) - n_s...]
    all_to_all x1 -> x0, waiting for transfers between devices: 4.59 us -> none  [on_device(): coef = lax.all_to_all(jnp.tile(coeffs, (n, 1)), 'col', 0, 0, tiled=True)]
    another operation x1 -> x0, local copies, waits for them, and re-layouts: 1.36 us -> none  [on_device(): coef = lax.all_to_all(jnp.tile(coeffs, (n, 1)), 'col', 0, 0, tiled=True)]
    unnamed x16 -> x21, local copies, waits for them, and re-layouts: 2.4 us -> 3.09 us
  transfers between devices with their start and end apart: 11 -> 18, of which waited for: 11 -> 11; matrix products, arithmetic and copies ran while one was open for 0% -> 0% of each run, Pallas kernels for 27% -> 23%
where the time goes in v3:
time: 57.1 us; the launch traced here: 56.9 us
  starting transfers between devices  21.9 us (38%)
  Pallas kernels  19.3 us (34%)
  waiting for transfers between devices  10.2 us (18%)
  local copies, waits for them, and re-layouts  3.24 us (6%)
  between operations  1.62 us (3%)
  other arithmetic  0.66 us (1%)
    ppermute x18, starting transfers between devices, swap(): lax.ppermute(value, 'col', [(i, i ^ masks[i % 2]) for i in range(n) if ma...  21.9 us
    pallas_call x8, Pallas kernels, call(): pl.pallas_call(kernel, in_specs=scalars(n_scalar) + whole(len(args) - n_s...  19.3 us
    ppermute x18, waiting for transfers between devices, swap(): lax.ppermute(value, 'col', [(i, i ^ masks[i % 2]) for i in range(n) if ma...  10.2 us
    unnamed x21, local copies, waits for them, and re-layouts  3.09 us
  transfers between devices with their start and end apart: 18, of which 11 were waited for; matrix products, arithmetic and copies ran while one was open for 0% of the time, Pallas kernels for 23%

profile of v3, /device:TPU:0, one launch (start us, length us, event | category | flops | bytes accessed | tf_op | source)
XLA Modules:
  0.0 56.9 jit_solution(12747094117891040125)
XLA Ops:
  0.6 0.0 copy-start.5
  0.6 0.5 collective-permute-start
  1.2 0.0 copy-start.6
  1.2 1.0 %collective-permute-done = bf16[16,256]{1,0:T(8,128)(2,1)S(1)} collective-permute-done((bf16[16,256]{1,0:T(8,128)(2,1)}, bf16[16,256]{1,0:T(8,128)(2,1)S(1)}, u32[]{:S(2)}, u32[]{:S(2)}) %collective-permute-start) | collective-permute-done | bytes 8224 | tf_op jit(solution)/shard_map/ppermute | solution.py:267
  2.2 0.0 copy-done.5
  2.2 0.7 %collective-permute-start.4 = (bf16[32,256]{1,0:T(8,128)(2,1)S(1)}, bf16[32,256]{1,0:T(8,128)(2,1)S(1)}, u32[]{:S(2)}, u32[]{:S(2)}) collective-permute-start(bf16[32,256]{1,0:T(8,128)(2,1)S(1)} %maximum_select_fusion.2.refs_0_), channel_id=1, source_target_pairs={{1,15},{3,13},{5,11},{7,9},{9,7},{11,5},{13,3},{15,1},{17,31},{19,... | collective-permute-start | bytes 49160 | tf_op jit(solution)/shard_map/ppermute | solution.py:267
  2.9 3.9 %collective-permute-start.3 = (bf16[32,256]{1,0:T(8,128)(2,1)S(1)}, bf16[32,256]{1,0:T(8,128)(2,1)S(1)}, u32[]{:S(2)}, u32[]{:S(2)}) collective-permute-start(bf16[32,256]{1,0:T(8,128)(2,1)S(1)} %maximum_select_fusion.2.refs_0_), channel_id=1, source_target_pairs={{0,6},{1,13},{2,4},{3,15},{4,2},{5,9},{6,0},{7,11},{8,14},{9,5},{1... | collective-permute-start | bytes 49160 | tf_op jit(solution)/shard_map/ppermute | solution.py:267
  6.8 0.4 collective-permute-start.2
  7.3 0.2 collective-permute-start.1
  7.5 0.0 copy-done.6
  7.5 0.0 copy-done.7
  8.1 0.0 copy-start.8
  8.1 0.6 %copy-done.8 = f32[8]{0:T(128)S(1)} copy-done((f32[8]{0:T(128)S(1)}, f32[8]{0:T(128)}, u32[]{:S(2)}) %copy-start.8) | copy-done | bytes 56
  8.8 0.1 copy.12
  8.9 0.0 copy-start.2
  8.9 0.0 copy-start.3
  8.9 0.0 copy-start.4
  8.9 0.7 %copy-done.2 = f32[16,8]{0,1:T(8,128)S(1)} copy-done((f32[16,8]{0,1:T(8,128)S(1)}, f32[16,8]{0,1:T(8,128)}, u32[]{:S(2)}) %copy-start.2) | copy-done | bytes 536
  9.5 0.0 copy-done.3
  9.6 0.0 copy-done.4
  9.6 0.0 copy-start
  9.6 1.0 %copy-done = f32[512,256]{1,0:T(8,128)S(1)} copy-done((f32[512,256]{1,0:T(8,128)S(1)}, f32[512,256]{1,0:T(8,128)}, u32[]{:S(2)}) %copy-start) | copy-done | bytes 524312
  10.6 0.9 %shard_map.113 = (f32[512,256]{1,0:T(8,128)S(1)}, f32[8,256]{1,0:T(8,128)S(1)}, f32[64,256]{1,0:T(8,128)S(1)}) custom-call(s32[1]{0:T(128)S(6)} %copy.16.counts_ref, f32[8,16]{1,0:T(8,128)S(1)} %bitcast.24, f32[512,256]{1,0:T(8,128)S(1)} %copy-done, f32[1,64]{1,0:T(1,128)S(1)} %copy-done.4, s32[1,256]{1,0:T(1,128)S(1)} %bitcast.25), custom_call_target="tpu_custom_call" | custom-call | tf_op jit(solution)/shard_map/pallas_call | solution.py:252
  11.5 0.0 collective-permute-done.4
  11.5 0.0 collective-permute-done.3
  11.6 0.0 collective-permute-done.2
  11.6 0.0 collective-permute-done.1
  11.6 5.0 %collective-permute-start.5 = (bf16[128,256]{1,0:T(8,128)(2,1)S(1)}, bf16[128,256]{1,0:T(8,128)(2,1)S(1)}, u32[]{:S(2)}, u32[]{:S(2)}) collective-permute-start(bf16[128,256]{1,0:T(8,128)(2,1)S(1)} %constant_dynamic-update-slice_fusion.refs_1_), channel_id=1, source_target_pairs={{0,1},{1,0},{2,3},{3,2},{4,5},{5,4},{6,7},{7,6},{8,9},{9,8},{10,11... | collective-permute-start | bytes 196616 | tf_op jit(solution)/shard_map/ppermute | solution.py:267
  16.6 0.1 pad_maximum_fusion.6.weight_ref
  16.7 0.8 %collective-permute-done.5.refs_2_ = bf16[128,256]{1,0:T(8,128)(2,1)S(1)} collective-permute-done((bf16[128,256]{1,0:T(8,128)(2,1)S(1)}, bf16[128,256]{1,0:T(8,128)(2,1)S(1)}, u32[]{:S(2)}, u32[]{:S(2)}) %collective-permute-start.5) | collective-permute-done | bytes 65568 | tf_op jit(solution)/shard_map/ppermute | solution.py:267
  17.5 0.7 %copy-done.1 = s32[12,2]{0,1:T(2,128)S(1)} copy-done((s32[12,2]{0,1:T(2,128)S(1)}, s32[12,2]{0,1:T(2,128)}, u32[]{:S(2)}) %copy-start.1) | copy-done | bytes 120
  18.2 2.0 %shard_map.114 = (bf16[512,256]{1,0:T(8,128)(2,1)S(1)}, f32[256,256]{1,0:T(8,128)S(1)}, f32[8,256]{1,0:T(8,128)S(1)}, bf16[256,256]{1,0:T(8,128)(2,1)S(1)}) custom-call(s32[1]{0:T(128)S(6)} %copy.16.counts_ref, s32[2,12]{1,0:T(2,128)S(1)} %bitcast.22, f32[8,13]{1,0:T(8,128)S(1)} %pad_maximum_fusion.6.weight_ref, ...), custom_call_target="tpu_custom_call" | custom-call | tf_op jit(solution)/shard_map/pallas_call | solution.py:252
  20.2 0.4 collective-permute-start.6
  20.6 1.0 %collective-permute-done.6 = f32[136,256]{1,0:T(8,128)S(1)} collective-permute-done((f32[136,256]{1,0:T(8,128)S(1)}, f32[136,256]{1,0:T(8,128)S(1)}, u32[]{:S(2)}, u32[]{:S(2)}) %collective-permute-start.6) | collective-permute-done | bytes 139296 | tf_op jit(solution)/shard_map/ppermute | solution.py:267
  21.7 2.4 %collective-permute-start.9 = (f16[136,256]{1,0:T(8,128)(2,1)S(1)}, f16[136,256]{1,0:T(8,128)(2,1)S(1)}, u32[]{:S(2)}, u32[]{:S(2)}) collective-permute-start(f16[136,256]{1,0:T(8,128)(2,1)S(1)} %pad_maximum_fusion.2), channel_id=1, source_target_pairs={{0,6},{1,7},{2,4},{3,5},{4,2},{5,3},{6,0},{7,1},{8,14},{9,15},{10,... | collective-permute-start | bytes 208904 | tf_op jit(solution)/shard_map/ppermute | solution.py:267
  24.1 0.6 %collective-permute-start.8 = (f16[136,256]{1,0:T(8,128)(2,1)S(1)}, f16[136,256]{1,0:T(8,128)(2,1)S(1)}, u32[]{:S(2)}, u32[]{:S(2)}) collective-permute-start(f16[136,256]{1,0:T(8,128)(2,1)S(1)} %pad_maximum_fusion.2), channel_id=1, source_target_pairs={{0,4},{1,5},{2,6},{3,7},{4,0},{5,1},{6,2},{7,3},{8,12},{9,13},{10,... | collective-permute-start | bytes 208904 | tf_op jit(solution)/shard_map/ppermute | solution.py:267
  24.8 0.5 collective-permute-start.7
  25.3 2.5 %shard_map.115 = (bf16[256,256]{1,0:T(8,128)(2,1)S(1)}, bf16[256,256]{1,0:T(8,128)(2,1)S(1)}, f32[256,256]{1,0:T(8,128)S(1)}, f32[8,256]{1,0:T(8,128)S(1)}) custom-call(bf16[256,256]{1,0:T(8,128)(2,1)S(1)} %get-tuple-element.73.coef_ref), custom_call_target="tpu_custom_call" | custom-call | tf_op jit(solution)/shard_map/pallas_call | solution.py:252
  27.8 0.0 collective-permute-done.9
  27.8 0.9 %collective-permute-done.8 = f16[136,256]{1,0:T(8,128)(2,1)S(1)} collective-permute-done((f16[136,256]{1,0:T(8,128)(2,1)S(1)}, f16[136,256]{1,0:T(8,128)(2,1)S(1)}, u32[]{:S(2)}, u32[]{:S(2)}) %collective-permute-start.8) | collective-permute-done | bytes 69664 | tf_op jit(solution)/shard_map/ppermute | solution.py:267
  28.7 0.4 collective-permute-done.7
  29.1 0.1 multiply_convert_fusion.1
  29.2 2.1 %collective-permute-start.10 = (f16[136,256]{1,0:T(8,128)(2,1)S(1)}, f16[136,256]{1,0:T(8,128)(2,1)S(1)}, u32[]{:S(2)}, u32[]{:S(2)}) collective-permute-start(f16[136,256]{1,0:T(8,128)(2,1)S(1)} %pad_maximum_fusion.3), channel_id=1, source_target_pairs={{0,8},{1,9},{2,10},{3,11},{4,12},{5,13},{6,14},{7,15},{8,0},{9,1},... | collective-permute-start | bytes 208904 | tf_op jit(solution)/shard_map/ppermute | solution.py:267
  31.3 3.5 %shard_map.116 = (f32[256,256]{1,0:T(8,128)S(1)}, f32[512,256]{1,0:T(8,128)S(1)}) custom-call(f32[8,256]{1,0:T(8,128)S(1)} %get-tuple-element.85.gap_in_ref, bf16[256,256]{1,0:T(8,128)(2,1)S(1)} %get-tuple-element.86.high_ref, bf16[256,256]{1,0:T(8,128)(2,1)S(1)} %get-tuple-element.87.low_ref, f32[256,256]{1,0:T(8,128)S(1)} %get-tuple-element.88.inv_in_ref, ...), custom_call_target="tpu_custom_call" | custom-call | tf_op jit(solution)/shard_map/pallas_call | solution.py:252
  34.8 0.0 collective-permute-done.10
  34.9 0.1 collective-permute-start.11
  34.9 1.3 %collective-permute-done.11 = f32[128,256]{1,0:T(8,128)S(1)} collective-permute-done((f32[128,256]{1,0:T(8,128)S(1)}, f32[128,256]{1,0:T(8,128)S(1)}, u32[]{:S(2)}, u32[]{:S(2)}) %collective-permute-start.11) | collective-permute-done | bytes 131104 | tf_op jit(solution)/shard_map/ppermute | solution.py:267
  36.3 2.8 %shard_map.117 = (f32[512,256]{1,0:T(8,128)S(1)}, bf16[512,256]{1,0:T(8,128)(2,1)S(1)}, f32[256,256]{1,0:T(8,128)S(1)}, f32[8,256]{1,0:T(8,128)S(1)}, bf16[256,256]{1,0:T(8,128)(2,1)S(1)}) custom-call(s32[1]{0:T(128)S(6)} %copy.16.counts_ref, s32[2,12]{1,0:T(2,128)S(1)} %bitcast.23, f32[8,13]{1,0:T(8,128)S(1)} %pad_maximum_fusion.6.weight_ref, ...), custom_call_target="tpu_custom_call" | custom-call | tf_op jit(solution)/shard_map/pallas_call | solution.py:252
  39.2 0.2 collective-permute-start.12
  39.4 1.2 %collective-permute-done.12 = f32[136,256]{1,0:T(8,128)S(1)} collective-permute-done((f32[136,256]{1,0:T(8,128)S(1)}, f32[136,256]{1,0:T(8,128)S(1)}, u32[]{:S(2)}, u32[]{:S(2)}) %collective-permute-start.12) | collective-permute-done | bytes 139296 | tf_op jit(solution)/shard_map/ppermute | solution.py:267
  40.7 2.6 %collective-permute-start.15 = (f16[136,256]{1,0:T(8,128)(2,1)S(1)}, f16[136,256]{1,0:T(8,128)(2,1)S(1)}, u32[]{:S(2)}, u32[]{:S(2)}) collective-permute-start(f16[136,256]{1,0:T(8,128)(2,1)S(1)} %pad_maximum_fusion.4), channel_id=1, source_target_pairs={{0,6},{1,7},{2,4},{3,5},{4,2},{5,3},{6,0},{7,1},{8,14},{9,15},{10,... | collective-permute-start | bytes 208904 | tf_op jit(solution)/shard_map/ppermute | solution.py:267
  43.3 0.8 %collective-permute-start.14 = (f16[136,256]{1,0:T(8,128)(2,1)S(1)}, f16[136,256]{1,0:T(8,128)(2,1)S(1)}, u32[]{:S(2)}, u32[]{:S(2)}) collective-permute-start(f16[136,256]{1,0:T(8,128)(2,1)S(1)} %pad_maximum_fusion.4), channel_id=1, source_target_pairs={{0,4},{1,5},{2,6},{3,7},{4,0},{5,1},{6,2},{7,3},{8,12},{9,13},{10,... | collective-permute-start | bytes 208904 | tf_op jit(solution)/shard_map/ppermute | solution.py:267
  44.0 0.2 collective-permute-start.13
  44.2 2.5 %shard_map.118 = (bf16[256,256]{1,0:T(8,128)(2,1)S(1)}, bf16[256,256]{1,0:T(8,128)(2,1)S(1)}, f32[256,256]{1,0:T(8,128)S(1)}, f32[8,256]{1,0:T(8,128)S(1)}) custom-call(bf16[256,256]{1,0:T(8,128)(2,1)S(1)} %get-tuple-element.100.coef_ref), custom_call_target="tpu_custom_call" | custom-call | tf_op jit(solution)/shard_map/pallas_call | solution.py:252
  46.8 0.0 collective-permute-done.15
  46.8 1.0 %collective-permute-done.14 = f16[136,256]{1,0:T(8,128)(2,1)S(1)} collective-permute-done((f16[136,256]{1,0:T(8,128)(2,1)S(1)}, f16[136,256]{1,0:T(8,128)(2,1)S(1)}, u32[]{:S(2)}, u32[]{:S(2)}) %collective-permute-start.14) | collective-permute-done | bytes 69664 | tf_op jit(solution)/shard_map/ppermute | solution.py:267
  47.8 0.5 collective-permute-done.13
  48.4 0.1 multiply_convert_fusion
  48.5 1.2 %collective-permute-start.16 = (f16[136,256]{1,0:T(8,128)(2,1)S(1)}, f16[136,256]{1,0:T(8,128)(2,1)S(1)}, u32[]{:S(2)}, u32[]{:S(2)}) collective-permute-start(f16[136,256]{1,0:T(8,128)(2,1)S(1)} %pad_maximum_fusion.5), channel_id=1, source_target_pairs={{0,8},{1,9},{2,10},{3,11},{4,12},{5,13},{6,14},{7,15},{8,0},{9,1},... | collective-permute-start | bytes 208904 | tf_op jit(solution)/shard_map/ppermute | solution.py:267
  49.7 3.5 %shard_map.119 = (f32[256,256]{1,0:T(8,128)S(1)}, f32[512,256]{1,0:T(8,128)S(1)}) custom-call(f32[8,256]{1,0:T(8,128)S(1)} %get-tuple-element.112.gap_in_ref, bf16[256,256]{1,0:T(8,128)(2,1)S(1)} %get-tuple-element.113.high_ref, bf16[256,256]{1,0:T(8,128)(2,1)S(1)} %get-tuple-element.114.low_ref, f32[256,256]{1,0:T(8,128)S(1)} %get-tuple-element.115.inv_in_ref, ...), custom_call_target="tpu_custom_call" | custom-call | tf_op jit(solution)/shard_map/pallas_call | solution.py:252
  53.2 0.5 collective-permute-done.16
  53.8 0.1 collective-permute-start.17
  53.9 1.3 %collective-permute-done.17 = f32[128,256]{1,0:T(8,128)S(1)} collective-permute-done((f32[128,256]{1,0:T(8,128)S(1)}, f32[128,256]{1,0:T(8,128)S(1)}, u32[]{:S(2)}, u32[]{:S(2)}) %collective-permute-start.17) | collective-permute-done | bytes 131104 | tf_op jit(solution)/shard_map/ppermute | solution.py:267
  55.3 1.6 %shard_map.120 = (f32[512,256]{1,0:T(8,128)}, bf16[16,256]{1,0:T(8,128)(2,1)}) custom-call(f32[512,256]{1,0:T(8,128)S(1)} %get-tuple-element.96.diff_in_ref, f32[512,256]{1,0:T(8,128)S(1)} %get-tuple-element.119.pull_ref, f32[256,256]{1,0:T(8,128)S(1)} %get-tuple-element.120.solve_ref, f32[256,256]{1,0:T(8,128)S(1)} %maximum_select_fusion.1.sum_ref, ...), custom_call_target="tpu_custom_call" | custom-call | tf_op jit(solution)/shard_map/pallas_call | solution.py:252
  (38 shorter events, 0.5 us)
Async XLA Ops:
  0.6 1.6 %copy-start.5 = (bf16[16,256]{1,0:T(8,128)(2,1)S(1)}, bf16[16,256]{1,0:T(8,128)(2,1)}, u32[]{:S(2)}) copy-start(bf16[16,256]{1,0:T(8,128)(2,1)} %param.11) | copy-start | bytes 24580
  0.6 1.6 %collective-permute-start = (bf16[16,256]{1,0:T(8,128)(2,1)}, bf16[16,256]{1,0:T(8,128)(2,1)S(1)}, u32[]{:S(2)}, u32[]{:S(2)}) collective-permute-start(bf16[16,256]{1,0:T(8,128)(2,1)} %param.11), channel_id=1, source_target_pairs={{0,1},{1,0},{2,3},{3,2},{4,5},{5,4},{6,7},{7,6},{8,9},{9,8},{10,11... | collective-permute-start | bytes 24584 | tf_op jit(solution)/shard_map/ppermute | solution.py:267
  1.2 6.3 %copy-start.6 = (s32[12,8]{0,1:T(8,128)S(1)}, s32[12,8]{0,1:T(8,128)}, u32[]{:S(2)}) copy-start(s32[12,8]{0,1:T(8,128)} %param.17) | copy-start | bytes 1156
  1.2 6.3 %copy-start.7 = (f32[12]{0:T(128)S(1)}, f32[12]{0:T(128)}, u32[]{:S(2)}) copy-start(f32[12]{0:T(128)} %param.18) | copy-start | bytes 148
  2.2 9.3 %collective-permute-start.4 = (bf16[32,256]{1,0:T(8,128)(2,1)S(1)}, bf16[32,256]{1,0:T(8,128)(2,1)S(1)}, u32[]{:S(2)}, u32[]{:S(2)}) collective-permute-start(bf16[32,256]{1,0:T(8,128)(2,1)S(1)} %maximum_select_fusion.2.refs_0_), channel_id=1, source_target_pairs={{1,15},{3,13},{5,11},{7,9},{9,7},{11,5},{13,3},{15,1},{17,31},{19,... | collective-permute-start | bytes 49160 | tf_op jit(solution)/shard_map/ppermute | solution.py:267
  2.9 8.7 %collective-permute-start.3 = (bf16[32,256]{1,0:T(8,128)(2,1)S(1)}, bf16[32,256]{1,0:T(8,128)(2,1)S(1)}, u32[]{:S(2)}, u32[]{:S(2)}) collective-permute-start(bf16[32,256]{1,0:T(8,128)(2,1)S(1)} %maximum_select_fusion.2.refs_0_), channel_id=1, source_target_pairs={{0,6},{1,13},{2,4},{3,15},{4,2},{5,9},{6,0},{7,11},{8,14},{9,5},{1... | collective-permute-start | bytes 49160 | tf_op jit(solution)/shard_map/ppermute | solution.py:267
  6.8 4.7 %collective-permute-start.2 = (bf16[32,256]{1,0:T(8,128)(2,1)S(1)}, bf16[32,256]{1,0:T(8,128)(2,1)S(1)}, u32[]{:S(2)}, u32[]{:S(2)}) collective-permute-start(bf16[32,256]{1,0:T(8,128)(2,1)S(1)} %maximum_select_fusion.2.refs_0_), channel_id=1, source_target_pairs={{0,4},{1,11},{2,6},{3,9},{4,0},{5,15},{6,2},{7,13},{8,12},{9,3},{1... | collective-permute-start | bytes 49160 | tf_op jit(solution)/shard_map/ppermute | solution.py:267
  7.3 4.3 %collective-permute-start.1 = (bf16[32,256]{1,0:T(8,128)(2,1)S(1)}, bf16[32,256]{1,0:T(8,128)(2,1)S(1)}, u32[]{:S(2)}, u32[]{:S(2)}) collective-permute-start(bf16[32,256]{1,0:T(8,128)(2,1)S(1)} %maximum_select_fusion.2.refs_0_), channel_id=1, source_target_pairs={{0,2},{1,9},{2,0},{3,11},{4,6},{5,13},{6,4},{7,15},{8,10},{9,1},{1... | collective-permute-start | bytes 49160 | tf_op jit(solution)/shard_map/ppermute | solution.py:267
  8.1 0.7 %copy-start.8 = (f32[8]{0:T(128)S(1)}, f32[8]{0:T(128)}, u32[]{:S(2)}) copy-start(f32[8]{0:T(128)} %param.19) | copy-start | bytes 100
  8.9 0.7 %copy-start.2 = (f32[16,8]{0,1:T(8,128)S(1)}, f32[16,8]{0,1:T(8,128)}, u32[]{:S(2)}) copy-start(f32[16,8]{0,1:T(8,128)} %param.15) | copy-start | bytes 1540
  8.9 0.7 %copy-start.3 = (s32[256]{0:T(256)S(1)}, s32[256]{0:T(256)}, u32[]{:S(2)}) copy-start(s32[256]{0:T(256)} %param.14) | copy-start | bytes 3076
  8.9 0.7 %copy-start.4 = (f32[1,64]{1,0:T(1,128)S(1)}, f32[1,64]{1,0:T(1,128)}, u32[]{:S(2)}) copy-start(f32[1,64]{1,0:T(1,128)} %level_face_ref.1) | copy-start | bytes 772
  9.6 1.0 %copy-start = (f32[512,256]{1,0:T(8,128)S(1)}, f32[512,256]{1,0:T(8,128)}, u32[]{:S(2)}) copy-start(f32[512,256]{1,0:T(8,128)} %modes_ref) | copy-start | bytes 1572868
  11.6 5.9 %collective-permute-start.5 = (bf16[128,256]{1,0:T(8,128)(2,1)S(1)}, bf16[128,256]{1,0:T(8,128)(2,1)S(1)}, u32[]{:S(2)}, u32[]{:S(2)}) collective-permute-start(bf16[128,256]{1,0:T(8,128)(2,1)S(1)} %constant_dynamic-update-slice_fusion.refs_1_), channel_id=1, source_target_pairs={{0,1},{1,0},{2,3},{3,2},{4,5},{5,4},{6,7},{7,6},{8,9},{9,8},{10,11... | collective-permute-start | bytes 196616 | tf_op jit(solution)/shard_map/ppermute | solution.py:267
  17.5 0.7 %copy-start.1 = (s32[12,2]{0,1:T(2,128)S(1)}, s32[12,2]{0,1:T(2,128)}, u32[]{:S(2)}) copy-start(s32[12,2]{0,1:T(2,128)} %param.16) | copy-start | bytes 292
  20.2 1.4 %collective-permute-start.6 = (f32[136,256]{1,0:T(8,128)S(1)}, f32[136,256]{1,0:T(8,128)S(1)}, u32[]{:S(2)}, u32[]{:S(2)}) collective-permute-start(f32[136,256]{1,0:T(8,128)S(1)} %pad_maximum_fusion), channel_id=1, source_target_pairs={{0,1},{1,0},{2,3},{3,2},{4,5},{5,4},{6,7},{7,6},{8,9},{9,8},{10,11... | collective-permute-start | bytes 417800 | tf_op jit(solution)/shard_map/ppermute | solution.py:267
  21.7 6.1 %collective-permute-start.9 = (f16[136,256]{1,0:T(8,128)(2,1)S(1)}, f16[136,256]{1,0:T(8,128)(2,1)S(1)}, u32[]{:S(2)}, u32[]{:S(2)}) collective-permute-start(f16[136,256]{1,0:T(8,128)(2,1)S(1)} %pad_maximum_fusion.2), channel_id=1, source_target_pairs={{0,6},{1,7},{2,4},{3,5},{4,2},{5,3},{6,0},{7,1},{8,14},{9,15},{10,... | collective-permute-start | bytes 208904 | tf_op jit(solution)/shard_map/ppermute | solution.py:267
  24.1 4.5 %collective-permute-start.8 = (f16[136,256]{1,0:T(8,128)(2,1)S(1)}, f16[136,256]{1,0:T(8,128)(2,1)S(1)}, u32[]{:S(2)}, u32[]{:S(2)}) collective-permute-start(f16[136,256]{1,0:T(8,128)(2,1)S(1)} %pad_maximum_fusion.2), channel_id=1, source_target_pairs={{0,4},{1,5},{2,6},{3,7},{4,0},{5,1},{6,2},{7,3},{8,12},{9,13},{10,... | collective-permute-start | bytes 208904 | tf_op jit(solution)/shard_map/ppermute | solution.py:267
  24.8 4.3 %collective-permute-start.7 = (f16[136,256]{1,0:T(8,128)(2,1)S(1)}, f16[136,256]{1,0:T(8,128)(2,1)S(1)}, u32[]{:S(2)}, u32[]{:S(2)}) collective-permute-start(f16[136,256]{1,0:T(8,128)(2,1)S(1)} %pad_maximum_fusion.2), channel_id=1, source_target_pairs={{0,2},{1,3},{2,0},{3,1},{4,6},{5,7},{6,4},{7,5},{8,10},{9,11},{10,... | collective-permute-start | bytes 208904 | tf_op jit(solution)/shard_map/ppermute | solution.py:267
  29.2 5.6 %collective-permute-start.10 = (f16[136,256]{1,0:T(8,128)(2,1)S(1)}, f16[136,256]{1,0:T(8,128)(2,1)S(1)}, u32[]{:S(2)}, u32[]{:S(2)}) collective-permute-start(f16[136,256]{1,0:T(8,128)(2,1)S(1)} %pad_maximum_fusion.3), channel_id=1, source_target_pairs={{0,8},{1,9},{2,10},{3,11},{4,12},{5,13},{6,14},{7,15},{8,0},{9,1},... | collective-permute-start | bytes 208904 | tf_op jit(solution)/shard_map/ppermute | solution.py:267
  34.9 1.4 %collective-permute-start.11 = (f32[128,256]{1,0:T(8,128)S(1)}, f32[128,256]{1,0:T(8,128)S(1)}, u32[]{:S(2)}, u32[]{:S(2)}) collective-permute-start(f32[128,256]{1,0:T(8,128)S(1)} %multiply_add_fusion.1), channel_id=1, source_target_pairs={{0,1},{1,0},{2,3},{3,2},{4,5},{5,4},{6,7},{7,6},{8,9},{9,8},{10,11... | collective-permute-start | bytes 393224 | tf_op jit(solution)/shard_map/ppermute | solution.py:267
  39.2 1.4 %collective-permute-start.12 = (f32[136,256]{1,0:T(8,128)S(1)}, f32[136,256]{1,0:T(8,128)S(1)}, u32[]{:S(2)}, u32[]{:S(2)}) collective-permute-start(f32[136,256]{1,0:T(8,128)S(1)} %pad_maximum_fusion.1), channel_id=1, source_target_pairs={{0,1},{1,0},{2,3},{3,2},{4,5},{5,4},{6,7},{7,6},{8,9},{9,8},{10,11... | collective-permute-start | bytes 417800 | tf_op jit(solution)/shard_map/ppermute | solution.py:267
  40.7 6.1 %collective-permute-start.15 = (f16[136,256]{1,0:T(8,128)(2,1)S(1)}, f16[136,256]{1,0:T(8,128)(2,1)S(1)}, u32[]{:S(2)}, u32[]{:S(2)}) collective-permute-start(f16[136,256]{1,0:T(8,128)(2,1)S(1)} %pad_maximum_fusion.4), channel_id=1, source_target_pairs={{0,6},{1,7},{2,4},{3,5},{4,2},{5,3},{6,0},{7,1},{8,14},{9,15},{10,... | collective-permute-start | bytes 208904 | tf_op jit(solution)/shard_map/ppermute | solution.py:267
  43.3 4.5 %collective-permute-start.14 = (f16[136,256]{1,0:T(8,128)(2,1)S(1)}, f16[136,256]{1,0:T(8,128)(2,1)S(1)}, u32[]{:S(2)}, u32[]{:S(2)}) collective-permute-start(f16[136,256]{1,0:T(8,128)(2,1)S(1)} %pad_maximum_fusion.4), channel_id=1, source_target_pairs={{0,4},{1,5},{2,6},{3,7},{4,0},{5,1},{6,2},{7,3},{8,12},{9,13},{10,... | collective-permute-start | bytes 208904 | tf_op jit(solution)/shard_map/ppermute | solution.py:267
  44.0 4.3 %collective-permute-start.13 = (f16[136,256]{1,0:T(8,128)(2,1)S(1)}, f16[136,256]{1,0:T(8,128)(2,1)S(1)}, u32[]{:S(2)}, u32[]{:S(2)}) collective-permute-start(f16[136,256]{1,0:T(8,128)(2,1)S(1)} %pad_maximum_fusion.4), channel_id=1, source_target_pairs={{0,2},{1,3},{2,0},{3,1},{4,6},{5,7},{6,4},{7,5},{8,10},{9,11},{10,... | collective-permute-start | bytes 208904 | tf_op jit(solution)/shard_map/ppermute | solution.py:267
  48.5 5.3 %collective-permute-start.16 = (f16[136,256]{1,0:T(8,128)(2,1)S(1)}, f16[136,256]{1,0:T(8,128)(2,1)S(1)}, u32[]{:S(2)}, u32[]{:S(2)}) collective-permute-start(f16[136,256]{1,0:T(8,128)(2,1)S(1)} %pad_maximum_fusion.5), channel_id=1, source_target_pairs={{0,8},{1,9},{2,10},{3,11},{4,12},{5,13},{6,14},{7,15},{8,0},{9,1},... | collective-permute-start | bytes 208904 | tf_op jit(solution)/shard_map/ppermute | solution.py:267
  53.8 1.4 %collective-permute-start.17 = (f32[128,256]{1,0:T(8,128)S(1)}, f32[128,256]{1,0:T(8,128)S(1)}, u32[]{:S(2)}, u32[]{:S(2)}) collective-permute-start(f32[128,256]{1,0:T(8,128)S(1)} %multiply_add_fusion), channel_id=1, source_target_pairs={{0,1},{1,0},{2,3},{3,2},{4,5},{5,4},{6,7},{7,6},{8,9},{9,8},{10,11... | collective-permute-start | bytes 393224 | tf_op jit(solution)/shard_map/ppermute | solution.py:267

commit v4 on v3

--- a/solution.py
+++ b/solution.py
@@ -50,8 +50,23 @@
     return modes + flux - pltpu.roll(flux, 1, 0)
 
 
+def fetch(sources, targets, sems):
+    copies = [
+        pltpu.make_async_copy(source, target, sems.at[i])
+        for i, (source, target) in enumerate(zip(sources, targets, strict=True))
+    ]
+    for copy in copies:
+        copy.start()
+
+    def wait():
+        for copy in copies:
+            copy.wait()
+
+    return wait
+
+
 def react(
-    diffused, coef_ref, emis_ref, counts_ref, pair_ref, weight_ref,
+    diffused, coef_ref, emis_ref, ready, counts_ref, pair_ref, stoich_ref, speed_ref, loss_ref,
     field_ref, tend_ref, rate_ref, top_ref, columns,
 ):
     mode_bf = diffused.astype(BF16)
@@ -63,6 +78,8 @@
     for b in range(members // block):
         lanes = slice(b * block, (b + 1) * block)
         field_ref[...] = mm(mode_bf, coef_ref[lanes, :], NT) * (1.0 / math.sqrt(R))
+        if b == 0:
+            ready()
 
         def part(i, _):
             c = i // steps
@@ -77,11 +94,11 @@
 
             total = []
             for s in range(S):
-                total.append(emis_ref[s : s + 1, lanes] * profile - weight_ref[s, NREAC] * amount(s))
+                total.append(emis_ref[s : s + 1, lanes] * profile - loss_ref[s] * amount(s))
             for r in range(NREAC):
-                speed = amount(pair_ref[0, r]) * amount(pair_ref[1, r])
+                speed = speed_ref[r] * amount(pair_ref[0, r]) * amount(pair_ref[1, r])
                 for s in range(S):
-                    total[s] = total[s] + weight_ref[s, r] * speed
+                    total[s] = total[s] + stoich_ref[s, r].astype(F32) * speed
             for s in range(S):
                 tend_ref[pl.ds(pl.multiple_of(base + s * LEV, step), step), lanes] = jnp.where(
                     live, total[s], 0.0
@@ -96,12 +113,19 @@
     top_ref[...] = jnp.broadcast_to(power, top_ref.shape)
 
 
-def setup_kernel(
+def stage_kernel(
     columns,
-    counts_ref, table_ref,
-    modes_ref, level_face_ref, idx_ref,
-    diff_ref, emis_ref, face_ref,
-):
+    counts_ref, table_hbm, level_face_hbm, idx_hbm, modes_hbm,
+    modes_ref, emis_ref, face_ref,
+    table_ref, level_face_ref, idx_ref, sems,
+):
+    modes_copy = pltpu.make_async_copy(modes_hbm, modes_ref, sems.at[3])
+    modes_copy.start()
+    fetch(
+        (table_hbm, level_face_hbm, idx_hbm),
+        (table_ref, level_face_ref, idx_ref),
+        sems,
+    )()
     index = idx_ref[...]
     for s in range(S):
         row = jnp.zeros(index.shape, F32)
@@ -114,16 +138,22 @@
         inner = (down == across) & (down + 1 < counts_ref[c])
         face = jnp.sum(jnp.where(inner, level_face_ref[c : c + 1, :], 0.0), axis=1, keepdims=True)
         face_ref[c * LEV : (c + 1) * LEV, :] = jnp.broadcast_to(face, (LEV, R))
+    modes_copy.wait()
+
+
+def diffuse_kernel(modes_ref, face_ref, diff_ref):
     diff_ref[...] = diffuse_rows(modes_ref[...], face_ref)
 
 
 def first_kernel(
     columns, plan,
-    counts_ref, pair_ref, weight_ref,
-    diff_ref, emis_ref, *refs,
-):
+    counts_ref, *allrefs,
+):
+    chem_hbm, chem, sems = allrefs[:4], allrefs[-5:-1], allrefs[-1]
+    diff_ref, emis_ref, *refs, field_ref = allrefs[4:-5]
+    ready = fetch(chem_hbm, chem, sems)
     if plan:
-        chip_ref, mine_ref, theirs_ref, tend_ref, rate_ref, top_ref, coef_ref, field_ref = refs
+        chip_ref, mine_ref, theirs_ref, tend_ref, rate_ref, top_ref, coef_ref = refs
         rows = chip_ref.shape[0]
         place = lax.axis_index("col")
         chip, side = place // 2, place % 2
@@ -136,35 +166,41 @@
                 coef_ref[pl.ds(spot, rows), :] = ref[j * rows : (j + 1) * rows, :]
         coef_ref[pl.ds(pl.multiple_of(chip * rows, rows), rows), :] = chip_ref[...]
     else:
-        coef_ref, tend_ref, rate_ref, top_ref, field_ref = refs
+        coef_ref, tend_ref, rate_ref, top_ref = refs
     react(
-        diff_ref[...], coef_ref, emis_ref, counts_ref, pair_ref, weight_ref,
+        diff_ref[...], coef_ref, emis_ref, ready, counts_ref, *chem,
         field_ref, tend_ref, rate_ref, top_ref, columns,
     )
 
 
-def advance(diffused, pull, solve_ref, rate):
-    transfer = mm3(split(rate), split(solve_ref[...]), TN)
-    moved = mm3(split(diffused), split(transfer))
+def transfer_of(solve_ref, rate):
+    return split(mm3(split(rate), split(solve_ref[...]), TN))
+
+
+def advance(diffused, pull, transfer):
+    moved = mm3(split(diffused), transfer)
     return diffused + (TIME_STEP * math.sqrt(R)) * (pull - moved)
 
 
 def middle_kernel(
     columns, total_rows,
-    counts_ref, pair_ref, weight_ref,
+    counts_ref, pair_hbm, stoich_hbm, speed_hbm, loss_hbm,
     diff_in_ref, pull_ref, solve_ref, sum_ref, coef_ref, face_ref, emis_ref,
     diff_ref, tend_ref, rate_ref, top_ref, coef_out_ref,
-    field_ref,
-):
+    field_ref, *chem_sems,
+):
+    *chem, sems = chem_sems
+    ready = fetch((pair_hbm, stoich_hbm, speed_hbm, loss_hbm), chem, sems)
     raw = sum_ref[...]
     coef_out_ref[...] = (
         coef_ref[...].astype(F32) + RATE_STEP * (raw * (math.sqrt(R) / total_rows))
     ).astype(BF16)
-    modes = advance(diff_in_ref[...], pull_ref[...], solve_ref, raw * (1.0 / total_rows))
+    transfer = transfer_of(solve_ref, raw * (1.0 / total_rows))
+    modes = advance(diff_in_ref[...], pull_ref[...], transfer)
     diffused = diffuse_rows(modes, face_ref)
     diff_ref[...] = diffused
     react(
-        diffused, coef_out_ref, emis_ref, counts_ref, pair_ref, weight_ref,
+        diffused, coef_out_ref, emis_ref, ready, counts_ref, *chem,
         field_ref, tend_ref, rate_ref, top_ref, columns,
     )
 
@@ -172,7 +208,8 @@
 def last_kernel(
     total_rows,
     diff_in_ref, pull_ref, solve_ref, sum_ref, coef_ref,
-    modes_ref, coef_out_ref,
+    modes_hbm, coef_out_ref,
+    modes_ref, sems,
 ):
     mine = coef_out_ref.shape[0]
     own = pl.ds(pl.multiple_of(lax.axis_index("col") * mine, mine), mine)
@@ -180,9 +217,23 @@
         coef_ref[own, :].astype(F32)
         + RATE_STEP * (sum_ref[own, :] * (math.sqrt(R) / total_rows))
     ).astype(BF16)
-    modes_ref[...] = advance(
-        diff_in_ref[...], pull_ref[...], solve_ref, sum_ref[...] * (1.0 / total_rows)
-    )
+    transfer = transfer_of(solve_ref, sum_ref[...] * (1.0 / total_rows))
+    parts = sems.shape[0]
+    rows = modes_ref.shape[0] // parts
+    copies = []
+    for i in range(parts):
+        block = slice(i * rows, (i + 1) * rows)
+        modes_ref[block, :] = advance(diff_in_ref[block, :], pull_ref[block, :], transfer)
+        copies.append(
+            pltpu.make_async_copy(
+                modes_ref.at[pl.ds(i * rows, rows), :],
+                modes_hbm.at[pl.ds(i * rows, rows), :],
+                sems.at[i],
+            )
+        )
+        copies[-1].start()
+    for copy in copies:
+        copy.wait()
 
 
 def identity():
@@ -240,21 +291,24 @@
 VMEM_LIMIT = 48 * 1024 * 1024
 
 
-def whole(n):
-    return [pl.BlockSpec(memory_space=pltpu.VMEM)] * n
-
-
-def scalars(n):
-    return [pl.BlockSpec(memory_space=pltpu.SMEM)] * n
-
-
-def call(kernel, n_scalar, outs, scratch, *args):
+def call(kernel, n_hbm, outs, scratch, *args, counts=None, hbm_outs=0):
+    def spaces(n, left):
+        return [pl.BlockSpec(memory_space=pltpu.HBM if i < left else pltpu.VMEM) for i in range(n)]
+
+    in_specs = spaces(len(args), n_hbm)
+    args = [
+        pltpu.with_memory_space_constraint(arg, pltpu.HBM) if i < n_hbm else arg
+        for i, arg in enumerate(args)
+    ]
+    if counts is not None:
+        in_specs = [pl.BlockSpec(memory_space=pltpu.SMEM)] + in_specs
+        args = [counts] + args
     return pl.pallas_call(
         kernel,
-        in_specs=scalars(n_scalar) + whole(len(args) - n_scalar),
-        out_specs=whole(len(outs)),
+        in_specs=in_specs,
+        out_specs=spaces(len(outs), hbm_outs),
         out_shape=[jax.ShapeDtypeStruct(shape, dtype) for shape, dtype in outs],
-        scratch_shapes=[pltpu.VMEM(shape, dtype) for shape, dtype in scratch],
+        scratch_shapes=scratch,
         compiler_params=pltpu.CompilerParams(vmem_limit_bytes=VMEM_LIMIT),
     )(*args)
 
@@ -346,43 +400,59 @@
     rate_out = ((members, R), F32)
     top_out = ((EXTRA, R), F32)
     coef_out = ((members, R), BF16)
-    field_tmp = ((rows, block), F32)
+    chem = (reactants.T, stoich.T, rate_consts, loss_rates)
+    react_tmp = [
+        pltpu.VMEM((rows, block), F32),
+        *(pltpu.SMEM(value.shape, value.dtype) for value in chem),
+        pltpu.SemaphoreType.DMA((len(chem),)),
+    ]
     square = ((R, R), F32)
     square_bf = ((R, R), BF16)
-    weights = stoich.astype(F32).T * rate_consts[None, :]
-    chem = (counts, reactants.T, jnp.concatenate([weights, loss_rates[:, None]], 1))
-
-    def setup(modes):
+
+    def stage(counts):
+        index = emis_idx.reshape(1, members)
         return call(
-            functools.partial(setup_kernel, columns), 2,
-            [rows_f32, ((S, members), F32), ((columns * LEV, R), F32)], [],
-            counts, emis_table.T, modes, diffusivity, emis_idx.reshape(1, members),
-        )
+            functools.partial(stage_kernel, columns), 4,
+            [rows_f32, ((S, members), F32), ((columns * LEV, R), F32)],
+            [
+                pltpu.SMEM((S, NEMIS), F32),
+                pltpu.VMEM(diffusivity.shape, F32),
+                pltpu.VMEM((1, members), jnp.int32),
+                pltpu.SemaphoreType.DMA((4,)),
+            ],
+            emis_table.T, diffusivity, index, mode_rows, counts=counts,
+        )
+
+    def spread(modes, face):
+        return call(diffuse_kernel, 0, [rows_f32], [], modes, face)[0]
 
     if n == 16:
-        plan = ((1, 4), (2, 5), (3, 6), (0, 7))
+        plan = ((1, 2), (4, 3), (5, 6), (0, 7))
         other = swap(coeffs, n, (1, 1))
+        modes, emis, face = stage(counts)
+        other, modes = lax.optimization_barrier((other, modes))
         side = lax.axis_index("col") & 1
         chip = jnp.where(
             side == 0, jnp.concatenate([coeffs, other], 0), jnp.concatenate([other, coeffs], 0)
         )
-        fetched = [swap(chip, n, (2 * a, 2 * b)) for a, b in plan]
-        diff, emis, face = setup(tied(mode_rows, chip))
-        fetched, diff = lax.optimization_barrier((fetched, diff))
-        mine_rows = jnp.concatenate(fetched, 0)
-        gathered = (chip, mine_rows, swap(mine_rows, n, (1, 1)))
+        mine_rows = jnp.concatenate([swap(chip, n, (2 * a, 2 * b)) for a, b in plan], 0)
+        theirs = swap(mine_rows, n, (1, 1))
+        diff = spread(tied(modes, mine_rows), face)
+        theirs, diff = lax.optimization_barrier((theirs, diff))
+        gathered = (chip, mine_rows, theirs)
         tend, rate, top, coef = call(
-            functools.partial(first_kernel, columns, plan), 3,
-            [tend_out, rate_out, top_out, coef_out], [field_tmp],
-            *chem, diff, emis, *gathered,
+            functools.partial(first_kernel, columns, plan), 4,
+            [tend_out, rate_out, top_out, coef_out], react_tmp,
+            *chem, diff, emis, *gathered, counts=counts,
         )
     else:
         coef = lax.all_to_all(jnp.tile(coeffs, (n, 1)), "col", 0, 0, tiled=True)
-        diff, emis, face = setup(mode_rows)
+        modes, emis, face = stage(counts)
+        diff = spread(modes, face)
         tend, rate, top = call(
-            functools.partial(first_kernel, columns, ()), 3,
-            [tend_out, rate_out, top_out], [field_tmp],
-            *chem, diff, emis, coef,
+            functools.partial(first_kernel, columns, ()), 4,
+            [tend_out, rate_out, top_out], react_tmp,
+            *chem, diff, emis, coef, counts=counts,
         )
 
     def summed(rate, top, coef, tend):
@@ -395,7 +465,7 @@
         def end(state, ready):
             high, low, inv, gap = tied(state, ready)
             return call(
-                inverse_end, 0, [rate_out, rows_f32], [square], gap, high, low, inv, coef, tend
+                inverse_end, 0, [rate_out, rows_f32], [pltpu.VMEM((R, R), F32)], gap, high, low, inv, coef, tend
             )
 
         return sum_over(rate, top, n, (start, end))
@@ -403,16 +473,17 @@
     for _ in range(NSUB - 1):
         total, (solved, pull) = summed(rate, top, coef, tend)
         diff, tend, rate, top, coef = call(
-            functools.partial(middle_kernel, columns, total_rows), 3,
-            [rows_f32, tend_out, rate_out, top_out, coef_out], [field_tmp],
-            *chem, diff, pull, solved, total, coef, face, emis,
+            functools.partial(middle_kernel, columns, total_rows), 4,
+            [rows_f32, tend_out, rate_out, top_out, coef_out], react_tmp,
+            *chem, diff, pull, solved, total, coef, face, emis, counts=counts,
         )
     total, (solved, pull) = summed(rate, top, coef, tend)
     return tuple(
         call(
             functools.partial(last_kernel, total_rows), 0,
-            [rows_f32, ((mine, R), BF16)], [],
-            diff, pull, solved, total, coef,
+            [rows_f32, ((mine, R), BF16)],
+            [pltpu.VMEM((rows, R), F32), pltpu.SemaphoreType.DMA((4,))],
+            diff, pull, solved, total, coef, hbm_outs=1,
         )
     )
 

time: 57.1 us -> 55.4 us (0.970)
  waiting for transfers between devices: 10.2 us -> 15.1 us
  starting transfers between devices: 21.9 us -> 18.2 us
  local copies, waits for them, and re-layouts: 3.24 us -> 0.08 us
    ppermute x18, waiting for transfers between devices: 10.2 us -> 15.1 us  [swap(): lax.ppermute(value, 'col', [(i, i ^ masks[i % 2]) for i in range(n) if ma...]
    ppermute x18, starting transfers between devices: 21.9 us -> 18.2 us  [swap(): lax.ppermute(value, 'col', [(i, i ^ masks[i % 2]) for i in range(n) if ma...]
    unnamed x21 -> x5, local copies, waits for them, and re-layouts: 3.09 us -> 0.01 us
    pallas_call x8 -> x9, Pallas kernels: 19.3 us -> 19.7 us  [call(): pl.pallas_call(kernel, in_specs=in_specs, out_specs=spaces(len(outs), hbm...]
  transfers between devices with their start and end apart: 18 -> 18, of which waited for: 11 -> 10; matrix products, arithmetic and copies ran while one was open for 0% -> 0% of each run, Pallas kernels for 23% -> 24%
where the time goes in v4:
time: 55.4 us; the launch traced here: 55.2 us
  Pallas kernels  19.7 us (36%)
  starting transfers between devices  18.2 us (33%)
  waiting for transfers between devices  15.1 us (27%)
  between operations  1.6 us (3%)
  other arithmetic  0.58 us (1%)
    pallas_call x9, Pallas kernels, call(): pl.pallas_call(kernel, in_specs=in_specs, out_specs=spaces(len(outs), hbm...  19.7 us
    ppermute x18, starting transfers between devices, swap(): lax.ppermute(value, 'col', [(i, i ^ masks[i % 2]) for i in range(n) if ma...  18.2 us
    ppermute x18, waiting for transfers between devices, swap(): lax.ppermute(value, 'col', [(i, i ^ masks[i % 2]) for i in range(n) if ma...  15.1 us
  transfers between devices with their start and end apart: 18, of which 10 were waited for; matrix products, arithmetic and copies ran while one was open for 0% of the time, Pallas kernels for 24%

profile of v4, /device:TPU:0, one launch (start us, length us, event | category | flops | bytes accessed | tf_op | source)
XLA Modules:
  0.0 55.2 jit_solution(8595701147902471640)
XLA Ops:
  0.6 0.5 collective-permute-start
  1.8 0.0 copy-start
  1.8 1.1 %shard_map.113 = (f32[512,256]{1,0:T(8,128)S(1)}, f32[8,256]{1,0:T(8,128)S(1)}, f32[64,256]{1,0:T(8,128)S(1)}) custom-call(s32[1]{0:T(128)S(6)} %copy.15.counts_ref, f32[8,16]{1,0:T(8,128)} %bitcast.22, f32[1,64]{1,0:T(1,128)} %level_face_hbm.1, s32[1,256]{1,0:T(1,128)} %bitcast.41, f32[512,256]{1,0:T(8,128)} %modes_hbm.1), custom_call_target="tpu_custom_call" | custom-call | tf_op jit(solution)/shard_map/pallas_call | solution.py:306
  2.9 0.0 collective-permute-done
  2.9 0.0 copy-done
  2.9 2.6 %collective-permute-start.1 = (bf16[32,256]{1,0:T(8,128)(2,1)S(1)}, bf16[32,256]{1,0:T(8,128)(2,1)S(1)}, u32[]{:S(2)}, u32[]{:S(2)}) collective-permute-start(bf16[32,256]{1,0:T(8,128)(2,1)S(1)} %maximum_select_fusion.2.allrefs_6_), channel_id=1, source_target_pairs={{0,2},{1,5},{2,0},{3,7},{4,6},{5,1},{6,4},{7,3},{8,10},{9,13},{10,... | collective-permute-start | bytes 49160 | tf_op jit(solution)/shard_map/ppermute | solution.py:321
  5.5 0.7 %collective-permute-start.4 = (bf16[32,256]{1,0:T(8,128)(2,1)S(1)}, bf16[32,256]{1,0:T(8,128)(2,1)S(1)}, u32[]{:S(2)}, u32[]{:S(2)}) collective-permute-start(bf16[32,256]{1,0:T(8,128)(2,1)S(1)} %maximum_select_fusion.2.allrefs_6_), channel_id=1, source_target_pairs={{1,15},{3,13},{5,11},{7,9},{9,7},{11,5},{13,3},{15,1},{17,31},{19,... | collective-permute-start | bytes 49160 | tf_op jit(solution)/shard_map/ppermute | solution.py:321
  6.2 2.6 %collective-permute-start.3 = (bf16[32,256]{1,0:T(8,128)(2,1)S(1)}, bf16[32,256]{1,0:T(8,128)(2,1)S(1)}, u32[]{:S(2)}, u32[]{:S(2)}) collective-permute-start(bf16[32,256]{1,0:T(8,128)(2,1)S(1)} %maximum_select_fusion.2.allrefs_6_), channel_id=1, source_target_pairs={{0,10},{1,13},{2,8},{3,15},{4,14},{5,9},{6,12},{7,11},{8,2},{9,5},... | collective-permute-start | bytes 49160 | tf_op jit(solution)/shard_map/ppermute | solution.py:321
  8.8 0.1 collective-permute-start.2
  8.9 0.0 collective-permute-done.1
  8.9 4.5 %collective-permute-done.2 = bf16[32,256]{1,0:T(8,128)(2,1)S(1)} collective-permute-done((bf16[32,256]{1,0:T(8,128)(2,1)S(1)}, bf16[32,256]{1,0:T(8,128)(2,1)S(1)}, u32[]{:S(2)}, u32[]{:S(2)}) %collective-permute-start.2) | collective-permute-done | bytes 16416 | tf_op jit(solution)/shard_map/ppermute | solution.py:321
  13.4 0.0 collective-permute-done.3
  13.4 0.0 collective-permute-done.4
  13.5 2.2 %collective-permute-start.5 = (bf16[128,256]{1,0:T(8,128)(2,1)S(1)}, bf16[128,256]{1,0:T(8,128)(2,1)S(1)}, u32[]{:S(2)}, u32[]{:S(2)}) collective-permute-start(bf16[128,256]{1,0:T(8,128)(2,1)S(1)} %constant_dynamic-update-slice_fusion.allrefs_7_), channel_id=1, source_target_pairs={{0,1},{1,0},{2,3},{3,2},{4,5},{5,4},{6,7},{7,6},{8,9},{9,8},{10,11... | collective-permute-start | bytes 196616 | tf_op jit(solution)/shard_map/ppermute | solution.py:321
  15.6 0.1 shard_map.114.allrefs_4_.diff_in_ref
  15.8 0.8 %collective-permute-done.5.allrefs_8_ = bf16[128,256]{1,0:T(8,128)(2,1)S(1)} collective-permute-done((bf16[128,256]{1,0:T(8,128)(2,1)S(1)}, bf16[128,256]{1,0:T(8,128)(2,1)S(1)}, u32[]{:S(2)}, u32[]{:S(2)}) %collective-permute-start.5) | collective-permute-done | bytes 65568 | tf_op jit(solution)/shard_map/ppermute | solution.py:321
  16.6 2.1 %shard_map.115 = (bf16[512,256]{1,0:T(8,128)(2,1)S(1)}, f32[256,256]{1,0:T(8,128)S(1)}, f32[8,256]{1,0:T(8,128)S(1)}, bf16[256,256]{1,0:T(8,128)(2,1)S(1)}) custom-call(s32[1]{0:T(128)S(6)} %copy.15.counts_ref, s32[2,12]{1,0:T(2,128)} %bitcast.23, s32[8,12]{1,0:T(8,128)} %bitcast.20, f32[12]{0:T(128)} %speed_hbm.1, f32[8]{0:T(128)} %loss_hbm.1, ...), custom_call_target="tpu_custom_call" | custom-call | tf_op jit(solution)/shard_map/pallas_call | solution.py:306
  18.7 0.4 collective-permute-start.6
  19.1 1.0 %collective-permute-done.6 = f32[136,256]{1,0:T(8,128)S(1)} collective-permute-done((f32[136,256]{1,0:T(8,128)S(1)}, f32[136,256]{1,0:T(8,128)S(1)}, u32[]{:S(2)}, u32[]{:S(2)}) %collective-permute-start.6) | collective-permute-done | bytes 139296 | tf_op jit(solution)/shard_map/ppermute | solution.py:321
  20.2 1.0 %collective-permute-start.9 = (f16[136,256]{1,0:T(8,128)(2,1)S(1)}, f16[136,256]{1,0:T(8,128)(2,1)S(1)}, u32[]{:S(2)}, u32[]{:S(2)}) collective-permute-start(f16[136,256]{1,0:T(8,128)(2,1)S(1)} %pad_maximum_fusion.2), channel_id=1, source_target_pairs={{0,6},{1,7},{2,4},{3,5},{4,2},{5,3},{6,0},{7,1},{8,14},{9,15},{10,... | collective-permute-start | bytes 208904 | tf_op jit(solution)/shard_map/ppermute | solution.py:321
  21.1 1.1 %collective-permute-start.8 = (f16[136,256]{1,0:T(8,128)(2,1)S(1)}, f16[136,256]{1,0:T(8,128)(2,1)S(1)}, u32[]{:S(2)}, u32[]{:S(2)}) collective-permute-start(f16[136,256]{1,0:T(8,128)(2,1)S(1)} %pad_maximum_fusion.2), channel_id=1, source_target_pairs={{0,4},{1,5},{2,6},{3,7},{4,0},{5,1},{6,2},{7,3},{8,12},{9,13},{10,... | collective-permute-start | bytes 208904 | tf_op jit(solution)/shard_map/ppermute | solution.py:321
  22.2 1.5 %collective-permute-start.7 = (f16[136,256]{1,0:T(8,128)(2,1)S(1)}, f16[136,256]{1,0:T(8,128)(2,1)S(1)}, u32[]{:S(2)}, u32[]{:S(2)}) collective-permute-start(f16[136,256]{1,0:T(8,128)(2,1)S(1)} %pad_maximum_fusion.2), channel_id=1, source_target_pairs={{0,2},{1,3},{2,0},{3,1},{4,6},{5,7},{6,4},{7,5},{8,10},{9,11},{10,... | collective-permute-start | bytes 208904 | tf_op jit(solution)/shard_map/ppermute | solution.py:321
  23.8 2.5 %shard_map.116 = (bf16[256,256]{1,0:T(8,128)(2,1)S(1)}, bf16[256,256]{1,0:T(8,128)(2,1)S(1)}, f32[256,256]{1,0:T(8,128)S(1)}, f32[8,256]{1,0:T(8,128)S(1)}) custom-call(bf16[256,256]{1,0:T(8,128)(2,1)S(1)} %get-tuple-element.72.coef_ref), custom_call_target="tpu_custom_call" | custom-call | tf_op jit(solution)/shard_map/pallas_call | solution.py:306
  26.3 0.0 collective-permute-done.9
  26.3 0.0 collective-permute-done.8
  26.3 0.8 %collective-permute-done.7 = f16[136,256]{1,0:T(8,128)(2,1)S(1)} collective-permute-done((f16[136,256]{1,0:T(8,128)(2,1)S(1)}, f16[136,256]{1,0:T(8,128)(2,1)S(1)}, u32[]{:S(2)}, u32[]{:S(2)}) %collective-permute-start.7) | collective-permute-done | bytes 69664 | tf_op jit(solution)/shard_map/ppermute | solution.py:321
  27.1 0.1 multiply_convert_fusion.1
  27.2 1.0 %collective-permute-start.10 = (f16[136,256]{1,0:T(8,128)(2,1)S(1)}, f16[136,256]{1,0:T(8,128)(2,1)S(1)}, u32[]{:S(2)}, u32[]{:S(2)}) collective-permute-start(f16[136,256]{1,0:T(8,128)(2,1)S(1)} %pad_maximum_fusion.3), channel_id=1, source_target_pairs={{0,8},{1,9},{2,10},{3,11},{4,12},{5,13},{6,14},{7,15},{8,0},{9,1},... | collective-permute-start | bytes 208904 | tf_op jit(solution)/shard_map/ppermute | solution.py:321
  28.2 3.5 %shard_map.117 = (f32[256,256]{1,0:T(8,128)S(1)}, f32[512,256]{1,0:T(8,128)S(1)}) custom-call(f32[8,256]{1,0:T(8,128)S(1)} %get-tuple-element.84.gap_in_ref, bf16[256,256]{1,0:T(8,128)(2,1)S(1)} %get-tuple-element.85.high_ref, bf16[256,256]{1,0:T(8,128)(2,1)S(1)} %get-tuple-element.86.low_ref, f32[256,256]{1,0:T(8,128)S(1)} %get-tuple-element.87.inv_in_ref, ...), custom_call_target="tpu_custom_call" | custom-call | tf_op jit(solution)/shard_map/pallas_call | solution.py:306
  31.7 1.5 %collective-permute-done.10 = f16[136,256]{1,0:T(8,128)(2,1)S(1)} collective-permute-done((f16[136,256]{1,0:T(8,128)(2,1)S(1)}, f16[136,256]{1,0:T(8,128)(2,1)S(1)}, u32[]{:S(2)}, u32[]{:S(2)}) %collective-permute-start.10) | collective-permute-done | bytes 69664 | tf_op jit(solution)/shard_map/ppermute | solution.py:321
  33.3 0.1 collective-permute-start.11
  33.4 1.3 %collective-permute-done.11 = f32[128,256]{1,0:T(8,128)S(1)} collective-permute-done((f32[128,256]{1,0:T(8,128)S(1)}, f32[128,256]{1,0:T(8,128)S(1)}, u32[]{:S(2)}, u32[]{:S(2)}) %collective-permute-start.11) | collective-permute-done | bytes 131104 | tf_op jit(solution)/shard_map/ppermute | solution.py:321
  34.7 2.3 %shard_map.118 = (f32[512,256]{1,0:T(8,128)S(1)}, bf16[512,256]{1,0:T(8,128)(2,1)S(1)}, f32[256,256]{1,0:T(8,128)S(1)}, f32[8,256]{1,0:T(8,128)S(1)}, bf16[256,256]{1,0:T(8,128)(2,1)S(1)}) custom-call(s32[1]{0:T(128)S(6)} %copy.15.counts_ref, s32[2,12]{1,0:T(2,128)} %bitcast.24, s32[8,12]{1,0:T(8,128)} %bitcast.21, f32[12]{0:T(128)} %speed_hbm.1, ...), custom_call_target="tpu_custom_call" | custom-call | tf_op jit(solution)/shard_map/pallas_call | solution.py:306
  37.1 0.2 collective-permute-start.12
  37.3 1.2 %collective-permute-done.12 = f32[136,256]{1,0:T(8,128)S(1)} collective-permute-done((f32[136,256]{1,0:T(8,128)S(1)}, f32[136,256]{1,0:T(8,128)S(1)}, u32[]{:S(2)}, u32[]{:S(2)}) %collective-permute-start.12) | collective-permute-done | bytes 139296 | tf_op jit(solution)/shard_map/ppermute | solution.py:321
  38.6 1.0 %collective-permute-start.15 = (f16[136,256]{1,0:T(8,128)(2,1)S(1)}, f16[136,256]{1,0:T(8,128)(2,1)S(1)}, u32[]{:S(2)}, u32[]{:S(2)}) collective-permute-start(f16[136,256]{1,0:T(8,128)(2,1)S(1)} %pad_maximum_fusion.4), channel_id=1, source_target_pairs={{0,6},{1,7},{2,4},{3,5},{4,2},{5,3},{6,0},{7,1},{8,14},{9,15},{10,... | collective-permute-start | bytes 208904 | tf_op jit(solution)/shard_map/ppermute | solution.py:321
  39.7 1.3 %collective-permute-start.14 = (f16[136,256]{1,0:T(8,128)(2,1)S(1)}, f16[136,256]{1,0:T(8,128)(2,1)S(1)}, u32[]{:S(2)}, u32[]{:S(2)}) collective-permute-start(f16[136,256]{1,0:T(8,128)(2,1)S(1)} %pad_maximum_fusion.4), channel_id=1, source_target_pairs={{0,4},{1,5},{2,6},{3,7},{4,0},{5,1},{6,2},{7,3},{8,12},{9,13},{10,... | collective-permute-start | bytes 208904 | tf_op jit(solution)/shard_map/ppermute | solution.py:321
  41.0 1.2 %collective-permute-start.13 = (f16[136,256]{1,0:T(8,128)(2,1)S(1)}, f16[136,256]{1,0:T(8,128)(2,1)S(1)}, u32[]{:S(2)}, u32[]{:S(2)}) collective-permute-start(f16[136,256]{1,0:T(8,128)(2,1)S(1)} %pad_maximum_fusion.4), channel_id=1, source_target_pairs={{0,2},{1,3},{2,0},{3,1},{4,6},{5,7},{6,4},{7,5},{8,10},{9,11},{10,... | collective-permute-start | bytes 208904 | tf_op jit(solution)/shard_map/ppermute | solution.py:321
  42.2 2.5 %shard_map.119 = (bf16[256,256]{1,0:T(8,128)(2,1)S(1)}, bf16[256,256]{1,0:T(8,128)(2,1)S(1)}, f32[256,256]{1,0:T(8,128)S(1)}, f32[8,256]{1,0:T(8,128)S(1)}) custom-call(bf16[256,256]{1,0:T(8,128)(2,1)S(1)} %get-tuple-element.98.coef_ref), custom_call_target="tpu_custom_call" | custom-call | tf_op jit(solution)/shard_map/pallas_call | solution.py:306
  44.7 0.0 collective-permute-done.15
  44.7 0.0 collective-permute-done.14
  44.7 0.7 %collective-permute-done.13 = f16[136,256]{1,0:T(8,128)(2,1)S(1)} collective-permute-done((f16[136,256]{1,0:T(8,128)(2,1)S(1)}, f16[136,256]{1,0:T(8,128)(2,1)S(1)}, u32[]{:S(2)}, u32[]{:S(2)}) %collective-permute-start.13) | collective-permute-done | bytes 69664 | tf_op jit(solution)/shard_map/ppermute | solution.py:321
  45.4 0.1 multiply_convert_fusion
  45.5 0.6 %collective-permute-start.16 = (f16[136,256]{1,0:T(8,128)(2,1)S(1)}, f16[136,256]{1,0:T(8,128)(2,1)S(1)}, u32[]{:S(2)}, u32[]{:S(2)}) collective-permute-start(f16[136,256]{1,0:T(8,128)(2,1)S(1)} %pad_maximum_fusion.5), channel_id=1, source_target_pairs={{0,8},{1,9},{2,10},{3,11},{4,12},{5,13},{6,14},{7,15},{8,0},{9,1},... | collective-permute-start | bytes 208904 | tf_op jit(solution)/shard_map/ppermute | solution.py:321
  46.2 3.5 %shard_map.120 = (f32[256,256]{1,0:T(8,128)S(1)}, f32[512,256]{1,0:T(8,128)S(1)}) custom-call(f32[8,256]{1,0:T(8,128)S(1)} %get-tuple-element.110.gap_in_ref, bf16[256,256]{1,0:T(8,128)(2,1)S(1)} %get-tuple-element.111.high_ref, bf16[256,256]{1,0:T(8,128)(2,1)S(1)} %get-tuple-element.112.low_ref, f32[256,256]{1,0:T(8,128)S(1)} %get-tuple-element.113.inv_in_ref, ...), custom_call_target="tpu_custom_call" | custom-call | tf_op jit(solution)/shard_map/pallas_call | solution.py:306
  49.7 1.9 %collective-permute-done.16 = f16[136,256]{1,0:T(8,128)(2,1)S(1)} collective-permute-done((f16[136,256]{1,0:T(8,128)(2,1)S(1)}, f16[136,256]{1,0:T(8,128)(2,1)S(1)}, u32[]{:S(2)}, u32[]{:S(2)}) %collective-permute-start.16) | collective-permute-done | bytes 69664 | tf_op jit(solution)/shard_map/ppermute | solution.py:321
  51.6 0.1 collective-permute-start.17
  51.7 1.3 %collective-permute-done.17 = f32[128,256]{1,0:T(8,128)S(1)} collective-permute-done((f32[128,256]{1,0:T(8,128)S(1)}, f32[128,256]{1,0:T(8,128)S(1)}, u32[]{:S(2)}, u32[]{:S(2)}) %collective-permute-start.17) | collective-permute-done | bytes 131104 | tf_op jit(solution)/shard_map/ppermute | solution.py:321
  53.0 2.1 %shard_map.121 = (f32[512,256]{1,0:T(8,128)}, bf16[16,256]{1,0:T(8,128)(2,1)}) custom-call(f32[512,256]{1,0:T(8,128)S(1)} %get-tuple-element.94.diff_in_ref, f32[512,256]{1,0:T(8,128)S(1)} %get-tuple-element.117.pull_ref, f32[256,256]{1,0:T(8,128)S(1)} %get-tuple-element.118.solve_ref, f32[256,256]{1,0:T(8,128)S(1)} %maximum_select_fusion.1.sum_ref, ...), custom_call_target="tpu_custom_call" | custom-call | tf_op jit(solution)/shard_map/pallas_call | solution.py:306
  (35 shorter events, 0.5 us)
Async XLA Ops:
  0.6 2.3 %collective-permute-start = (bf16[16,256]{1,0:T(8,128)(2,1)}, bf16[16,256]{1,0:T(8,128)(2,1)S(1)}, u32[]{:S(2)}, u32[]{:S(2)}) collective-permute-start(bf16[16,256]{1,0:T(8,128)(2,1)} %param.11), channel_id=1, source_target_pairs={{0,1},{1,0},{2,3},{3,2},{4,5},{5,4},{6,7},{7,6},{8,9},{9,8},{10,11... | collective-permute-start | bytes 24584 | tf_op jit(solution)/shard_map/ppermute | solution.py:321
  1.8 1.1 %copy-start = (bf16[16,256]{1,0:T(8,128)(2,1)S(1)}, bf16[16,256]{1,0:T(8,128)(2,1)}, u32[]{:S(2)}) copy-start(bf16[16,256]{1,0:T(8,128)(2,1)} %param.11) | copy-start | bytes 24580
  2.9 6.0 %collective-permute-start.1 = (bf16[32,256]{1,0:T(8,128)(2,1)S(1)}, bf16[32,256]{1,0:T(8,128)(2,1)S(1)}, u32[]{:S(2)}, u32[]{:S(2)}) collective-permute-start(bf16[32,256]{1,0:T(8,128)(2,1)S(1)} %maximum_select_fusion.2.allrefs_6_), channel_id=1, source_target_pairs={{0,2},{1,5},{2,0},{3,7},{4,6},{5,1},{6,4},{7,3},{8,10},{9,13},{10,... | collective-permute-start | bytes 49160 | tf_op jit(solution)/shard_map/ppermute | solution.py:321
  5.5 7.9 %collective-permute-start.4 = (bf16[32,256]{1,0:T(8,128)(2,1)S(1)}, bf16[32,256]{1,0:T(8,128)(2,1)S(1)}, u32[]{:S(2)}, u32[]{:S(2)}) collective-permute-start(bf16[32,256]{1,0:T(8,128)(2,1)S(1)} %maximum_select_fusion.2.allrefs_6_), channel_id=1, source_target_pairs={{1,15},{3,13},{5,11},{7,9},{9,7},{11,5},{13,3},{15,1},{17,31},{19,... | collective-permute-start | bytes 49160 | tf_op jit(solution)/shard_map/ppermute | solution.py:321
  6.2 7.2 %collective-permute-start.3 = (bf16[32,256]{1,0:T(8,128)(2,1)S(1)}, bf16[32,256]{1,0:T(8,128)(2,1)S(1)}, u32[]{:S(2)}, u32[]{:S(2)}) collective-permute-start(bf16[32,256]{1,0:T(8,128)(2,1)S(1)} %maximum_select_fusion.2.allrefs_6_), channel_id=1, source_target_pairs={{0,10},{1,13},{2,8},{3,15},{4,14},{5,9},{6,12},{7,11},{8,2},{9,5},... | collective-permute-start | bytes 49160 | tf_op jit(solution)/shard_map/ppermute | solution.py:321
  8.8 4.6 %collective-permute-start.2 = (bf16[32,256]{1,0:T(8,128)(2,1)S(1)}, bf16[32,256]{1,0:T(8,128)(2,1)S(1)}, u32[]{:S(2)}, u32[]{:S(2)}) collective-permute-start(bf16[32,256]{1,0:T(8,128)(2,1)S(1)} %maximum_select_fusion.2.allrefs_6_), channel_id=1, source_target_pairs={{0,8},{1,7},{2,10},{3,5},{4,12},{5,3},{6,14},{7,1},{8,0},{9,15},{1... | collective-permute-start | bytes 49160 | tf_op jit(solution)/shard_map/ppermute | solution.py:321
  13.5 3.1 %collective-permute-start.5 = (bf16[128,256]{1,0:T(8,128)(2,1)S(1)}, bf16[128,256]{1,0:T(8,128)(2,1)S(1)}, u32[]{:S(2)}, u32[]{:S(2)}) collective-permute-start(bf16[128,256]{1,0:T(8,128)(2,1)S(1)} %constant_dynamic-update-slice_fusion.allrefs_7_), channel_id=1, source_target_pairs={{0,1},{1,0},{2,3},{3,2},{4,5},{5,4},{6,7},{7,6},{8,9},{9,8},{10,11... | collective-permute-start | bytes 196616 | tf_op jit(solution)/shard_map/ppermute | solution.py:321
  18.7 1.4 %collective-permute-start.6 = (f32[136,256]{1,0:T(8,128)S(1)}, f32[136,256]{1,0:T(8,128)S(1)}, u32[]{:S(2)}, u32[]{:S(2)}) collective-permute-start(f32[136,256]{1,0:T(8,128)S(1)} %pad_maximum_fusion), channel_id=1, source_target_pairs={{0,1},{1,0},{2,3},{3,2},{4,5},{5,4},{6,7},{7,6},{8,9},{9,8},{10,11... | collective-permute-start | bytes 417800 | tf_op jit(solution)/shard_map/ppermute | solution.py:321
  20.2 6.1 %collective-permute-start.9 = (f16[136,256]{1,0:T(8,128)(2,1)S(1)}, f16[136,256]{1,0:T(8,128)(2,1)S(1)}, u32[]{:S(2)}, u32[]{:S(2)}) collective-permute-start(f16[136,256]{1,0:T(8,128)(2,1)S(1)} %pad_maximum_fusion.2), channel_id=1, source_target_pairs={{0,6},{1,7},{2,4},{3,5},{4,2},{5,3},{6,0},{7,1},{8,14},{9,15},{10,... | collective-permute-start | bytes 208904 | tf_op jit(solution)/shard_map/ppermute | solution.py:321
  21.1 5.1 %collective-permute-start.8 = (f16[136,256]{1,0:T(8,128)(2,1)S(1)}, f16[136,256]{1,0:T(8,128)(2,1)S(1)}, u32[]{:S(2)}, u32[]{:S(2)}) collective-permute-start(f16[136,256]{1,0:T(8,128)(2,1)S(1)} %pad_maximum_fusion.2), channel_id=1, source_target_pairs={{0,4},{1,5},{2,6},{3,7},{4,0},{5,1},{6,2},{7,3},{8,12},{9,13},{10,... | collective-permute-start | bytes 208904 | tf_op jit(solution)/shard_map/ppermute | solution.py:321
  22.2 4.9 %collective-permute-start.7 = (f16[136,256]{1,0:T(8,128)(2,1)S(1)}, f16[136,256]{1,0:T(8,128)(2,1)S(1)}, u32[]{:S(2)}, u32[]{:S(2)}) collective-permute-start(f16[136,256]{1,0:T(8,128)(2,1)S(1)} %pad_maximum_fusion.2), channel_id=1, source_target_pairs={{0,2},{1,3},{2,0},{3,1},{4,6},{5,7},{6,4},{7,5},{8,10},{9,11},{10,... | collective-permute-start | bytes 208904 | tf_op jit(solution)/shard_map/ppermute | solution.py:321
  27.2 6.0 %collective-permute-start.10 = (f16[136,256]{1,0:T(8,128)(2,1)S(1)}, f16[136,256]{1,0:T(8,128)(2,1)S(1)}, u32[]{:S(2)}, u32[]{:S(2)}) collective-permute-start(f16[136,256]{1,0:T(8,128)(2,1)S(1)} %pad_maximum_fusion.3), channel_id=1, source_target_pairs={{0,8},{1,9},{2,10},{3,11},{4,12},{5,13},{6,14},{7,15},{8,0},{9,1},... | collective-permute-start | bytes 208904 | tf_op jit(solution)/shard_map/ppermute | solution.py:321
  33.3 1.4 %collective-permute-start.11 = (f32[128,256]{1,0:T(8,128)S(1)}, f32[128,256]{1,0:T(8,128)S(1)}, u32[]{:S(2)}, u32[]{:S(2)}) collective-permute-start(f32[128,256]{1,0:T(8,128)S(1)} %multiply_add_fusion.1), channel_id=1, source_target_pairs={{0,1},{1,0},{2,3},{3,2},{4,5},{5,4},{6,7},{7,6},{8,9},{9,8},{10,11... | collective-permute-start | bytes 393224 | tf_op jit(solution)/shard_map/ppermute | solution.py:321
  37.1 1.4 %collective-permute-start.12 = (f32[136,256]{1,0:T(8,128)S(1)}, f32[136,256]{1,0:T(8,128)S(1)}, u32[]{:S(2)}, u32[]{:S(2)}) collective-permute-start(f32[136,256]{1,0:T(8,128)S(1)} %pad_maximum_fusion.1), channel_id=1, source_target_pairs={{0,1},{1,0},{2,3},{3,2},{4,5},{5,4},{6,7},{7,6},{8,9},{9,8},{10,11... | collective-permute-start | bytes 417800 | tf_op jit(solution)/shard_map/ppermute | solution.py:321
  38.6 6.1 %collective-permute-start.15 = (f16[136,256]{1,0:T(8,128)(2,1)S(1)}, f16[136,256]{1,0:T(8,128)(2,1)S(1)}, u32[]{:S(2)}, u32[]{:S(2)}) collective-permute-start(f16[136,256]{1,0:T(8,128)(2,1)S(1)} %pad_maximum_fusion.4), channel_id=1, source_target_pairs={{0,6},{1,7},{2,4},{3,5},{4,2},{5,3},{6,0},{7,1},{8,14},{9,15},{10,... | collective-permute-start | bytes 208904 | tf_op jit(solution)/shard_map/ppermute | solution.py:321
  39.7 5.0 %collective-permute-start.14 = (f16[136,256]{1,0:T(8,128)(2,1)S(1)}, f16[136,256]{1,0:T(8,128)(2,1)S(1)}, u32[]{:S(2)}, u32[]{:S(2)}) collective-permute-start(f16[136,256]{1,0:T(8,128)(2,1)S(1)} %pad_maximum_fusion.4), channel_id=1, source_target_pairs={{0,4},{1,5},{2,6},{3,7},{4,0},{5,1},{6,2},{7,3},{8,12},{9,13},{10,... | collective-permute-start | bytes 208904 | tf_op jit(solution)/shard_map/ppermute | solution.py:321
  41.0 4.4 %collective-permute-start.13 = (f16[136,256]{1,0:T(8,128)(2,1)S(1)}, f16[136,256]{1,0:T(8,128)(2,1)S(1)}, u32[]{:S(2)}, u32[]{:S(2)}) collective-permute-start(f16[136,256]{1,0:T(8,128)(2,1)S(1)} %pad_maximum_fusion.4), channel_id=1, source_target_pairs={{0,2},{1,3},{2,0},{3,1},{4,6},{5,7},{6,4},{7,5},{8,10},{9,11},{10,... | collective-permute-start | bytes 208904 | tf_op jit(solution)/shard_map/ppermute | solution.py:321
  45.5 6.0 %collective-permute-start.16 = (f16[136,256]{1,0:T(8,128)(2,1)S(1)}, f16[136,256]{1,0:T(8,128)(2,1)S(1)}, u32[]{:S(2)}, u32[]{:S(2)}) collective-permute-start(f16[136,256]{1,0:T(8,128)(2,1)S(1)} %pad_maximum_fusion.5), channel_id=1, source_target_pairs={{0,8},{1,9},{2,10},{3,11},{4,12},{5,13},{6,14},{7,15},{8,0},{9,1},... | collective-permute-start | bytes 208904 | tf_op jit(solution)/shard_map/ppermute | solution.py:321
  51.6 1.4 %collective-permute-start.17 = (f32[128,256]{1,0:T(8,128)S(1)}, f32[128,256]{1,0:T(8,128)S(1)}, u32[]{:S(2)}, u32[]{:S(2)}) collective-permute-start(f32[128,256]{1,0:T(8,128)S(1)} %multiply_add_fusion), channel_id=1, source_target_pairs={{0,1},{1,0},{2,3},{3,2},{4,5},{5,4},{6,7},{7,6},{8,9},{9,8},{10,11... | collective-permute-start | bytes 393224 | tf_op jit(solution)/shard_map/ppermute | solution.py:321

commit v5 on v4

--- a/solution.py
+++ b/solution.py
@@ -66,7 +66,7 @@
 
 
 def react(
-    diffused, coef_ref, emis_ref, ready, counts_ref, pair_ref, stoich_ref, speed_ref, loss_ref,
+    diffused, coef_ref, emis_ref, live_ref, ready, pair_ref, stoich_ref, speed_ref, loss_ref,
     field_ref, tend_ref, rate_ref, top_ref, columns,
 ):
     mode_bf = diffused.astype(BF16)
@@ -87,16 +87,16 @@
             base = c * (S * LEV) + low
             level = lax.broadcasted_iota(jnp.int32, (step, block), 0) + low
             profile = jnp.exp(level.astype(F32) * (-4.0 / LEV))
-            live = level < counts_ref[c]
+            live = live_ref[pl.ds(pl.multiple_of(c * LEV + low, step), step), 0:block] > 0.5
 
             def amount(s):
                 return field_ref[pl.ds(pl.multiple_of(base + s * LEV, step), step), :]
 
             total = []
             for s in range(S):
-                total.append(emis_ref[s : s + 1, lanes] * profile - loss_ref[s] * amount(s))
+                total.append(emis_ref[s : s + 1, lanes] * profile - loss_ref[0, s] * amount(s))
             for r in range(NREAC):
-                speed = speed_ref[r] * amount(pair_ref[0, r]) * amount(pair_ref[1, r])
+                speed = speed_ref[0, r] * amount(pair_ref[0, r]) * amount(pair_ref[1, r])
                 for s in range(S):
                     total[s] = total[s] + stoich_ref[s, r].astype(F32) * speed
             for s in range(S):
@@ -115,16 +115,18 @@
 
 def stage_kernel(
     columns,
-    counts_ref, table_hbm, level_face_hbm, idx_hbm, modes_hbm,
-    modes_ref, emis_ref, face_ref,
+    pair_hbm, stoich_hbm, speed_hbm, loss_hbm, table_hbm, level_face_hbm, idx_hbm, modes_hbm,
+    counts_ref,
+    pair_ref, stoich_ref, speed_ref, loss_ref, modes_ref, emis_ref, face_ref, live_ref,
     table_ref, level_face_ref, idx_ref, sems,
 ):
-    modes_copy = pltpu.make_async_copy(modes_hbm, modes_ref, sems.at[3])
-    modes_copy.start()
+    later = fetch(
+        (pair_hbm, stoich_hbm, speed_hbm, loss_hbm, modes_hbm),
+        (pair_ref, stoich_ref, speed_ref, loss_ref, modes_ref),
+        sems,
+    )
     fetch(
-        (table_hbm, level_face_hbm, idx_hbm),
-        (table_ref, level_face_ref, idx_ref),
-        sems,
+        (table_hbm, level_face_hbm, idx_hbm), (table_ref, level_face_ref, idx_ref), sems.at[5:8]
     )()
     index = idx_ref[...]
     for s in range(S):
@@ -134,11 +136,15 @@
         emis_ref[s : s + 1, :] = row
     down = lax.broadcasted_iota(jnp.int32, (LEV, LEV), 0)
     across = lax.broadcasted_iota(jnp.int32, (LEV, LEV), 1)
+    level = lax.broadcasted_iota(jnp.int32, (LEV, R), 0)
     for c in range(columns):
-        inner = (down == across) & (down + 1 < counts_ref[c])
+        part = slice(c * LEV, (c + 1) * LEV)
+        count = counts_ref[:, c : c + 1]
+        inner = (down == across) & (down + 1 < count)
         face = jnp.sum(jnp.where(inner, level_face_ref[c : c + 1, :], 0.0), axis=1, keepdims=True)
-        face_ref[c * LEV : (c + 1) * LEV, :] = jnp.broadcast_to(face, (LEV, R))
-    modes_copy.wait()
+        face_ref[part, :] = jnp.broadcast_to(face, (LEV, R))
+        live_ref[part, :] = jnp.where(level < count, 1.0, 0.0)
+    later()
 
 
 def diffuse_kernel(modes_ref, face_ref, diff_ref):
@@ -147,11 +153,11 @@
 
 def first_kernel(
     columns, plan,
-    counts_ref, *allrefs,
-):
-    chem_hbm, chem, sems = allrefs[:4], allrefs[-5:-1], allrefs[-1]
-    diff_ref, emis_ref, *refs, field_ref = allrefs[4:-5]
-    ready = fetch(chem_hbm, chem, sems)
+    *allrefs,
+):
+    chem_in, chem, sems = allrefs[:4], allrefs[-5:-1], allrefs[-1]
+    diff_ref, emis_ref, live_ref, *refs, field_ref = allrefs[4:-5]
+    ready = fetch(chem_in, chem, sems)
     if plan:
         chip_ref, mine_ref, theirs_ref, tend_ref, rate_ref, top_ref, coef_ref = refs
         rows = chip_ref.shape[0]
@@ -168,7 +174,7 @@
     else:
         coef_ref, tend_ref, rate_ref, top_ref = refs
     react(
-        diff_ref[...], coef_ref, emis_ref, ready, counts_ref, *chem,
+        diff_ref[...], coef_ref, emis_ref, live_ref, ready, *chem,
         field_ref, tend_ref, rate_ref, top_ref, columns,
     )
 
@@ -184,13 +190,13 @@
 
 def middle_kernel(
     columns, total_rows,
-    counts_ref, pair_hbm, stoich_hbm, speed_hbm, loss_hbm,
-    diff_in_ref, pull_ref, solve_ref, sum_ref, coef_ref, face_ref, emis_ref,
+    pair_in_ref, stoich_in_ref, speed_in_ref, loss_in_ref,
+    diff_in_ref, pull_ref, solve_ref, sum_ref, coef_ref, face_ref, emis_ref, live_ref,
     diff_ref, tend_ref, rate_ref, top_ref, coef_out_ref,
     field_ref, *chem_sems,
 ):
     *chem, sems = chem_sems
-    ready = fetch((pair_hbm, stoich_hbm, speed_hbm, loss_hbm), chem, sems)
+    ready = fetch((pair_in_ref, stoich_in_ref, speed_in_ref, loss_in_ref), chem, sems)
     raw = sum_ref[...]
     coef_out_ref[...] = (
         coef_ref[...].astype(F32) + RATE_STEP * (raw * (math.sqrt(R) / total_rows))
@@ -200,7 +206,7 @@
     diffused = diffuse_rows(modes, face_ref)
     diff_ref[...] = diffused
     react(
-        diffused, coef_out_ref, emis_ref, ready, counts_ref, *chem,
+        diffused, coef_out_ref, emis_ref, live_ref, ready, *chem,
         field_ref, tend_ref, rate_ref, top_ref, columns,
     )
 
@@ -208,8 +214,7 @@
 def last_kernel(
     total_rows,
     diff_in_ref, pull_ref, solve_ref, sum_ref, coef_ref,
-    modes_hbm, coef_out_ref,
-    modes_ref, sems,
+    modes_ref, coef_out_ref,
 ):
     mine = coef_out_ref.shape[0]
     own = pl.ds(pl.multiple_of(lax.axis_index("col") * mine, mine), mine)
@@ -218,22 +223,7 @@
         + RATE_STEP * (sum_ref[own, :] * (math.sqrt(R) / total_rows))
     ).astype(BF16)
     transfer = transfer_of(solve_ref, sum_ref[...] * (1.0 / total_rows))
-    parts = sems.shape[0]
-    rows = modes_ref.shape[0] // parts
-    copies = []
-    for i in range(parts):
-        block = slice(i * rows, (i + 1) * rows)
-        modes_ref[block, :] = advance(diff_in_ref[block, :], pull_ref[block, :], transfer)
-        copies.append(
-            pltpu.make_async_copy(
-                modes_ref.at[pl.ds(i * rows, rows), :],
-                modes_hbm.at[pl.ds(i * rows, rows), :],
-                sems.at[i],
-            )
-        )
-        copies[-1].start()
-    for copy in copies:
-        copy.wait()
+    modes_ref[...] = advance(diff_in_ref[...], pull_ref[...], transfer)
 
 
 def identity():
@@ -291,22 +281,18 @@
 VMEM_LIMIT = 48 * 1024 * 1024
 
 
-def call(kernel, n_hbm, outs, scratch, *args, counts=None, hbm_outs=0):
-    def spaces(n, left):
-        return [pl.BlockSpec(memory_space=pltpu.HBM if i < left else pltpu.VMEM) for i in range(n)]
-
-    in_specs = spaces(len(args), n_hbm)
+def call(kernel, n_hbm, outs, scratch, *args):
     args = [
         pltpu.with_memory_space_constraint(arg, pltpu.HBM) if i < n_hbm else arg
         for i, arg in enumerate(args)
     ]
-    if counts is not None:
-        in_specs = [pl.BlockSpec(memory_space=pltpu.SMEM)] + in_specs
-        args = [counts] + args
     return pl.pallas_call(
         kernel,
-        in_specs=in_specs,
-        out_specs=spaces(len(outs), hbm_outs),
+        in_specs=[
+            pl.BlockSpec(memory_space=pltpu.HBM if i < n_hbm else pltpu.VMEM)
+            for i in range(len(args))
+        ],
+        out_specs=[pl.BlockSpec(memory_space=pltpu.VMEM)] * len(outs),
         out_shape=[jax.ShapeDtypeStruct(shape, dtype) for shape, dtype in outs],
         scratch_shapes=scratch,
         compiler_params=pltpu.CompilerParams(vmem_limit_bytes=VMEM_LIMIT),
@@ -400,28 +386,31 @@
     rate_out = ((members, R), F32)
     top_out = ((EXTRA, R), F32)
     coef_out = ((members, R), BF16)
-    chem = (reactants.T, stoich.T, rate_consts, loss_rates)
+    tables = (reactants.T, stoich.T, rate_consts.reshape(1, NREAC), loss_rates.reshape(1, S))
     react_tmp = [
         pltpu.VMEM((rows, block), F32),
-        *(pltpu.SMEM(value.shape, value.dtype) for value in chem),
-        pltpu.SemaphoreType.DMA((len(chem),)),
+        *(pltpu.SMEM(value.shape, value.dtype) for value in tables),
+        pltpu.SemaphoreType.DMA((len(tables),)),
     ]
     square = ((R, R), F32)
     square_bf = ((R, R), BF16)
 
-    def stage(counts):
+    def stage(modes):
+        by_level = ((columns * LEV, R), F32)
         index = emis_idx.reshape(1, members)
-        return call(
-            functools.partial(stage_kernel, columns), 4,
-            [rows_f32, ((S, members), F32), ((columns * LEV, R), F32)],
+        *chem, modes, emis, face, live = call(
+            functools.partial(stage_kernel, columns), 8,
+            [(value.shape, value.dtype) for value in tables]
+            + [rows_f32, ((S, members), F32), by_level, by_level],
             [
                 pltpu.SMEM((S, NEMIS), F32),
                 pltpu.VMEM(diffusivity.shape, F32),
                 pltpu.VMEM((1, members), jnp.int32),
-                pltpu.SemaphoreType.DMA((4,)),
+                pltpu.SemaphoreType.DMA((8,)),
             ],
-            emis_table.T, diffusivity, index, mode_rows, counts=counts,
-        )
+            *tables, emis_table.T, diffusivity, index, modes, counts.reshape(1, columns),
+        )
+        return chem, modes, emis, face, live
 
     def spread(modes, face):
         return call(diffuse_kernel, 0, [rows_f32], [], modes, face)[0]
@@ -429,30 +418,31 @@
     if n == 16:
         plan = ((1, 2), (4, 3), (5, 6), (0, 7))
         other = swap(coeffs, n, (1, 1))
-        modes, emis, face = stage(counts)
-        other, modes = lax.optimization_barrier((other, modes))
         side = lax.axis_index("col") & 1
         chip = jnp.where(
             side == 0, jnp.concatenate([coeffs, other], 0), jnp.concatenate([other, coeffs], 0)
         )
-        mine_rows = jnp.concatenate([swap(chip, n, (2 * a, 2 * b)) for a, b in plan], 0)
+        fetched = [swap(chip, n, (2 * a, 2 * b)) for a, b in plan]
+        chem, modes, emis, face, live = stage(tied(mode_rows, chip))
+        fetched, modes = lax.optimization_barrier((fetched, modes))
+        mine_rows = jnp.concatenate(fetched, 0)
         theirs = swap(mine_rows, n, (1, 1))
         diff = spread(tied(modes, mine_rows), face)
         theirs, diff = lax.optimization_barrier((theirs, diff))
         gathered = (chip, mine_rows, theirs)
         tend, rate, top, coef = call(
-            functools.partial(first_kernel, columns, plan), 4,
+            functools.partial(first_kernel, columns, plan), 0,
             [tend_out, rate_out, top_out, coef_out], react_tmp,
-            *chem, diff, emis, *gathered, counts=counts,
+            *chem, diff, emis, live, *gathered,
         )
     else:
         coef = lax.all_to_all(jnp.tile(coeffs, (n, 1)), "col", 0, 0, tiled=True)
-        modes, emis, face = stage(counts)
+        chem, modes, emis, face, live = stage(mode_rows)
         diff = spread(modes, face)
         tend, rate, top = call(
-            functools.partial(first_kernel, columns, ()), 4,
+            functools.partial(first_kernel, columns, ()), 0,
             [tend_out, rate_out, top_out], react_tmp,
-            *chem, diff, emis, coef, counts=counts,
+            *chem, diff, emis, live, coef,
         )
 
     def summed(rate, top, coef, tend):
@@ -473,17 +463,16 @@
     for _ in range(NSUB - 1):
         total, (solved, pull) = summed(rate, top, coef, tend)
         diff, tend, rate, top, coef = call(
-            functools.partial(middle_kernel, columns, total_rows), 4,
+            functools.partial(middle_kernel, columns, total_rows), 0,
             [rows_f32, tend_out, rate_out, top_out, coef_out], react_tmp,
-            *chem, diff, pull, solved, total, coef, face, emis, counts=counts,
+            *chem, diff, pull, solved, total, coef, face, emis, live,
         )
     total, (solved, pull) = summed(rate, top, coef, tend)
     return tuple(
         call(
             functools.partial(last_kernel, total_rows), 0,
-            [rows_f32, ((mine, R), BF16)],
-            [pltpu.VMEM((rows, R), F32), pltpu.SemaphoreType.DMA((4,))],
-            diff, pull, solved, total, coef, hbm_outs=1,
+            [rows_f32, ((mine, R), BF16)], [],
+            diff, pull, solved, total, coef,
         )
     )
 

time: 55.4 us -> 53.7 us (0.969)
  waiting for transfers between devices: 15.1 us -> 11.3 us
  starting transfers between devices: 18.2 us -> 20.8 us
    ppermute x18, waiting for transfers between devices: 15.1 us -> 11.3 us  [swap(): lax.ppermute(value, 'col', [(i, i ^ masks[i % 2]) for i in range(n) if ma...]
    ppermute x18, starting transfers between devices: 18.2 us -> 20.8 us  [swap(): lax.ppermute(value, 'col', [(i, i ^ masks[i % 2]) for i in range(n) if ma...]
  transfers between devices with their start and end apart: 18 -> 18, of which waited for: 10 -> 12; matrix products, arithmetic and copies ran while one was open for 0% -> 0% of each run, Pallas kernels for 24% -> 25%
where the time goes in v5:
time: 53.7 us; the launch traced here: 53.5 us
  starting transfers between devices  20.8 us (39%)
  Pallas kernels  19.2 us (36%)
  waiting for transfers between devices  11.3 us (21%)
  between operations  1.58 us (3%)
  other arithmetic  0.57 us (1%)
    ppermute x18, starting transfers between devices, swap(): lax.ppermute(value, 'col', [(i, i ^ masks[i % 2]) for i in range(n) if ma...  20.8 us
    pallas_call x9, Pallas kernels, call(): pl.pallas_call(kernel, in_specs=[pl.BlockSpec(memory_space=pltpu.HBM if i...  19.2 us
    ppermute x18, waiting for transfers between devices, swap(): lax.ppermute(value, 'col', [(i, i ^ masks[i % 2]) for i in range(n) if ma...  11.3 us
  transfers between devices with their start and end apart: 18, of which 12 were waited for; matrix products, arithmetic and copies ran while one was open for 0% of the time, Pallas kernels for 25%

profile of v5, /device:TPU:0, one launch (start us, length us, event | category | flops | bytes accessed | tf_op | source)
XLA Modules:
  0.0 53.5 jit_solution(17365002133202633371)
XLA Ops:
  0.6 0.0 copy-start
  0.6 0.5 collective-permute-start
  1.2 1.0 %collective-permute-done = bf16[16,256]{1,0:T(8,128)(2,1)S(1)} collective-permute-done((bf16[16,256]{1,0:T(8,128)(2,1)}, bf16[16,256]{1,0:T(8,128)(2,1)S(1)}, u32[]{:S(2)}, u32[]{:S(2)}) %collective-permute-start) | collective-permute-done | bytes 8224 | tf_op jit(solution)/shard_map/ppermute | solution.py:307
  2.2 0.0 copy-done
  2.2 0.7 %collective-permute-start.4 = (bf16[32,256]{1,0:T(8,128)(2,1)S(1)}, bf16[32,256]{1,0:T(8,128)(2,1)S(1)}, u32[]{:S(2)}, u32[]{:S(2)}) collective-permute-start(bf16[32,256]{1,0:T(8,128)(2,1)S(1)} %maximum_select_fusion.2.allrefs_7_), channel_id=1, source_target_pairs={{1,15},{3,13},{5,11},{7,9},{9,7},{11,5},{13,3},{15,1},{17,31},{19,... | collective-permute-start | bytes 49160 | tf_op jit(solution)/shard_map/ppermute | solution.py:307
  2.9 5.0 %collective-permute-start.3 = (bf16[32,256]{1,0:T(8,128)(2,1)S(1)}, bf16[32,256]{1,0:T(8,128)(2,1)S(1)}, u32[]{:S(2)}, u32[]{:S(2)}) collective-permute-start(bf16[32,256]{1,0:T(8,128)(2,1)S(1)} %maximum_select_fusion.2.allrefs_7_), channel_id=1, source_target_pairs={{0,10},{1,13},{2,8},{3,15},{4,14},{5,9},{6,12},{7,11},{8,2},{9,5},... | collective-permute-start | bytes 49160 | tf_op jit(solution)/shard_map/ppermute | solution.py:307
  7.8 0.3 collective-permute-start.2
  8.2 0.3 collective-permute-start.1
  9.1 1.2 %shard_map.113 = (s32[2,12]{1,0:T(2,128)S(1)}, s32[8,12]{1,0:T(8,128)S(1)}, f32[1,12]{1,0:T(1,128)S(1)}, f32[1,8]{1,0:T(1,128)S(1)}, f32[512,256]{1,0:T(8,128)S(...) custom-call(s32[2,12]{1,0:T(2,128)} %bitcast.42, s32[8,12]{1,0:T(8,128)} %bitcast.24, ...), custom_call_target="tpu_custom_call" | custom-call | tf_op jit(solution)/shard_map/pallas_call | solution.py:289
  10.3 0.0 collective-permute-done.4
  10.3 0.0 collective-permute-done.3
  10.3 2.1 %collective-permute-done.2 = bf16[32,256]{1,0:T(8,128)(2,1)S(1)} collective-permute-done((bf16[32,256]{1,0:T(8,128)(2,1)S(1)}, bf16[32,256]{1,0:T(8,128)(2,1)S(1)}, u32[]{:S(2)}, u32[]{:S(2)}) %collective-permute-start.2) | collective-permute-done | bytes 16416 | tf_op jit(solution)/shard_map/ppermute | solution.py:307
  12.5 0.0 collective-permute-done.1
  12.5 2.0 %collective-permute-start.5 = (bf16[128,256]{1,0:T(8,128)(2,1)S(1)}, bf16[128,256]{1,0:T(8,128)(2,1)S(1)}, u32[]{:S(2)}, u32[]{:S(2)}) collective-permute-start(bf16[128,256]{1,0:T(8,128)(2,1)S(1)} %constant_dynamic-update-slice_fusion.allrefs_8_), channel_id=1, source_target_pairs={{0,1},{1,0},{2,3},{3,2},{4,5},{5,4},{6,7},{7,6},{8,9},{9,8},{10,11... | collective-permute-start | bytes 196616 | tf_op jit(solution)/shard_map/ppermute | solution.py:307
  14.5 0.1 shard_map.114.allrefs_4_.diff_in_ref
  14.6 0.8 %collective-permute-done.5.allrefs_9_ = bf16[128,256]{1,0:T(8,128)(2,1)S(1)} collective-permute-done((bf16[128,256]{1,0:T(8,128)(2,1)S(1)}, bf16[128,256]{1,0:T(8,128)(2,1)S(1)}, u32[]{:S(2)}, u32[]{:S(2)}) %collective-permute-start.5) | collective-permute-done | bytes 65568 | tf_op jit(solution)/shard_map/ppermute | solution.py:307
  15.4 1.7 %shard_map.115 = (bf16[512,256]{1,0:T(8,128)(2,1)S(1)}, f32[256,256]{1,0:T(8,128)S(1)}, f32[8,256]{1,0:T(8,128)S(1)}, bf16[256,256]{1,0:T(8,128)(2,1)S(1)}) custom-call(s32[2,12]{1,0:T(2,128)S(1)} %get-tuple-element.71.allrefs_0_.pair_in_ref, s32[8,12]{1,0:T(8,128)S(1)} %get-tuple-element.72.allrefs_1_.stoich_in_ref, ...), custom_call_target="tpu_custom_call" | custom-call | tf_op jit(solution)/shard_map/pallas_call | solution.py:289
  17.1 0.4 collective-permute-start.6
  17.5 1.0 %collective-permute-done.6 = f32[136,256]{1,0:T(8,128)S(1)} collective-permute-done((f32[136,256]{1,0:T(8,128)S(1)}, f32[136,256]{1,0:T(8,128)S(1)}, u32[]{:S(2)}, u32[]{:S(2)}) %collective-permute-start.6) | collective-permute-done | bytes 139296 | tf_op jit(solution)/shard_map/ppermute | solution.py:307
  18.6 1.0 %collective-permute-start.9 = (f16[136,256]{1,0:T(8,128)(2,1)S(1)}, f16[136,256]{1,0:T(8,128)(2,1)S(1)}, u32[]{:S(2)}, u32[]{:S(2)}) collective-permute-start(f16[136,256]{1,0:T(8,128)(2,1)S(1)} %pad_maximum_fusion.2), channel_id=1, source_target_pairs={{0,6},{1,7},{2,4},{3,5},{4,2},{5,3},{6,0},{7,1},{8,14},{9,15},{10,... | collective-permute-start | bytes 208904 | tf_op jit(solution)/shard_map/ppermute | solution.py:307
  19.6 1.1 %collective-permute-start.8 = (f16[136,256]{1,0:T(8,128)(2,1)S(1)}, f16[136,256]{1,0:T(8,128)(2,1)S(1)}, u32[]{:S(2)}, u32[]{:S(2)}) collective-permute-start(f16[136,256]{1,0:T(8,128)(2,1)S(1)} %pad_maximum_fusion.2), channel_id=1, source_target_pairs={{0,4},{1,5},{2,6},{3,7},{4,0},{5,1},{6,2},{7,3},{8,12},{9,13},{10,... | collective-permute-start | bytes 208904 | tf_op jit(solution)/shard_map/ppermute | solution.py:307
  20.7 1.5 %collective-permute-start.7 = (f16[136,256]{1,0:T(8,128)(2,1)S(1)}, f16[136,256]{1,0:T(8,128)(2,1)S(1)}, u32[]{:S(2)}, u32[]{:S(2)}) collective-permute-start(f16[136,256]{1,0:T(8,128)(2,1)S(1)} %pad_maximum_fusion.2), channel_id=1, source_target_pairs={{0,2},{1,3},{2,0},{3,1},{4,6},{5,7},{6,4},{7,5},{8,10},{9,11},{10,... | collective-permute-start | bytes 208904 | tf_op jit(solution)/shard_map/ppermute | solution.py:307
  22.2 2.5 %shard_map.116 = (bf16[256,256]{1,0:T(8,128)(2,1)S(1)}, bf16[256,256]{1,0:T(8,128)(2,1)S(1)}, f32[256,256]{1,0:T(8,128)S(1)}, f32[8,256]{1,0:T(8,128)S(1)}) custom-call(bf16[256,256]{1,0:T(8,128)(2,1)S(1)} %get-tuple-element.90.coef_ref), custom_call_target="tpu_custom_call" | custom-call | tf_op jit(solution)/shard_map/pallas_call | solution.py:289
  24.7 0.0 collective-permute-done.9
  24.7 0.0 collective-permute-done.8
  24.7 0.8 %collective-permute-done.7 = f16[136,256]{1,0:T(8,128)(2,1)S(1)} collective-permute-done((f16[136,256]{1,0:T(8,128)(2,1)S(1)}, f16[136,256]{1,0:T(8,128)(2,1)S(1)}, u32[]{:S(2)}, u32[]{:S(2)}) %collective-permute-start.7) | collective-permute-done | bytes 69664 | tf_op jit(solution)/shard_map/ppermute | solution.py:307
  25.6 0.1 multiply_convert_fusion.1
  25.7 2.5 %collective-permute-start.10 = (f16[136,256]{1,0:T(8,128)(2,1)S(1)}, f16[136,256]{1,0:T(8,128)(2,1)S(1)}, u32[]{:S(2)}, u32[]{:S(2)}) collective-permute-start(f16[136,256]{1,0:T(8,128)(2,1)S(1)} %pad_maximum_fusion.3), channel_id=1, source_target_pairs={{0,8},{1,9},{2,10},{3,11},{4,12},{5,13},{6,14},{7,15},{8,0},{9,1},... | collective-permute-start | bytes 208904 | tf_op jit(solution)/shard_map/ppermute | solution.py:307
  28.2 3.5 %shard_map.117 = (f32[256,256]{1,0:T(8,128)S(1)}, f32[512,256]{1,0:T(8,128)S(1)}) custom-call(f32[8,256]{1,0:T(8,128)S(1)} %get-tuple-element.102.gap_in_ref, bf16[256,256]{1,0:T(8,128)(2,1)S(1)} %get-tuple-element.103.high_ref, bf16[256,256]{1,0:T(8,128)(2,1)S(1)} %get-tuple-element.104.low_ref, f32[256,256]{1,0:T(8,128)S(1)} %get-tuple-element.105.inv_in_ref, ...), custom_call_target="tpu_custom_call" | custom-call | tf_op jit(solution)/shard_map/pallas_call | solution.py:289
  31.7 0.1 collective-permute-done.10
  31.9 0.1 collective-permute-start.11
  31.9 1.3 %collective-permute-done.11 = f32[128,256]{1,0:T(8,128)S(1)} collective-permute-done((f32[128,256]{1,0:T(8,128)S(1)}, f32[128,256]{1,0:T(8,128)S(1)}, u32[]{:S(2)}, u32[]{:S(2)}) %collective-permute-start.11) | collective-permute-done | bytes 131104 | tf_op jit(solution)/shard_map/ppermute | solution.py:307
  33.3 2.5 %shard_map.118 = (f32[512,256]{1,0:T(8,128)S(1)}, bf16[512,256]{1,0:T(8,128)(2,1)S(1)}, f32[256,256]{1,0:T(8,128)S(1)}, f32[8,256]{1,0:T(8,128)S(1)}, bf16[256,256]{1,0:T(8,128)(2,1)S(1)}) custom-call(s32[2,12]{1,0:T(2,128)S(1)} %get-tuple-element.71.allrefs_0_.pair_in_ref, s32[8,12]{1,0:T(8,128)S(1)} %get-tuple-element.72.allrefs_1_.stoich_in_ref, ...), custom_call_target="tpu_custom_call" | custom-call | tf_op jit(solution)/shard_map/pallas_call | solution.py:289
  35.9 0.2 collective-permute-start.12
  36.1 1.2 %collective-permute-done.12 = f32[136,256]{1,0:T(8,128)S(1)} collective-permute-done((f32[136,256]{1,0:T(8,128)S(1)}, f32[136,256]{1,0:T(8,128)S(1)}, u32[]{:S(2)}, u32[]{:S(2)}) %collective-permute-start.12) | collective-permute-done | bytes 139296 | tf_op jit(solution)/shard_map/ppermute | solution.py:307
  37.4 1.5 %collective-permute-start.15 = (f16[136,256]{1,0:T(8,128)(2,1)S(1)}, f16[136,256]{1,0:T(8,128)(2,1)S(1)}, u32[]{:S(2)}, u32[]{:S(2)}) collective-permute-start(f16[136,256]{1,0:T(8,128)(2,1)S(1)} %pad_maximum_fusion.4), channel_id=1, source_target_pairs={{0,6},{1,7},{2,4},{3,5},{4,2},{5,3},{6,0},{7,1},{8,14},{9,15},{10,... | collective-permute-start | bytes 208904 | tf_op jit(solution)/shard_map/ppermute | solution.py:307
  38.9 1.0 %collective-permute-start.14 = (f16[136,256]{1,0:T(8,128)(2,1)S(1)}, f16[136,256]{1,0:T(8,128)(2,1)S(1)}, u32[]{:S(2)}, u32[]{:S(2)}) collective-permute-start(f16[136,256]{1,0:T(8,128)(2,1)S(1)} %pad_maximum_fusion.4), channel_id=1, source_target_pairs={{0,4},{1,5},{2,6},{3,7},{4,0},{5,1},{6,2},{7,3},{8,12},{9,13},{10,... | collective-permute-start | bytes 208904 | tf_op jit(solution)/shard_map/ppermute | solution.py:307
  39.9 1.1 %collective-permute-start.13 = (f16[136,256]{1,0:T(8,128)(2,1)S(1)}, f16[136,256]{1,0:T(8,128)(2,1)S(1)}, u32[]{:S(2)}, u32[]{:S(2)}) collective-permute-start(f16[136,256]{1,0:T(8,128)(2,1)S(1)} %pad_maximum_fusion.4), channel_id=1, source_target_pairs={{0,2},{1,3},{2,0},{3,1},{4,6},{5,7},{6,4},{7,5},{8,10},{9,11},{10,... | collective-permute-start | bytes 208904 | tf_op jit(solution)/shard_map/ppermute | solution.py:307
  41.0 2.5 %shard_map.119 = (bf16[256,256]{1,0:T(8,128)(2,1)S(1)}, bf16[256,256]{1,0:T(8,128)(2,1)S(1)}, f32[256,256]{1,0:T(8,128)S(1)}, f32[8,256]{1,0:T(8,128)S(1)}) custom-call(bf16[256,256]{1,0:T(8,128)(2,1)S(1)} %get-tuple-element.116.coef_ref), custom_call_target="tpu_custom_call" | custom-call | tf_op jit(solution)/shard_map/pallas_call | solution.py:289
  43.5 0.0 collective-permute-done.15
  43.5 0.1 collective-permute-done.14
  43.6 0.6 %collective-permute-done.13 = f16[136,256]{1,0:T(8,128)(2,1)S(1)} collective-permute-done((f16[136,256]{1,0:T(8,128)(2,1)S(1)}, f16[136,256]{1,0:T(8,128)(2,1)S(1)}, u32[]{:S(2)}, u32[]{:S(2)}) %collective-permute-start.13) | collective-permute-done | bytes 69664 | tf_op jit(solution)/shard_map/ppermute | solution.py:307
  44.3 0.1 multiply_convert_fusion
  44.4 1.7 %collective-permute-start.16 = (f16[136,256]{1,0:T(8,128)(2,1)S(1)}, f16[136,256]{1,0:T(8,128)(2,1)S(1)}, u32[]{:S(2)}, u32[]{:S(2)}) collective-permute-start(f16[136,256]{1,0:T(8,128)(2,1)S(1)} %pad_maximum_fusion.5), channel_id=1, source_target_pairs={{0,8},{1,9},{2,10},{3,11},{4,12},{5,13},{6,14},{7,15},{8,0},{9,1},... | collective-permute-start | bytes 208904 | tf_op jit(solution)/shard_map/ppermute | solution.py:307
  46.1 3.5 %shard_map.120 = (f32[256,256]{1,0:T(8,128)S(1)}, f32[512,256]{1,0:T(8,128)S(1)}) custom-call(f32[8,256]{1,0:T(8,128)S(1)} %get-tuple-element.128.gap_in_ref, bf16[256,256]{1,0:T(8,128)(2,1)S(1)} %get-tuple-element.129.high_ref, bf16[256,256]{1,0:T(8,128)(2,1)S(1)} %get-tuple-element.130.low_ref, f32[256,256]{1,0:T(8,128)S(1)} %get-tuple-element.131.inv_in_ref, ...), custom_call_target="tpu_custom_call" | custom-call | tf_op jit(solution)/shard_map/pallas_call | solution.py:289
  49.6 0.8 %collective-permute-done.16 = f16[136,256]{1,0:T(8,128)(2,1)S(1)} collective-permute-done((f16[136,256]{1,0:T(8,128)(2,1)S(1)}, f16[136,256]{1,0:T(8,128)(2,1)S(1)}, u32[]{:S(2)}, u32[]{:S(2)}) %collective-permute-start.16) | collective-permute-done | bytes 69664 | tf_op jit(solution)/shard_map/ppermute | solution.py:307
  50.5 0.1 collective-permute-start.17
  50.6 1.3 %collective-permute-done.17 = f32[128,256]{1,0:T(8,128)S(1)} collective-permute-done((f32[128,256]{1,0:T(8,128)S(1)}, f32[128,256]{1,0:T(8,128)S(1)}, u32[]{:S(2)}, u32[]{:S(2)}) %collective-permute-start.17) | collective-permute-done | bytes 131104 | tf_op jit(solution)/shard_map/ppermute | solution.py:307
  51.9 1.6 %shard_map.121 = (f32[512,256]{1,0:T(8,128)}, bf16[16,256]{1,0:T(8,128)(2,1)}) custom-call(f32[512,256]{1,0:T(8,128)S(1)} %get-tuple-element.112.diff_in_ref, f32[512,256]{1,0:T(8,128)S(1)} %get-tuple-element.135.pull_ref, f32[256,256]{1,0:T(8,128)S(1)} %get-tuple-element.136.solve_ref, f32[256,256]{1,0:T(8,128)S(1)} %maximum_select_fusion.1.sum_ref, ...), custom_call_target="tpu_custom_call" | custom-call | tf_op jit(solution)/shard_map/pallas_call | solution.py:289
  (35 shorter events, 0.5 us)
Async XLA Ops:
  0.6 1.6 %copy-start = (bf16[16,256]{1,0:T(8,128)(2,1)S(1)}, bf16[16,256]{1,0:T(8,128)(2,1)}, u32[]{:S(2)}) copy-start(bf16[16,256]{1,0:T(8,128)(2,1)} %param.11) | copy-start | bytes 24580
  0.6 1.6 %collective-permute-start = (bf16[16,256]{1,0:T(8,128)(2,1)}, bf16[16,256]{1,0:T(8,128)(2,1)S(1)}, u32[]{:S(2)}, u32[]{:S(2)}) collective-permute-start(bf16[16,256]{1,0:T(8,128)(2,1)} %param.11), channel_id=1, source_target_pairs={{0,1},{1,0},{2,3},{3,2},{4,5},{5,4},{6,7},{7,6},{8,9},{9,8},{10,11... | collective-permute-start | bytes 24584 | tf_op jit(solution)/shard_map/ppermute | solution.py:307
  2.2 8.1 %collective-permute-start.4 = (bf16[32,256]{1,0:T(8,128)(2,1)S(1)}, bf16[32,256]{1,0:T(8,128)(2,1)S(1)}, u32[]{:S(2)}, u32[]{:S(2)}) collective-permute-start(bf16[32,256]{1,0:T(8,128)(2,1)S(1)} %maximum_select_fusion.2.allrefs_7_), channel_id=1, source_target_pairs={{1,15},{3,13},{5,11},{7,9},{9,7},{11,5},{13,3},{15,1},{17,31},{19,... | collective-permute-start | bytes 49160 | tf_op jit(solution)/shard_map/ppermute | solution.py:307
  2.9 7.5 %collective-permute-start.3 = (bf16[32,256]{1,0:T(8,128)(2,1)S(1)}, bf16[32,256]{1,0:T(8,128)(2,1)S(1)}, u32[]{:S(2)}, u32[]{:S(2)}) collective-permute-start(bf16[32,256]{1,0:T(8,128)(2,1)S(1)} %maximum_select_fusion.2.allrefs_7_), channel_id=1, source_target_pairs={{0,10},{1,13},{2,8},{3,15},{4,14},{5,9},{6,12},{7,11},{8,2},{9,5},... | collective-permute-start | bytes 49160 | tf_op jit(solution)/shard_map/ppermute | solution.py:307
  7.8 4.6 %collective-permute-start.2 = (bf16[32,256]{1,0:T(8,128)(2,1)S(1)}, bf16[32,256]{1,0:T(8,128)(2,1)S(1)}, u32[]{:S(2)}, u32[]{:S(2)}) collective-permute-start(bf16[32,256]{1,0:T(8,128)(2,1)S(1)} %maximum_select_fusion.2.allrefs_7_), channel_id=1, source_target_pairs={{0,8},{1,7},{2,10},{3,5},{4,12},{5,3},{6,14},{7,1},{8,0},{9,15},{1... | collective-permute-start | bytes 49160 | tf_op jit(solution)/shard_map/ppermute | solution.py:307
  8.2 4.3 %collective-permute-start.1 = (bf16[32,256]{1,0:T(8,128)(2,1)S(1)}, bf16[32,256]{1,0:T(8,128)(2,1)S(1)}, u32[]{:S(2)}, u32[]{:S(2)}) collective-permute-start(bf16[32,256]{1,0:T(8,128)(2,1)S(1)} %maximum_select_fusion.2.allrefs_7_), channel_id=1, source_target_pairs={{0,2},{1,5},{2,0},{3,7},{4,6},{5,1},{6,4},{7,3},{8,10},{9,13},{10,... | collective-permute-start | bytes 49160 | tf_op jit(solution)/shard_map/ppermute | solution.py:307
  12.5 2.9 %collective-permute-start.5 = (bf16[128,256]{1,0:T(8,128)(2,1)S(1)}, bf16[128,256]{1,0:T(8,128)(2,1)S(1)}, u32[]{:S(2)}, u32[]{:S(2)}) collective-permute-start(bf16[128,256]{1,0:T(8,128)(2,1)S(1)} %constant_dynamic-update-slice_fusion.allrefs_8_), channel_id=1, source_target_pairs={{0,1},{1,0},{2,3},{3,2},{4,5},{5,4},{6,7},{7,6},{8,9},{9,8},{10,11... | collective-permute-start | bytes 196616 | tf_op jit(solution)/shard_map/ppermute | solution.py:307
  17.1 1.4 %collective-permute-start.6 = (f32[136,256]{1,0:T(8,128)S(1)}, f32[136,256]{1,0:T(8,128)S(1)}, u32[]{:S(2)}, u32[]{:S(2)}) collective-permute-start(f32[136,256]{1,0:T(8,128)S(1)} %pad_maximum_fusion), channel_id=1, source_target_pairs={{0,1},{1,0},{2,3},{3,2},{4,5},{5,4},{6,7},{7,6},{8,9},{9,8},{10,11... | collective-permute-start | bytes 417800 | tf_op jit(solution)/shard_map/ppermute | solution.py:307
  18.6 6.1 %collective-permute-start.9 = (f16[136,256]{1,0:T(8,128)(2,1)S(1)}, f16[136,256]{1,0:T(8,128)(2,1)S(1)}, u32[]{:S(2)}, u32[]{:S(2)}) collective-permute-start(f16[136,256]{1,0:T(8,128)(2,1)S(1)} %pad_maximum_fusion.2), channel_id=1, source_target_pairs={{0,6},{1,7},{2,4},{3,5},{4,2},{5,3},{6,0},{7,1},{8,14},{9,15},{10,... | collective-permute-start | bytes 208904 | tf_op jit(solution)/shard_map/ppermute | solution.py:307
  19.6 5.1 %collective-permute-start.8 = (f16[136,256]{1,0:T(8,128)(2,1)S(1)}, f16[136,256]{1,0:T(8,128)(2,1)S(1)}, u32[]{:S(2)}, u32[]{:S(2)}) collective-permute-start(f16[136,256]{1,0:T(8,128)(2,1)S(1)} %pad_maximum_fusion.2), channel_id=1, source_target_pairs={{0,4},{1,5},{2,6},{3,7},{4,0},{5,1},{6,2},{7,3},{8,12},{9,13},{10,... | collective-permute-start | bytes 208904 | tf_op jit(solution)/shard_map/ppermute | solution.py:307
  20.7 4.8 %collective-permute-start.7 = (f16[136,256]{1,0:T(8,128)(2,1)S(1)}, f16[136,256]{1,0:T(8,128)(2,1)S(1)}, u32[]{:S(2)}, u32[]{:S(2)}) collective-permute-start(f16[136,256]{1,0:T(8,128)(2,1)S(1)} %pad_maximum_fusion.2), channel_id=1, source_target_pairs={{0,2},{1,3},{2,0},{3,1},{4,6},{5,7},{6,4},{7,5},{8,10},{9,11},{10,... | collective-permute-start | bytes 208904 | tf_op jit(solution)/shard_map/ppermute | solution.py:307
  25.7 6.1 %collective-permute-start.10 = (f16[136,256]{1,0:T(8,128)(2,1)S(1)}, f16[136,256]{1,0:T(8,128)(2,1)S(1)}, u32[]{:S(2)}, u32[]{:S(2)}) collective-permute-start(f16[136,256]{1,0:T(8,128)(2,1)S(1)} %pad_maximum_fusion.3), channel_id=1, source_target_pairs={{0,8},{1,9},{2,10},{3,11},{4,12},{5,13},{6,14},{7,15},{8,0},{9,1},... | collective-permute-start | bytes 208904 | tf_op jit(solution)/shard_map/ppermute | solution.py:307
  31.9 1.4 %collective-permute-start.11 = (f32[128,256]{1,0:T(8,128)S(1)}, f32[128,256]{1,0:T(8,128)S(1)}, u32[]{:S(2)}, u32[]{:S(2)}) collective-permute-start(f32[128,256]{1,0:T(8,128)S(1)} %multiply_add_fusion.1), channel_id=1, source_target_pairs={{0,1},{1,0},{2,3},{3,2},{4,5},{5,4},{6,7},{7,6},{8,9},{9,8},{10,11... | collective-permute-start | bytes 393224 | tf_op jit(solution)/shard_map/ppermute | solution.py:307
  35.9 1.4 %collective-permute-start.12 = (f32[136,256]{1,0:T(8,128)S(1)}, f32[136,256]{1,0:T(8,128)S(1)}, u32[]{:S(2)}, u32[]{:S(2)}) collective-permute-start(f32[136,256]{1,0:T(8,128)S(1)} %pad_maximum_fusion.1), channel_id=1, source_target_pairs={{0,1},{1,0},{2,3},{3,2},{4,5},{5,4},{6,7},{7,6},{8,9},{9,8},{10,11... | collective-permute-start | bytes 417800 | tf_op jit(solution)/shard_map/ppermute | solution.py:307
  37.4 6.1 %collective-permute-start.15 = (f16[136,256]{1,0:T(8,128)(2,1)S(1)}, f16[136,256]{1,0:T(8,128)(2,1)S(1)}, u32[]{:S(2)}, u32[]{:S(2)}) collective-permute-start(f16[136,256]{1,0:T(8,128)(2,1)S(1)} %pad_maximum_fusion.4), channel_id=1, source_target_pairs={{0,6},{1,7},{2,4},{3,5},{4,2},{5,3},{6,0},{7,1},{8,14},{9,15},{10,... | collective-permute-start | bytes 208904 | tf_op jit(solution)/shard_map/ppermute | solution.py:307
  38.9 4.7 %collective-permute-start.14 = (f16[136,256]{1,0:T(8,128)(2,1)S(1)}, f16[136,256]{1,0:T(8,128)(2,1)S(1)}, u32[]{:S(2)}, u32[]{:S(2)}) collective-permute-start(f16[136,256]{1,0:T(8,128)(2,1)S(1)} %pad_maximum_fusion.4), channel_id=1, source_target_pairs={{0,4},{1,5},{2,6},{3,7},{4,0},{5,1},{6,2},{7,3},{8,12},{9,13},{10,... | collective-permute-start | bytes 208904 | tf_op jit(solution)/shard_map/ppermute | solution.py:307
  39.9 4.3 %collective-permute-start.13 = (f16[136,256]{1,0:T(8,128)(2,1)S(1)}, f16[136,256]{1,0:T(8,128)(2,1)S(1)}, u32[]{:S(2)}, u32[]{:S(2)}) collective-permute-start(f16[136,256]{1,0:T(8,128)(2,1)S(1)} %pad_maximum_fusion.4), channel_id=1, source_target_pairs={{0,2},{1,3},{2,0},{3,1},{4,6},{5,7},{6,4},{7,5},{8,10},{9,11},{10,... | collective-permute-start | bytes 208904 | tf_op jit(solution)/shard_map/ppermute | solution.py:307
  44.4 6.0 %collective-permute-start.16 = (f16[136,256]{1,0:T(8,128)(2,1)S(1)}, f16[136,256]{1,0:T(8,128)(2,1)S(1)}, u32[]{:S(2)}, u32[]{:S(2)}) collective-permute-start(f16[136,256]{1,0:T(8,128)(2,1)S(1)} %pad_maximum_fusion.5), channel_id=1, source_target_pairs={{0,8},{1,9},{2,10},{3,11},{4,12},{5,13},{6,14},{7,15},{8,0},{9,1},... | collective-permute-start | bytes 208904 | tf_op jit(solution)/shard_map/ppermute | solution.py:307
  50.5 1.4 %collective-permute-start.17 = (f32[128,256]{1,0:T(8,128)S(1)}, f32[128,256]{1,0:T(8,128)S(1)}, u32[]{:S(2)}, u32[]{:S(2)}) collective-permute-start(f32[128,256]{1,0:T(8,128)S(1)} %multiply_add_fusion), channel_id=1, source_target_pairs={{0,1},{1,0},{2,3},{3,2},{4,5},{5,4},{6,7},{7,6},{8,9},{9,8},{10,11... | collective-permute-start | bytes 393224 | tf_op jit(solution)/shard_map/ppermute | solution.py:307

commit v6 on v5

--- a/solution.py
+++ b/solution.py
@@ -66,51 +66,58 @@
 
 
 def react(
-    diffused, coef_ref, emis_ref, live_ref, ready, pair_ref, stoich_ref, speed_ref, loss_ref,
-    field_ref, tend_ref, rate_ref, top_ref, columns,
+    diffused, base, coef_ref, emis_ref, live_ref, ready, pair_ref, stoich_ref, speed_ref, loss_ref,
+    field_ref, tend_ref, rate_ref, top_ref,
 ):
     mode_bf = diffused.astype(BF16)
-    members = coef_ref.shape[0]
-    block = math.gcd(members, 256)
+    members = tend_ref.shape[1]
+    block = field_ref.shape[1]
+    columns = diffused.shape[0] // (S * LEV)
     step = 16
     steps = LEV // step
     largest = jnp.full((1, R), 2.0**-120, F32)
     for b in range(members // block):
         lanes = slice(b * block, (b + 1) * block)
-        field_ref[...] = mm(mode_bf, coef_ref[lanes, :], NT) * (1.0 / math.sqrt(R))
+        spot = pl.ds(pl.multiple_of(base + b * block, block), block)
+        field_ref[...] = mm(mode_bf, coef_ref[spot, :], NT) * (1.0 / math.sqrt(R))
         if b == 0:
             ready()
 
         def part(i, _):
             c = i // steps
             low = (i - c * steps) * step
-            base = c * (S * LEV) + low
+            first = c * (S * LEV) + low
             level = lax.broadcasted_iota(jnp.int32, (step, block), 0) + low
             profile = jnp.exp(level.astype(F32) * (-4.0 / LEV))
             live = live_ref[pl.ds(pl.multiple_of(c * LEV + low, step), step), 0:block] > 0.5
 
             def amount(s):
-                return field_ref[pl.ds(pl.multiple_of(base + s * LEV, step), step), :]
+                return field_ref[pl.ds(pl.multiple_of(first + s * LEV, step), step), :]
 
             total = []
             for s in range(S):
-                total.append(emis_ref[s : s + 1, lanes] * profile - loss_ref[0, s] * amount(s))
+                total.append(emis_ref[s : s + 1, spot] * profile - loss_ref[0, s] * amount(s))
             for r in range(NREAC):
                 speed = speed_ref[0, r] * amount(pair_ref[0, r]) * amount(pair_ref[1, r])
                 for s in range(S):
                     total[s] = total[s] + stoich_ref[s, r].astype(F32) * speed
             for s in range(S):
-                tend_ref[pl.ds(pl.multiple_of(base + s * LEV, step), step), lanes] = jnp.where(
+                tend_ref[pl.ds(pl.multiple_of(first + s * LEV, step), step), lanes] = jnp.where(
                     live, total[s], 0.0
                 ).astype(BF16)
             return 0
 
-        lax.fori_loop(0, columns * steps, part, 0)
+        lax.fori_loop(0, columns * steps, part, 0, unroll=members <= block)
         rate = mm(tend_ref[:, lanes], mode_bf, TN)
         rate_ref[lanes, :] = rate
         largest = jnp.maximum(largest, jnp.max(jnp.abs(rate), axis=0, keepdims=True))
     power = jnp.maximum(jnp.floor(jnp.log(largest) * (1.0 / math.log(2.0))) + 2.0, -100.0)
     top_ref[...] = jnp.broadcast_to(power, top_ref.shape)
+
+
+def half_start(members, keep):
+    side = lax.axis_index("col") & 1
+    return (side if keep else 1 - side) * members
 
 
 def stage_kernel(
@@ -151,10 +158,7 @@
     diff_ref[...] = diffuse_rows(modes_ref[...], face_ref)
 
 
-def first_kernel(
-    columns, plan,
-    *allrefs,
-):
+def first_kernel(plan, *allrefs):
     chem_in, chem, sems = allrefs[:4], allrefs[-5:-1], allrefs[-1]
     diff_ref, emis_ref, live_ref, *refs, field_ref = allrefs[4:-5]
     ready = fetch(chem_in, chem, sems)
@@ -174,24 +178,48 @@
     else:
         coef_ref, tend_ref, rate_ref, top_ref = refs
     react(
-        diff_ref[...], coef_ref, emis_ref, live_ref, ready, *chem,
-        field_ref, tend_ref, rate_ref, top_ref, columns,
-    )
-
-
-def transfer_of(solve_ref, rate):
-    return split(mm3(split(rate), split(solve_ref[...]), TN))
-
-
-def advance(diffused, pull, transfer):
-    moved = mm3(split(diffused), transfer)
-    return diffused + (TIME_STEP * math.sqrt(R)) * (pull - moved)
+        diff_ref[...], half_start(tend_ref.shape[1], False), coef_ref, emis_ref, live_ref,
+        ready, *chem, field_ref, tend_ref, rate_ref, top_ref,
+    )
+
+
+def second_kernel(
+    pair_in_ref, stoich_in_ref, speed_in_ref, loss_in_ref,
+    diff_ref, emis_ref, live_ref, coef_ref,
+    tend_ref, rate_ref, top_ref,
+    field_ref, *chem_sems,
+):
+    *chem, sems = chem_sems
+    ready = fetch((pair_in_ref, stoich_in_ref, speed_in_ref, loss_in_ref), chem, sems)
+    react(
+        diff_ref[...], half_start(tend_ref.shape[1], True), coef_ref, emis_ref, live_ref,
+        ready, *chem, field_ref, tend_ref, rate_ref, top_ref,
+    )
+
+
+STEP = TIME_STEP * math.sqrt(R)
+
+
+def ready_kernel(
+    diff_ref, pull_ref, solve_ref, base_ref, diff_high_ref, diff_low_ref, high_ref, low_ref
+):
+    diffused = diff_ref[...]
+    base_ref[...] = diffused + STEP * pull_ref[...]
+    diff_high_ref[...], diff_low_ref[...] = split(diffused)
+    high_ref[...], low_ref[...] = split(solve_ref[...])
+
+
+def advance(base_ref, diff_high_ref, diff_low_ref, high_ref, low_ref, rate):
+    transfer = mm3(split(rate), (high_ref[...], low_ref[...]), TN)
+    moved = mm3((diff_high_ref[...], diff_low_ref[...]), split(transfer))
+    return base_ref[...] - STEP * moved
 
 
 def middle_kernel(
-    columns, total_rows,
+    total_rows,
     pair_in_ref, stoich_in_ref, speed_in_ref, loss_in_ref,
-    diff_in_ref, pull_ref, solve_ref, sum_ref, coef_ref, face_ref, emis_ref, live_ref,
+    base_ref, diff_high_ref, diff_low_ref, high_ref, low_ref,
+    sum_ref, coef_ref, face_ref, emis_ref, live_ref,
     diff_ref, tend_ref, rate_ref, top_ref, coef_out_ref,
     field_ref, *chem_sems,
 ):
@@ -201,19 +229,21 @@
     coef_out_ref[...] = (
         coef_ref[...].astype(F32) + RATE_STEP * (raw * (math.sqrt(R) / total_rows))
     ).astype(BF16)
-    transfer = transfer_of(solve_ref, raw * (1.0 / total_rows))
-    modes = advance(diff_in_ref[...], pull_ref[...], transfer)
+    modes = advance(
+        base_ref, diff_high_ref, diff_low_ref, high_ref, low_ref, raw * (1.0 / total_rows)
+    )
     diffused = diffuse_rows(modes, face_ref)
     diff_ref[...] = diffused
     react(
-        diffused, coef_out_ref, emis_ref, live_ref, ready, *chem,
-        field_ref, tend_ref, rate_ref, top_ref, columns,
+        diffused, half_start(tend_ref.shape[1], False), coef_out_ref, emis_ref, live_ref,
+        ready, *chem, field_ref, tend_ref, rate_ref, top_ref,
     )
 
 
 def last_kernel(
     total_rows,
-    diff_in_ref, pull_ref, solve_ref, sum_ref, coef_ref,
+    base_ref, diff_high_ref, diff_low_ref, high_ref, low_ref,
+    sum_ref, coef_ref,
     modes_ref, coef_out_ref,
 ):
     mine = coef_out_ref.shape[0]
@@ -222,8 +252,10 @@
         coef_ref[own, :].astype(F32)
         + RATE_STEP * (sum_ref[own, :] * (math.sqrt(R) / total_rows))
     ).astype(BF16)
-    transfer = transfer_of(solve_ref, sum_ref[...] * (1.0 / total_rows))
-    modes_ref[...] = advance(diff_in_ref[...], pull_ref[...], transfer)
+    modes_ref[...] = advance(
+        base_ref, diff_high_ref, diff_low_ref, high_ref, low_ref,
+        sum_ref[...] * (1.0 / total_rows),
+    )
 
 
 def identity():
@@ -261,7 +293,8 @@
 
 
 def inverse_end(
-    gap_in_ref, high_ref, low_ref, inv_in_ref, coef_ref, tend_ref, solve_ref, pull_ref, inv_ref
+    gap_in_ref, high_ref, low_ref, inv_in_ref, coef_ref, give_ref, keep_ref,
+    solve_ref, pull_ref, inv_ref,
 ):
     eye = identity()
     inv_ref[...] = inv_in_ref[...]
@@ -274,8 +307,13 @@
     high, low = split(inv_ref[...])
     solve = mm(coef, high) + mm(coef, low)
     solve_ref[...] = solve
-    high, low = split(solve)
-    pull_ref[...] = mm(tend_ref[...], high) + mm(tend_ref[...], low)
+    half = give_ref.shape[1]
+    parts = []
+    for ref, keep in ((give_ref, False), (keep_ref, True)):
+        start = pl.multiple_of(half_start(half, keep), half)
+        high, low = split(solve_ref[pl.ds(start, half), :])
+        parts.append(mm(ref[...], high) + mm(ref[...], low))
+    pull_ref[...] = parts[0] + parts[1]
 
 
 VMEM_LIMIT = 48 * 1024 * 1024
@@ -323,20 +361,15 @@
     return message[:rows].astype(F32) * jnp.exp2(power - LIFT), power
 
 
-def sum_over(x, top, n, work):
-    state = ()
+def sum_over(give, top, keep_half, n, work, prepare):
+    got = swap(jnp.concatenate([give, top], 0), n, (1, 1))
+    keep, keep_top, state = keep_half()
+    got, keep = lax.optimization_barrier((got, keep))
+    half = give.shape[0]
+    side = lax.axis_index("col") & 1
+    part = keep + got[:half]
+    power = jnp.maximum(keep_top[:1], got[half : half + 1]) + 1.0
     work = list(work)
-    if n & (n - 1) or n < 4:
-        while work:
-            state = work.pop(0)(state, x)
-        return lax.psum(x, "col"), state
-    half = x.shape[0] // 2
-    side = lax.axis_index("col") & 1
-    keep = lax.dynamic_slice_in_dim(x, side * half, half, 0)
-    give = lax.dynamic_slice_in_dim(x, (1 - side) * half, half, 0)
-    got = swap(jnp.concatenate([give, top], 0), n, (1, 1))
-    part = keep + got[:half]
-    power = jnp.maximum(top[:1], got[half : half + 1]) + 1.0
     mask = 2
     while mask < n:
         masks = [mask, mask * 2, mask * 3] if mask * 2 < n else [mask]
@@ -355,6 +388,8 @@
             power = jnp.maximum(power, high)
         power = power + float(len(masks))
     other = swap(part, n, (1, 1))
+    state = prepare(state, part)
+    other, state = lax.optimization_barrier((other, state))
     total = jnp.where(
         side == 0, jnp.concatenate([part, other], 0), jnp.concatenate([other, part], 0)
     )
@@ -380,9 +415,12 @@
     members = mine * n
     columns = counts.shape[0]
     ridge = RIDGE_SHARE * members
-    block = math.gcd(members, 256)
+    half = members // 2
+    block = math.gcd(half, 256)
     rows_f32 = ((rows, R), F32)
-    tend_out = ((rows, members), BF16)
+    rows_bf = ((rows, R), BF16)
+    tend_out = ((rows, half), BF16)
+    half_out = ((half, R), F32)
     rate_out = ((members, R), F32)
     top_out = ((EXTRA, R), F32)
     coef_out = ((members, R), BF16)
@@ -431,8 +469,8 @@
         theirs, diff = lax.optimization_barrier((theirs, diff))
         gathered = (chip, mine_rows, theirs)
         tend, rate, top, coef = call(
-            functools.partial(first_kernel, columns, plan), 0,
-            [tend_out, rate_out, top_out, coef_out], react_tmp,
+            functools.partial(first_kernel, plan), 0,
+            [tend_out, half_out, top_out, coef_out], react_tmp,
             *chem, diff, emis, live, *gathered,
         )
     else:
@@ -440,39 +478,55 @@
         chem, modes, emis, face, live = stage(mode_rows)
         diff = spread(modes, face)
         tend, rate, top = call(
-            functools.partial(first_kernel, columns, ()), 0,
-            [tend_out, rate_out, top_out], react_tmp,
+            functools.partial(first_kernel, ()), 0,
+            [tend_out, half_out, top_out], react_tmp,
             *chem, diff, emis, live, coef,
         )
 
-    def summed(rate, top, coef, tend):
-        def start(state, ready):
-            return call(
-                functools.partial(inverse_start, ridge, 3), 0,
+    def summed(rate, top, coef, tend, diff):
+        def keep_half():
+            tend_keep, keep, keep_top = call(
+                second_kernel, 0, [tend_out, half_out, top_out], react_tmp,
+                *chem, tied(diff, rate), emis, live, coef,
+            )
+            return keep, keep_top, tend_keep
+
+        def start(tend_keep, ready):
+            return tend_keep, call(
+                functools.partial(inverse_start, ridge, 4), 0,
                 [square_bf, square_bf, square, top_out], [], tied(coef, ready),
             )
 
         def end(state, ready):
-            high, low, inv, gap = tied(state, ready)
+            tend_keep, (high, low, inv, gap) = tied(state, ready)
             return call(
-                inverse_end, 0, [rate_out, rows_f32], [pltpu.VMEM((R, R), F32)], gap, high, low, inv, coef, tend
+                inverse_end, 0, [rate_out, rows_f32], [pltpu.VMEM((R, R), F32)],
+                gap, high, low, inv, coef, tend, tend_keep,
             )
 
-        return sum_over(rate, top, n, (start, end))
+        def prepare(state, ready):
+            solved, pull = tied(state, ready)
+            return call(
+                ready_kernel, 0,
+                [rows_f32, rows_bf, rows_bf, ((members, R), BF16), ((members, R), BF16)], [],
+                diff, pull, solved,
+            )
+
+        return sum_over(rate, top, keep_half, n, (start, end), prepare)
 
     for _ in range(NSUB - 1):
-        total, (solved, pull) = summed(rate, top, coef, tend)
+        total, prepared = summed(rate, top, coef, tend, diff)
         diff, tend, rate, top, coef = call(
-            functools.partial(middle_kernel, columns, total_rows), 0,
-            [rows_f32, tend_out, rate_out, top_out, coef_out], react_tmp,
-            *chem, diff, pull, solved, total, coef, face, emis, live,
+            functools.partial(middle_kernel, total_rows), 0,
+            [rows_f32, tend_out, half_out, top_out, coef_out], react_tmp,
+            *chem, *prepared, total, coef, face, emis, live,
         )
-    total, (solved, pull) = summed(rate, top, coef, tend)
+    total, prepared = summed(rate, top, coef, tend, diff)
     return tuple(
         call(
             functools.partial(last_kernel, total_rows), 0,
             [rows_f32, ((mine, R), BF16)], [],
-            diff, pull, solved, total, coef,
+            *prepared, total, coef,
         )
     )
 

time: 53.7 us -> 53.1 us (0.989)
  waiting for transfers between devices: 11.3 us -> 8.01 us
  Pallas kernels: 19.2 us -> 21.6 us
    ppermute x18, waiting for transfers between devices: 11.3 us -> 8.01 us  [swap(): lax.ppermute(value, 'col', [(i, i ^ masks[i % 2]) for i in range(n) if ma...]
    pallas_call x9 -> x13, Pallas kernels: 19.2 us -> 21.6 us  [call(): pl.pallas_call(kernel, in_specs=[pl.BlockSpec(memory_space=pltpu.HBM if i...]
  transfers between devices with their start and end apart: 18 -> 18, of which waited for: 12 -> 8; matrix products, arithmetic and copies ran while one was open for 0% -> 0% of each run, Pallas kernels for 25% -> 31%
where the time goes in v6:
time: 53.1 us; the launch traced here: 53 us
  Pallas kernels  21.6 us (41%)
  starting transfers between devices  21.1 us (40%)
  waiting for transfers between devices  8.01 us (15%)
  between operations  1.64 us (3%)
  other arithmetic  0.58 us (1%)
    pallas_call x13, Pallas kernels, call(): pl.pallas_call(kernel, in_specs=[pl.BlockSpec(memory_space=pltpu.HBM if i...  21.6 us
    ppermute x18, starting transfers between devices, swap(): lax.ppermute(value, 'col', [(i, i ^ masks[i % 2]) for i in range(n) if ma...  21.1 us
    ppermute x18, waiting for transfers between devices, swap(): lax.ppermute(value, 'col', [(i, i ^ masks[i % 2]) for i in range(n) if ma...  8.01 us
  transfers between devices with their start and end apart: 18, of which 8 were waited for; matrix products, arithmetic and copies ran while one was open for 0% of the time, Pallas kernels for 31%

profile of v6, /device:TPU:0, one launch (start us, length us, event | category | flops | bytes accessed | tf_op | source)
XLA Modules:
  0.0 53.0 jit_solution(10175927241408339811)
XLA Ops:
  0.6 0.0 copy-start
  0.6 0.5 collective-permute-start
  1.2 1.0 %collective-permute-done = bf16[16,256]{1,0:T(8,128)(2,1)S(1)} collective-permute-done((bf16[16,256]{1,0:T(8,128)(2,1)}, bf16[16,256]{1,0:T(8,128)(2,1)S(1)}, u32[]{:S(2)}, u32[]{:S(2)}) %collective-permute-start) | collective-permute-done | bytes 8224 | tf_op jit(solution)/shard_map/ppermute | solution.py:345
  2.2 0.0 copy-done
  2.2 0.7 %collective-permute-start.4 = (bf16[32,256]{1,0:T(8,128)(2,1)S(1)}, bf16[32,256]{1,0:T(8,128)(2,1)S(1)}, u32[]{:S(2)}, u32[]{:S(2)}) collective-permute-start(bf16[32,256]{1,0:T(8,128)(2,1)S(1)} %maximum_select_fusion.2.allrefs_7_), channel_id=1, source_target_pairs={{1,15},{3,13},{5,11},{7,9},{9,7},{11,5},{13,3},{15,1},{17,31},{19,... | collective-permute-start | bytes 49160 | tf_op jit(solution)/shard_map/ppermute | solution.py:345
  2.9 5.0 %collective-permute-start.3 = (bf16[32,256]{1,0:T(8,128)(2,1)S(1)}, bf16[32,256]{1,0:T(8,128)(2,1)S(1)}, u32[]{:S(2)}, u32[]{:S(2)}) collective-permute-start(bf16[32,256]{1,0:T(8,128)(2,1)S(1)} %maximum_select_fusion.2.allrefs_7_), channel_id=1, source_target_pairs={{0,10},{1,13},{2,8},{3,15},{4,14},{5,9},{6,12},{7,11},{8,2},{9,5},... | collective-permute-start | bytes 49160 | tf_op jit(solution)/shard_map/ppermute | solution.py:345
  7.8 0.3 collective-permute-start.2
  8.2 0.3 collective-permute-start.1
  9.1 1.2 %shard_map.113 = (s32[2,12]{1,0:T(2,128)S(1)}, s32[8,12]{1,0:T(8,128)S(1)}, f32[1,12]{1,0:T(1,128)S(1)}, f32[1,8]{1,0:T(1,128)S(1)}, f32[512,256]{1,0:T(8,128)S(...) custom-call(s32[2,12]{1,0:T(2,128)} %bitcast.42, s32[8,12]{1,0:T(8,128)} %bitcast.24, ...), custom_call_target="tpu_custom_call" | custom-call | tf_op jit(solution)/shard_map/pallas_call | solution.py:327
  10.3 0.0 collective-permute-done.4
  10.3 0.0 collective-permute-done.3
  10.3 2.1 %collective-permute-done.2 = bf16[32,256]{1,0:T(8,128)(2,1)S(1)} collective-permute-done((bf16[32,256]{1,0:T(8,128)(2,1)S(1)}, bf16[32,256]{1,0:T(8,128)(2,1)S(1)}, u32[]{:S(2)}, u32[]{:S(2)}) %collective-permute-start.2) | collective-permute-done | bytes 16416 | tf_op jit(solution)/shard_map/ppermute | solution.py:345
  12.5 0.0 collective-permute-done.1
  12.5 2.0 %collective-permute-start.5 = (bf16[128,256]{1,0:T(8,128)(2,1)S(1)}, bf16[128,256]{1,0:T(8,128)(2,1)S(1)}, u32[]{:S(2)}, u32[]{:S(2)}) collective-permute-start(bf16[128,256]{1,0:T(8,128)(2,1)S(1)} %constant_dynamic-update-slice_fusion.allrefs_8_), channel_id=1, source_target_pairs={{0,1},{1,0},{2,3},{3,2},{4,5},{5,4},{6,7},{7,6},{8,9},{9,8},{10,11... | collective-permute-start | bytes 196616 | tf_op jit(solution)/shard_map/ppermute | solution.py:345
  14.5 0.1 shard_map.114.allrefs_4_.diff_ref
  14.6 0.8 %collective-permute-done.5.allrefs_9_ = bf16[128,256]{1,0:T(8,128)(2,1)S(1)} collective-permute-done((bf16[128,256]{1,0:T(8,128)(2,1)S(1)}, bf16[128,256]{1,0:T(8,128)(2,1)S(1)}, u32[]{:S(2)}, u32[]{:S(2)}) %collective-permute-start.5) | collective-permute-done | bytes 65568 | tf_op jit(solution)/shard_map/ppermute | solution.py:345
  15.4 1.3 %shard_map.115 = (bf16[512,128]{1,0:T(8,128)(2,1)S(1)}, f32[128,256]{1,0:T(8,128)S(1)}, f32[8,256]{1,0:T(8,128)S(1)}, bf16[256,256]{1,0:T(8,128)(2,1)S(1)}) custom-call(s32[2,12]{1,0:T(2,128)S(1)} %get-tuple-element.113.allrefs_0_.pair_in_ref, s32[8,12]{1,0:T(8,128)S(1)} %get-tuple-element.114.allrefs_1_.stoich_in_ref, ...), custom_call_target="tpu_custom_call" | custom-call | tf_op jit(solution)/shard_map/pallas_call | solution.py:327
  16.7 0.4 collective-permute-start.6
  17.1 1.3 %shard_map.116 = (bf16[512,128]{1,0:T(8,128)(2,1)S(1)}, f32[128,256]{1,0:T(8,128)S(1)}, f32[8,256]{1,0:T(8,128)S(1)}) custom-call(s32[2,12]{1,0:T(2,128)S(1)} %get-tuple-element.113.allrefs_0_.pair_in_ref, s32[8,12]{1,0:T(8,128)S(1)} %get-tuple-element.114.allrefs_1_.stoich_in_ref, f32[1,12]{1,0:T(1,128)S(1)} %get-tuple-element.115.allrefs_2_.speed_in_ref, ...), custom_call_target="tpu_custom_call" | custom-call | tf_op jit(solution)/shard_map/pallas_call | solution.py:327
  18.3 0.0 collective-permute-done.6
  18.5 1.0 %collective-permute-start.9 = (f16[136,256]{1,0:T(8,128)(2,1)S(1)}, f16[136,256]{1,0:T(8,128)(2,1)S(1)}, u32[]{:S(2)}, u32[]{:S(2)}) collective-permute-start(f16[136,256]{1,0:T(8,128)(2,1)S(1)} %pad_maximum_fusion.2), channel_id=1, source_target_pairs={{0,6},{1,7},{2,4},{3,5},{4,2},{5,3},{6,0},{7,1},{8,14},{9,15},{10,... | collective-permute-start | bytes 208904 | tf_op jit(solution)/shard_map/ppermute | solution.py:345
  19.4 1.1 %collective-permute-start.8 = (f16[136,256]{1,0:T(8,128)(2,1)S(1)}, f16[136,256]{1,0:T(8,128)(2,1)S(1)}, u32[]{:S(2)}, u32[]{:S(2)}) collective-permute-start(f16[136,256]{1,0:T(8,128)(2,1)S(1)} %pad_maximum_fusion.2), channel_id=1, source_target_pairs={{0,4},{1,5},{2,6},{3,7},{4,0},{5,1},{6,2},{7,3},{8,12},{9,13},{10,... | collective-permute-start | bytes 208904 | tf_op jit(solution)/shard_map/ppermute | solution.py:345
  20.5 1.5 %collective-permute-start.7 = (f16[136,256]{1,0:T(8,128)(2,1)S(1)}, f16[136,256]{1,0:T(8,128)(2,1)S(1)}, u32[]{:S(2)}, u32[]{:S(2)}) collective-permute-start(f16[136,256]{1,0:T(8,128)(2,1)S(1)} %pad_maximum_fusion.2), channel_id=1, source_target_pairs={{0,2},{1,3},{2,0},{3,1},{4,6},{5,7},{6,4},{7,5},{8,10},{9,11},{10,... | collective-permute-start | bytes 208904 | tf_op jit(solution)/shard_map/ppermute | solution.py:345
  22.0 3.2 %shard_map.117 = (bf16[256,256]{1,0:T(8,128)(2,1)S(1)}, bf16[256,256]{1,0:T(8,128)(2,1)S(1)}, f32[256,256]{1,0:T(8,128)S(1)}, f32[8,256]{1,0:T(8,128)S(1)}) custom-call(bf16[256,256]{1,0:T(8,128)(2,1)S(1)} %get-tuple-element.138.coef_ref), custom_call_target="tpu_custom_call" | custom-call | tf_op jit(solution)/shard_map/pallas_call | solution.py:327
  25.2 0.0 collective-permute-done.9
  25.2 0.0 collective-permute-done.8
  25.2 0.0 collective-permute-done.7
  25.3 0.1 multiply_convert_fusion.2
  25.4 2.6 %collective-permute-start.10 = (f16[136,256]{1,0:T(8,128)(2,1)S(1)}, f16[136,256]{1,0:T(8,128)(2,1)S(1)}, u32[]{:S(2)}, u32[]{:S(2)}) collective-permute-start(f16[136,256]{1,0:T(8,128)(2,1)S(1)} %pad_maximum_fusion.3), channel_id=1, source_target_pairs={{0,8},{1,9},{2,10},{3,11},{4,12},{5,13},{6,14},{7,15},{8,0},{9,1},... | collective-permute-start | bytes 208904 | tf_op jit(solution)/shard_map/ppermute | solution.py:345
  28.0 3.0 %shard_map.118 = (f32[256,256]{1,0:T(8,128)S(1)}, f32[512,256]{1,0:T(8,128)S(1)}) custom-call(f32[8,256]{1,0:T(8,128)S(1)} %get-tuple-element.151.gap_in_ref, bf16[256,256]{1,0:T(8,128)(2,1)S(1)} %get-tuple-element.152.high_ref, bf16[256,256]{1,0:T(8,128)(2,1)S(1)} %get-tuple-element.153.low_ref, f32[256,256]{1,0:T(8,128)S(1)} %get-tuple-element.154.inv_in_ref, ...), custom_call_target="tpu_custom_call" | custom-call | tf_op jit(solution)/shard_map/pallas_call | solution.py:327
  31.0 0.4 collective-permute-done.10
  31.5 0.1 collective-permute-start.11
  31.5 0.2 shard_map.119
  31.7 1.2 %collective-permute-done.11 = f32[128,256]{1,0:T(8,128)S(1)} collective-permute-done((f32[128,256]{1,0:T(8,128)S(1)}, f32[128,256]{1,0:T(8,128)S(1)}, u32[]{:S(2)}, u32[]{:S(2)}) %collective-permute-start.11) | collective-permute-done | bytes 131104 | tf_op jit(solution)/shard_map/ppermute | solution.py:345
  32.9 2.2 %shard_map.120 = (f32[512,256]{1,0:T(8,128)S(1)}, bf16[512,128]{1,0:T(8,128)(2,1)S(1)}, f32[128,256]{1,0:T(8,128)S(1)}, f32[8,256]{1,0:T(8,128)S(1)}, bf16[256,256]{1,0:T(8,128)(2,1)S(1)}) custom-call(s32[2,12]{1,0:T(2,128)S(1)} %get-tuple-element.113.allrefs_0_.pair_in_ref, s32[8,12]{1,0:T(8,128)S(1)} %get-tuple-element.114.allrefs_1_.stoich_in_ref, ...), custom_call_target="tpu_custom_call" | custom-call | tf_op jit(solution)/shard_map/pallas_call | solution.py:327
  35.1 0.2 collective-permute-start.12
  35.3 1.2 %shard_map.121 = (bf16[512,128]{1,0:T(8,128)(2,1)S(1)}, f32[128,256]{1,0:T(8,128)S(1)}, f32[8,256]{1,0:T(8,128)S(1)}) custom-call(s32[2,12]{1,0:T(2,128)S(1)} %get-tuple-element.113.allrefs_0_.pair_in_ref, s32[8,12]{1,0:T(8,128)S(1)} %get-tuple-element.114.allrefs_1_.stoich_in_ref, f32[1,12]{1,0:T(1,128)S(1)} %get-tuple-element.115.allrefs_2_.speed_in_ref, ...), custom_call_target="tpu_custom_call" | custom-call | tf_op jit(solution)/shard_map/pallas_call | solution.py:327
  36.6 0.0 collective-permute-done.12
  36.7 1.1 %collective-permute-start.15 = (f16[136,256]{1,0:T(8,128)(2,1)S(1)}, f16[136,256]{1,0:T(8,128)(2,1)S(1)}, u32[]{:S(2)}, u32[]{:S(2)}) collective-permute-start(f16[136,256]{1,0:T(8,128)(2,1)S(1)} %pad_maximum_fusion.4), channel_id=1, source_target_pairs={{0,6},{1,7},{2,4},{3,5},{4,2},{5,3},{6,0},{7,1},{8,14},{9,15},{10,... | collective-permute-start | bytes 208904 | tf_op jit(solution)/shard_map/ppermute | solution.py:345
  37.8 1.5 %collective-permute-start.14 = (f16[136,256]{1,0:T(8,128)(2,1)S(1)}, f16[136,256]{1,0:T(8,128)(2,1)S(1)}, u32[]{:S(2)}, u32[]{:S(2)}) collective-permute-start(f16[136,256]{1,0:T(8,128)(2,1)S(1)} %pad_maximum_fusion.4), channel_id=1, source_target_pairs={{0,4},{1,5},{2,6},{3,7},{4,0},{5,1},{6,2},{7,3},{8,12},{9,13},{10,... | collective-permute-start | bytes 208904 | tf_op jit(solution)/shard_map/ppermute | solution.py:345
  39.3 1.0 %collective-permute-start.13 = (f16[136,256]{1,0:T(8,128)(2,1)S(1)}, f16[136,256]{1,0:T(8,128)(2,1)S(1)}, u32[]{:S(2)}, u32[]{:S(2)}) collective-permute-start(f16[136,256]{1,0:T(8,128)(2,1)S(1)} %pad_maximum_fusion.4), channel_id=1, source_target_pairs={{0,2},{1,3},{2,0},{3,1},{4,6},{5,7},{6,4},{7,5},{8,10},{9,11},{10,... | collective-permute-start | bytes 208904 | tf_op jit(solution)/shard_map/ppermute | solution.py:345
  40.3 3.2 %shard_map.122 = (bf16[256,256]{1,0:T(8,128)(2,1)S(1)}, bf16[256,256]{1,0:T(8,128)(2,1)S(1)}, f32[256,256]{1,0:T(8,128)S(1)}, f32[8,256]{1,0:T(8,128)S(1)}) custom-call(bf16[256,256]{1,0:T(8,128)(2,1)S(1)} %get-tuple-element.185.coef_ref), custom_call_target="tpu_custom_call" | custom-call | tf_op jit(solution)/shard_map/pallas_call | solution.py:327
  43.5 0.0 collective-permute-done.15
  43.5 0.0 collective-permute-done.14
  43.5 0.2 collective-permute-done.13
  43.7 0.1 multiply_convert_fusion
  43.8 1.9 %collective-permute-start.16 = (f16[136,256]{1,0:T(8,128)(2,1)S(1)}, f16[136,256]{1,0:T(8,128)(2,1)S(1)}, u32[]{:S(2)}, u32[]{:S(2)}) collective-permute-start(f16[136,256]{1,0:T(8,128)(2,1)S(1)} %pad_maximum_fusion.5), channel_id=1, source_target_pairs={{0,8},{1,9},{2,10},{3,11},{4,12},{5,13},{6,14},{7,15},{8,0},{9,1},... | collective-permute-start | bytes 208904 | tf_op jit(solution)/shard_map/ppermute | solution.py:345
  45.7 3.0 %shard_map.123 = (f32[256,256]{1,0:T(8,128)S(1)}, f32[512,256]{1,0:T(8,128)S(1)}) custom-call(f32[8,256]{1,0:T(8,128)S(1)} %get-tuple-element.198.gap_in_ref, bf16[256,256]{1,0:T(8,128)(2,1)S(1)} %get-tuple-element.199.high_ref, bf16[256,256]{1,0:T(8,128)(2,1)S(1)} %get-tuple-element.200.low_ref, f32[256,256]{1,0:T(8,128)S(1)} %get-tuple-element.201.inv_in_ref, ...), custom_call_target="tpu_custom_call" | custom-call | tf_op jit(solution)/shard_map/pallas_call | solution.py:327
  48.7 1.1 %collective-permute-done.16 = f16[136,256]{1,0:T(8,128)(2,1)S(1)} collective-permute-done((f16[136,256]{1,0:T(8,128)(2,1)S(1)}, f16[136,256]{1,0:T(8,128)(2,1)S(1)}, u32[]{:S(2)}, u32[]{:S(2)}) %collective-permute-start.16) | collective-permute-done | bytes 69664 | tf_op jit(solution)/shard_map/ppermute | solution.py:345
  49.9 0.1 collective-permute-start.17
  50.0 0.2 shard_map.124
  50.1 1.2 %collective-permute-done.17 = f32[128,256]{1,0:T(8,128)S(1)} collective-permute-done((f32[128,256]{1,0:T(8,128)S(1)}, f32[128,256]{1,0:T(8,128)S(1)}, u32[]{:S(2)}, u32[]{:S(2)}) %collective-permute-start.17) | collective-permute-done | bytes 131104 | tf_op jit(solution)/shard_map/ppermute | solution.py:345
  51.3 1.6 %shard_map.125 = (f32[512,256]{1,0:T(8,128)}, bf16[16,256]{1,0:T(8,128)(2,1)}) custom-call(f32[512,256]{1,0:T(8,128)S(1)} %get-tuple-element.216.base_ref, bf16[512,256]{1,0:T(8,128)(2,1)S(1)} %get-tuple-element.217.diff_high_ref, bf16[512,256]{1,0:T(8,128)(2,1)S(1)} %get-tuple-element.218.diff_low_ref, bf16[256,256]{1,0:T(8,128)(2,1)S(1)} %get-tuple-element.219.high_ref, ...), custom_call_target="tpu_custom_call" | custom-call | tf_op jit(solution)/shard_map/pallas_call | solution.py:327
  (33 shorter events, 0.5 us)
Async XLA Ops:
  0.6 1.6 %copy-start = (bf16[16,256]{1,0:T(8,128)(2,1)S(1)}, bf16[16,256]{1,0:T(8,128)(2,1)}, u32[]{:S(2)}) copy-start(bf16[16,256]{1,0:T(8,128)(2,1)} %param.11) | copy-start | bytes 24580
  0.6 1.6 %collective-permute-start = (bf16[16,256]{1,0:T(8,128)(2,1)}, bf16[16,256]{1,0:T(8,128)(2,1)S(1)}, u32[]{:S(2)}, u32[]{:S(2)}) collective-permute-start(bf16[16,256]{1,0:T(8,128)(2,1)} %param.11), channel_id=1, source_target_pairs={{0,1},{1,0},{2,3},{3,2},{4,5},{5,4},{6,7},{7,6},{8,9},{9,8},{10,11... | collective-permute-start | bytes 24584 | tf_op jit(solution)/shard_map/ppermute | solution.py:345
  2.2 8.1 %collective-permute-start.4 = (bf16[32,256]{1,0:T(8,128)(2,1)S(1)}, bf16[32,256]{1,0:T(8,128)(2,1)S(1)}, u32[]{:S(2)}, u32[]{:S(2)}) collective-permute-start(bf16[32,256]{1,0:T(8,128)(2,1)S(1)} %maximum_select_fusion.2.allrefs_7_), channel_id=1, source_target_pairs={{1,15},{3,13},{5,11},{7,9},{9,7},{11,5},{13,3},{15,1},{17,31},{19,... | collective-permute-start | bytes 49160 | tf_op jit(solution)/shard_map/ppermute | solution.py:345
  2.9 7.5 %collective-permute-start.3 = (bf16[32,256]{1,0:T(8,128)(2,1)S(1)}, bf16[32,256]{1,0:T(8,128)(2,1)S(1)}, u32[]{:S(2)}, u32[]{:S(2)}) collective-permute-start(bf16[32,256]{1,0:T(8,128)(2,1)S(1)} %maximum_select_fusion.2.allrefs_7_), channel_id=1, source_target_pairs={{0,10},{1,13},{2,8},{3,15},{4,14},{5,9},{6,12},{7,11},{8,2},{9,5},... | collective-permute-start | bytes 49160 | tf_op jit(solution)/shard_map/ppermute | solution.py:345
  7.8 4.6 %collective-permute-start.2 = (bf16[32,256]{1,0:T(8,128)(2,1)S(1)}, bf16[32,256]{1,0:T(8,128)(2,1)S(1)}, u32[]{:S(2)}, u32[]{:S(2)}) collective-permute-start(bf16[32,256]{1,0:T(8,128)(2,1)S(1)} %maximum_select_fusion.2.allrefs_7_), channel_id=1, source_target_pairs={{0,8},{1,7},{2,10},{3,5},{4,12},{5,3},{6,14},{7,1},{8,0},{9,15},{1... | collective-permute-start | bytes 49160 | tf_op jit(solution)/shard_map/ppermute | solution.py:345
  8.2 4.3 %collective-permute-start.1 = (bf16[32,256]{1,0:T(8,128)(2,1)S(1)}, bf16[32,256]{1,0:T(8,128)(2,1)S(1)}, u32[]{:S(2)}, u32[]{:S(2)}) collective-permute-start(bf16[32,256]{1,0:T(8,128)(2,1)S(1)} %maximum_select_fusion.2.allrefs_7_), channel_id=1, source_target_pairs={{0,2},{1,5},{2,0},{3,7},{4,6},{5,1},{6,4},{7,3},{8,10},{9,13},{10,... | collective-permute-start | bytes 49160 | tf_op jit(solution)/shard_map/ppermute | solution.py:345
  12.5 2.9 %collective-permute-start.5 = (bf16[128,256]{1,0:T(8,128)(2,1)S(1)}, bf16[128,256]{1,0:T(8,128)(2,1)S(1)}, u32[]{:S(2)}, u32[]{:S(2)}) collective-permute-start(bf16[128,256]{1,0:T(8,128)(2,1)S(1)} %constant_dynamic-update-slice_fusion.allrefs_8_), channel_id=1, source_target_pairs={{0,1},{1,0},{2,3},{3,2},{4,5},{5,4},{6,7},{7,6},{8,9},{9,8},{10,11... | collective-permute-start | bytes 196616 | tf_op jit(solution)/shard_map/ppermute | solution.py:345
  16.7 1.7 %collective-permute-start.6 = (f32[136,256]{1,0:T(8,128)S(1)}, f32[136,256]{1,0:T(8,128)S(1)}, u32[]{:S(2)}, u32[]{:S(2)}) collective-permute-start(f32[136,256]{1,0:T(8,128)S(1)} %pad_maximum_fusion), channel_id=1, source_target_pairs={{0,1},{1,0},{2,3},{3,2},{4,5},{5,4},{6,7},{7,6},{8,9},{9,8},{10,11... | collective-permute-start | bytes 417800 | tf_op jit(solution)/shard_map/ppermute | solution.py:345
  18.5 6.7 %collective-permute-start.9 = (f16[136,256]{1,0:T(8,128)(2,1)S(1)}, f16[136,256]{1,0:T(8,128)(2,1)S(1)}, u32[]{:S(2)}, u32[]{:S(2)}) collective-permute-start(f16[136,256]{1,0:T(8,128)(2,1)S(1)} %pad_maximum_fusion.2), channel_id=1, source_target_pairs={{0,6},{1,7},{2,4},{3,5},{4,2},{5,3},{6,0},{7,1},{8,14},{9,15},{10,... | collective-permute-start | bytes 208904 | tf_op jit(solution)/shard_map/ppermute | solution.py:345
  19.4 5.8 %collective-permute-start.8 = (f16[136,256]{1,0:T(8,128)(2,1)S(1)}, f16[136,256]{1,0:T(8,128)(2,1)S(1)}, u32[]{:S(2)}, u32[]{:S(2)}) collective-permute-start(f16[136,256]{1,0:T(8,128)(2,1)S(1)} %pad_maximum_fusion.2), channel_id=1, source_target_pairs={{0,4},{1,5},{2,6},{3,7},{4,0},{5,1},{6,2},{7,3},{8,12},{9,13},{10,... | collective-permute-start | bytes 208904 | tf_op jit(solution)/shard_map/ppermute | solution.py:345
  20.5 4.7 %collective-permute-start.7 = (f16[136,256]{1,0:T(8,128)(2,1)S(1)}, f16[136,256]{1,0:T(8,128)(2,1)S(1)}, u32[]{:S(2)}, u32[]{:S(2)}) collective-permute-start(f16[136,256]{1,0:T(8,128)(2,1)S(1)} %pad_maximum_fusion.2), channel_id=1, source_target_pairs={{0,2},{1,3},{2,0},{3,1},{4,6},{5,7},{6,4},{7,5},{8,10},{9,11},{10,... | collective-permute-start | bytes 208904 | tf_op jit(solution)/shard_map/ppermute | solution.py:345
  25.4 6.0 %collective-permute-start.10 = (f16[136,256]{1,0:T(8,128)(2,1)S(1)}, f16[136,256]{1,0:T(8,128)(2,1)S(1)}, u32[]{:S(2)}, u32[]{:S(2)}) collective-permute-start(f16[136,256]{1,0:T(8,128)(2,1)S(1)} %pad_maximum_fusion.3), channel_id=1, source_target_pairs={{0,8},{1,9},{2,10},{3,11},{4,12},{5,13},{6,14},{7,15},{8,0},{9,1},... | collective-permute-start | bytes 208904 | tf_op jit(solution)/shard_map/ppermute | solution.py:345
  31.5 1.4 %collective-permute-start.11 = (f32[128,256]{1,0:T(8,128)S(1)}, f32[128,256]{1,0:T(8,128)S(1)}, u32[]{:S(2)}, u32[]{:S(2)}) collective-permute-start(f32[128,256]{1,0:T(8,128)S(1)} %multiply_add_fusion.1), channel_id=1, source_target_pairs={{0,1},{1,0},{2,3},{3,2},{4,5},{5,4},{6,7},{7,6},{8,9},{9,8},{10,11... | collective-permute-start | bytes 393224 | tf_op jit(solution)/shard_map/ppermute | solution.py:345
  35.1 1.5 %collective-permute-start.12 = (f32[136,256]{1,0:T(8,128)S(1)}, f32[136,256]{1,0:T(8,128)S(1)}, u32[]{:S(2)}, u32[]{:S(2)}) collective-permute-start(f32[136,256]{1,0:T(8,128)S(1)} %pad_maximum_fusion.1), channel_id=1, source_target_pairs={{0,1},{1,0},{2,3},{3,2},{4,5},{5,4},{6,7},{7,6},{8,9},{9,8},{10,11... | collective-permute-start | bytes 417800 | tf_op jit(solution)/shard_map/ppermute | solution.py:345
  36.7 6.8 %collective-permute-start.15 = (f16[136,256]{1,0:T(8,128)(2,1)S(1)}, f16[136,256]{1,0:T(8,128)(2,1)S(1)}, u32[]{:S(2)}, u32[]{:S(2)}) collective-permute-start(f16[136,256]{1,0:T(8,128)(2,1)S(1)} %pad_maximum_fusion.4), channel_id=1, source_target_pairs={{0,6},{1,7},{2,4},{3,5},{4,2},{5,3},{6,0},{7,1},{8,14},{9,15},{10,... | collective-permute-start | bytes 208904 | tf_op jit(solution)/shard_map/ppermute | solution.py:345
  37.8 5.6 %collective-permute-start.14 = (f16[136,256]{1,0:T(8,128)(2,1)S(1)}, f16[136,256]{1,0:T(8,128)(2,1)S(1)}, u32[]{:S(2)}, u32[]{:S(2)}) collective-permute-start(f16[136,256]{1,0:T(8,128)(2,1)S(1)} %pad_maximum_fusion.4), channel_id=1, source_target_pairs={{0,4},{1,5},{2,6},{3,7},{4,0},{5,1},{6,2},{7,3},{8,12},{9,13},{10,... | collective-permute-start | bytes 208904 | tf_op jit(solution)/shard_map/ppermute | solution.py:345
  39.3 4.4 %collective-permute-start.13 = (f16[136,256]{1,0:T(8,128)(2,1)S(1)}, f16[136,256]{1,0:T(8,128)(2,1)S(1)}, u32[]{:S(2)}, u32[]{:S(2)}) collective-permute-start(f16[136,256]{1,0:T(8,128)(2,1)S(1)} %pad_maximum_fusion.4), channel_id=1, source_target_pairs={{0,2},{1,3},{2,0},{3,1},{4,6},{5,7},{6,4},{7,5},{8,10},{9,11},{10,... | collective-permute-start | bytes 208904 | tf_op jit(solution)/shard_map/ppermute | solution.py:345
  43.8 6.0 %collective-permute-start.16 = (f16[136,256]{1,0:T(8,128)(2,1)S(1)}, f16[136,256]{1,0:T(8,128)(2,1)S(1)}, u32[]{:S(2)}, u32[]{:S(2)}) collective-permute-start(f16[136,256]{1,0:T(8,128)(2,1)S(1)} %pad_maximum_fusion.5), channel_id=1, source_target_pairs={{0,8},{1,9},{2,10},{3,11},{4,12},{5,13},{6,14},{7,15},{8,0},{9,1},... | collective-permute-start | bytes 208904 | tf_op jit(solution)/shard_map/ppermute | solution.py:345
  49.9 1.4 %collective-permute-start.17 = (f32[128,256]{1,0:T(8,128)S(1)}, f32[128,256]{1,0:T(8,128)S(1)}, u32[]{:S(2)}, u32[]{:S(2)}) collective-permute-start(f32[128,256]{1,0:T(8,128)S(1)} %multiply_add_fusion), channel_id=1, source_target_pairs={{0,1},{1,0},{2,3},{3,2},{4,5},{5,4},{6,7},{7,6},{8,9},{9,8},{10,11... | collective-permute-start | bytes 393224 | tf_op jit(solution)/shard_map/ppermute | solution.py:345

commit v7 on v6

--- a/solution.py
+++ b/solution.py
@@ -66,7 +66,7 @@
 
 
 def react(
-    diffused, base, coef_ref, emis_ref, live_ref, ready, pair_ref, stoich_ref, speed_ref, loss_ref,
+    diffused, base, coef_base, coef_ref, emis_ref, live_ref, ready, pair_ref, stoich_ref, speed_ref, loss_ref,
     field_ref, tend_ref, rate_ref, top_ref,
 ):
     mode_bf = diffused.astype(BF16)
@@ -79,7 +79,8 @@
     for b in range(members // block):
         lanes = slice(b * block, (b + 1) * block)
         spot = pl.ds(pl.multiple_of(base + b * block, block), block)
-        field_ref[...] = mm(mode_bf, coef_ref[spot, :], NT) * (1.0 / math.sqrt(R))
+        member = pl.ds(pl.multiple_of(coef_base + b * block, block), block)
+        field_ref[...] = mm(mode_bf, coef_ref[member, :], NT) * (1.0 / math.sqrt(R))
         if b == 0:
             ready()
 
@@ -124,8 +125,8 @@
     columns,
     pair_hbm, stoich_hbm, speed_hbm, loss_hbm, table_hbm, level_face_hbm, idx_hbm, modes_hbm,
     counts_ref,
-    pair_ref, stoich_ref, speed_ref, loss_ref, modes_ref, emis_ref, face_ref, live_ref,
-    table_ref, level_face_ref, idx_ref, sems,
+    pair_ref, stoich_ref, speed_ref, loss_ref, diff_ref, emis_ref, face_ref, live_ref,
+    table_ref, level_face_ref, idx_ref, modes_ref, sems,
 ):
     later = fetch(
         (pair_hbm, stoich_hbm, speed_hbm, loss_hbm, modes_hbm),
@@ -152,9 +153,199 @@
         face_ref[part, :] = jnp.broadcast_to(face, (LEV, R))
         live_ref[part, :] = jnp.where(level < count, 1.0, 0.0)
     later()
-
-
-def diffuse_kernel(modes_ref, face_ref, diff_ref):
+    diff_ref[...] = diffuse_rows(modes_ref[...], face_ref)
+
+
+def put_blocks(source_ref, target_ref, base):
+    chip = lax.axis_index("col") // 2
+    rows = source_ref.shape[0] // 4
+    for j in range(4):
+        spot = pl.multiple_of(base + ((chip ^ j) & 3) * rows, rows)
+        target_ref[pl.ds(spot, rows), :] = source_ref[j * rows : (j + 1) * rows, :]
+
+
+def give_kernel(
+    fetched,
+    pair_in_ref, stoich_in_ref, speed_in_ref, loss_in_ref,
+    diff_ref, emis_ref, live_ref, coef_in_ref,
+    tend_ref, rate_ref, top_ref,
+    field_ref, *chem_sems,
+):
+    if fetched:
+        *chem_sems, coef_ref = chem_sems
+    *chem, sems = chem_sems
+    ready = fetch((pair_in_ref, stoich_in_ref, speed_in_ref, loss_in_ref), chem, sems)
+    base = half_start(tend_ref.shape[1], False)
+    if fetched:
+        put_blocks(coef_in_ref, coef_ref, 0)
+    else:
+        coef_ref = coef_in_ref
+    react(
+        diff_ref[...], base, 0 if fetched else base, coef_ref, emis_ref, live_ref,
+        ready, *chem, field_ref, tend_ref, rate_ref, top_ref,
+    )
+
+
+def keep_kernel(
+    fetched,
+    pair_in_ref, stoich_in_ref, speed_in_ref, loss_in_ref,
+    diff_ref, emis_ref, live_ref, *refs,
+):
+    if fetched:
+        give_ref, keep_ref, tend_ref, rate_ref, top_ref, coef_ref, field_ref, *chem_sems = refs
+    else:
+        coef_ref, tend_ref, rate_ref, top_ref, field_ref, *chem_sems = refs
+    *chem, sems = chem_sems
+    ready = fetch((pair_in_ref, stoich_in_ref, speed_in_ref, loss_in_ref), chem, sems)
+    half = tend_ref.shape[1]
+    base = half_start(half, True)
+    if fetched:
+        put_blocks(give_ref, coef_ref, half_start(half, False))
+        put_blocks(keep_ref, coef_ref, base)
+    react(
+        diff_ref[...], base, base, coef_ref, emis_ref, live_ref,
+        ready, *chem, field_ref, tend_ref, rate_ref, top_ref,
+    )
+
+
+STEP = 0.1
+RATE_STEP = 0.3
+RIDGE_SHARE = 0.05
+
+F32 = jnp.float32
+BF16 = jnp.bfloat16
+
+NN = (((1,), (0,)), ((), ()))
+NT = (((1,), (1,)), ((), ()))
+TN = (((0,), (0,)), ((), ()))
+
+
+def mm(a, b, dims=NN):
+    return lax.dot_general(a, b, dims, preferred_element_type=F32)
+
+
+def split(x):
+    high = x.astype(BF16)
+    return high, (x - high.astype(F32)).astype(BF16)
+
+
+def mm3(a, b, dims=NN):
+    return mm(a[0], b[0], dims) + (mm(a[0], b[1], dims) + mm(a[1], b[0], dims))
+
+
+def diffuse_rows(modes, face_ref):
+    faces = []
+    for c in range(face_ref.shape[0] // LEV):
+        faces += [face_ref[c * LEV : (c + 1) * LEV, :]] * S
+    face = jnp.concatenate(faces, axis=0)
+    rows = modes.shape[0]
+    flux = face * (pltpu.roll(modes, rows - 1, 0) - modes)
+    return modes + flux - pltpu.roll(flux, 1, 0)
+
+
+def fetch(sources, targets, sems):
+    copies = [
+        pltpu.make_async_copy(source, target, sems.at[i])
+        for i, (source, target) in enumerate(zip(sources, targets, strict=True))
+    ]
+    for copy in copies:
+        copy.start()
+
+    def wait():
+        for copy in copies:
+            copy.wait()
+
+    return wait
+
+
+def react(
+    diffused, base, coef_base, coef_ref, emis_ref, live_ref, ready, pair_ref, stoich_ref, speed_ref, loss_ref,
+    field_ref, tend_ref, rate_ref, top_ref,
+):
+    mode_bf = diffused.astype(BF16)
+    members = tend_ref.shape[1]
+    block = field_ref.shape[1]
+    columns = diffused.shape[0] // (S * LEV)
+    step = 16
+    steps = LEV // step
+    largest = jnp.full((1, R), 2.0**-120, F32)
+    for b in range(members // block):
+        lanes = slice(b * block, (b + 1) * block)
+        spot = pl.ds(pl.multiple_of(base + b * block, block), block)
+        member = pl.ds(pl.multiple_of(coef_base + b * block, block), block)
+        field_ref[...] = mm(mode_bf, coef_ref[member, :], NT) * (1.0 / math.sqrt(R))
+        if b == 0:
+            ready()
+
+        def part(i, _):
+            c = i // steps
+            low = (i - c * steps) * step
+            first = c * (S * LEV) + low
+            level = lax.broadcasted_iota(jnp.int32, (step, block), 0) + low
+            profile = jnp.exp(level.astype(F32) * (-4.0 / LEV))
+            live = live_ref[pl.ds(pl.multiple_of(c * LEV + low, step), step), 0:block] > 0.5
+
+            def amount(s):
+                return field_ref[pl.ds(pl.multiple_of(first + s * LEV, step), step), :]
+
+            total = []
+            for s in range(S):
+                total.append(emis_ref[s : s + 1, spot] * profile - loss_ref[0, s] * amount(s))
+            for r in range(NREAC):
+                speed = speed_ref[0, r] * amount(pair_ref[0, r]) * amount(pair_ref[1, r])
+                for s in range(S):
+                    total[s] = total[s] + stoich_ref[s, r].astype(F32) * speed
+            for s in range(S):
+                tend_ref[pl.ds(pl.multiple_of(first + s * LEV, step), step), lanes] = jnp.where(
+                    live, total[s], 0.0
+                ).astype(BF16)
+            return 0
+
+        lax.fori_loop(0, columns * steps, part, 0, unroll=members <= block)
+        rate = mm(tend_ref[:, lanes], mode_bf, TN)
+        rate_ref[lanes, :] = rate
+        largest = jnp.maximum(largest, jnp.max(jnp.abs(rate), axis=0, keepdims=True))
+    power = jnp.maximum(jnp.floor(jnp.log(largest) * (1.0 / math.log(2.0))) + 2.0, -100.0)
+    top_ref[...] = jnp.broadcast_to(power, top_ref.shape)
+
+
+def half_start(members, keep):
+    side = lax.axis_index("col") & 1
+    return (side if keep else 1 - side) * members
+
+
+def stage_kernel(
+    columns,
+    pair_hbm, stoich_hbm, speed_hbm, loss_hbm, table_hbm, level_face_hbm, idx_hbm, modes_hbm,
+    counts_ref,
+    pair_ref, stoich_ref, speed_ref, loss_ref, diff_ref, emis_ref, face_ref, live_ref,
+    table_ref, level_face_ref, idx_ref, modes_ref, sems,
+):
+    later = fetch(
+        (pair_hbm, stoich_hbm, speed_hbm, loss_hbm, modes_hbm),
+        (pair_ref, stoich_ref, speed_ref, loss_ref, modes_ref),
+        sems,
+    )
+    fetch(
+        (table_hbm, level_face_hbm, idx_hbm), (table_ref, level_face_ref, idx_ref), sems.at[5:8]
+    )()
+    index = idx_ref[...]
+    for s in range(S):
+        row = jnp.zeros(index.shape, F32)
+        for k in range(NEMIS):
+            row = jnp.where(index == k, table_ref[s, k], row)
+        emis_ref[s : s + 1, :] = row
+    down = lax.broadcasted_iota(jnp.int32, (LEV, LEV), 0)
+    across = lax.broadcasted_iota(jnp.int32, (LEV, LEV), 1)
+    level = lax.broadcasted_iota(jnp.int32, (LEV, R), 0)
+    for c in range(columns):
+        part = slice(c * LEV, (c + 1) * LEV)
+        count = counts_ref[:, c : c + 1]
+        inner = (down == across) & (down + 1 < count)
+        face = jnp.sum(jnp.where(inner, level_face_ref[c : c + 1, :], 0.0), axis=1, keepdims=True)
+        face_ref[part, :] = jnp.broadcast_to(face, (LEV, R))
+        live_ref[part, :] = jnp.where(level < count, 1.0, 0.0)
+    later()
     diff_ref[...] = diffuse_rows(modes_ref[...], face_ref)
 
 
@@ -234,8 +425,9 @@
     )
     diffused = diffuse_rows(modes, face_ref)
     diff_ref[...] = diffused
+    base = half_start(tend_ref.shape[1], False)
     react(
-        diffused, half_start(tend_ref.shape[1], False), coef_out_ref, emis_ref, live_ref,
+        diffused, base, base, coef_out_ref, emis_ref, live_ref,
         ready, *chem, field_ref, tend_ref, rate_ref, top_ref,
     )
 
@@ -343,6 +535,23 @@
 
 def swap(value, n, masks):
     return lax.ppermute(value, "col", [(i, i ^ masks[i % 2]) for i in range(n) if masks[i % 2]])
+
+
+def fetch_half(chip_rows, n):
+    blocks = []
+    for j in range(4):
+        pairs = []
+        for target in range(n):
+            chip, side = target // 2, target % 2
+            if chip // 4 == 1 - side:
+                if j:
+                    pairs.append(((chip ^ j) * 2 + side, target))
+            else:
+                pairs.append(((chip ^ j ^ 4) * 2 + 1 - side, target))
+        blocks.append(lax.ppermute(chip_rows, "col", pairs))
+    place = lax.axis_index("col")
+    blocks[0] = jnp.where(place // 8 == 1 - place % 2, chip_rows, blocks[0])
+    return blocks
 
 
 EXTRA = 8
@@ -436,7 +645,7 @@
     def stage(modes):
         by_level = ((columns * LEV, R), F32)
         index = emis_idx.reshape(1, members)
-        *chem, modes, emis, face, live = call(
+        *chem, diff, emis, face, live = call(
             functools.partial(stage_kernel, columns), 8,
             [(value.shape, value.dtype) for value in tables]
             + [rows_f32, ((S, members), F32), by_level, by_level],
@@ -444,69 +653,64 @@
                 pltpu.SMEM((S, NEMIS), F32),
                 pltpu.VMEM(diffusivity.shape, F32),
                 pltpu.VMEM((1, members), jnp.int32),
+                pltpu.VMEM((rows, R), F32),
                 pltpu.SemaphoreType.DMA((8,)),
             ],
             *tables, emis_table.T, diffusivity, index, modes, counts.reshape(1, columns),
         )
-        return chem, modes, emis, face, live
-
-    def spread(modes, face):
-        return call(diffuse_kernel, 0, [rows_f32], [], modes, face)[0]
+        return chem, diff, emis, face, live
 
     if n == 16:
-        plan = ((1, 2), (4, 3), (5, 6), (0, 7))
         other = swap(coeffs, n, (1, 1))
         side = lax.axis_index("col") & 1
         chip = jnp.where(
             side == 0, jnp.concatenate([coeffs, other], 0), jnp.concatenate([other, coeffs], 0)
         )
-        fetched = [swap(chip, n, (2 * a, 2 * b)) for a, b in plan]
-        chem, modes, emis, face, live = stage(tied(mode_rows, chip))
-        fetched, modes = lax.optimization_barrier((fetched, modes))
-        mine_rows = jnp.concatenate(fetched, 0)
-        theirs = swap(mine_rows, n, (1, 1))
-        diff = spread(tied(modes, mine_rows), face)
-        theirs, diff = lax.optimization_barrier((theirs, diff))
-        gathered = (chip, mine_rows, theirs)
-        tend, rate, top, coef = call(
-            functools.partial(first_kernel, plan), 0,
-            [tend_out, half_out, top_out, coef_out], react_tmp,
-            *chem, diff, emis, live, *gathered,
-        )
+        blocks = fetch_half(chip, n)
+        chem, diff, emis, face, live = stage(tied(mode_rows, chip))
+        blocks, diff = lax.optimization_barrier((blocks, diff))
+        coef = jnp.concatenate(blocks, 0)
     else:
         coef = lax.all_to_all(jnp.tile(coeffs, (n, 1)), "col", 0, 0, tiled=True)
-        chem, modes, emis, face, live = stage(mode_rows)
-        diff = spread(modes, face)
-        tend, rate, top = call(
-            functools.partial(first_kernel, ()), 0,
-            [tend_out, half_out, top_out], react_tmp,
-            *chem, diff, emis, live, coef,
-        )
-
-    def summed(rate, top, coef, tend, diff):
+        chem, diff, emis, face, live = stage(mode_rows)
+    fetched = n == 16
+    keep_coef = swap(coef, n, (1, 1)) if fetched else None
+    tend, rate, top = call(
+        functools.partial(give_kernel, fetched), 0,
+        [tend_out, half_out, top_out],
+        react_tmp + [pltpu.VMEM((half, R), BF16)] * fetched,
+        *chem, diff, emis, live, coef,
+    )
+    if fetched:
+        keep_coef, rate = lax.optimization_barrier((keep_coef, rate))
+
+    def summed(rate, top, coef, tend, diff, keep_coef=None):
         def keep_half():
-            tend_keep, keep, keep_top = call(
-                second_kernel, 0, [tend_out, half_out, top_out], react_tmp,
-                *chem, tied(diff, rate), emis, live, coef,
+            fetched = keep_coef is not None
+            tend_keep, keep, keep_top, *made = call(
+                functools.partial(keep_kernel, fetched), 0,
+                [tend_out, half_out, top_out] + [coef_out] * fetched, react_tmp,
+                *chem, tied(diff, rate), emis, live, coef, *([keep_coef] if fetched else []),
             )
-            return keep, keep_top, tend_keep
-
-        def start(tend_keep, ready):
-            return tend_keep, call(
+            return keep, keep_top, (tend_keep, made[0] if fetched else coef)
+
+        def start(state, ready):
+            coef = state[1]
+            return state, call(
                 functools.partial(inverse_start, ridge, 4), 0,
                 [square_bf, square_bf, square, top_out], [], tied(coef, ready),
             )
 
         def end(state, ready):
-            tend_keep, (high, low, inv, gap) = tied(state, ready)
-            return call(
+            (tend_keep, coef), (high, low, inv, gap) = tied(state, ready)
+            return coef, *call(
                 inverse_end, 0, [rate_out, rows_f32], [pltpu.VMEM((R, R), F32)],
                 gap, high, low, inv, coef, tend, tend_keep,
             )
 
         def prepare(state, ready):
-            solved, pull = tied(state, ready)
-            return call(
+            coef, solved, pull = tied(state, ready)
+            return coef, call(
                 ready_kernel, 0,
                 [rows_f32, rows_bf, rows_bf, ((members, R), BF16), ((members, R), BF16)], [],
                 diff, pull, solved,
@@ -515,13 +719,14 @@
         return sum_over(rate, top, keep_half, n, (start, end), prepare)
 
     for _ in range(NSUB - 1):
-        total, prepared = summed(rate, top, coef, tend, diff)
+        total, (coef, prepared) = summed(rate, top, coef, tend, diff, keep_coef)
+        keep_coef = None
         diff, tend, rate, top, coef = call(
             functools.partial(middle_kernel, total_rows), 0,
             [rows_f32, tend_out, half_out, top_out, coef_out], react_tmp,
             *chem, *prepared, total, coef, face, emis, live,
         )
-    total, prepared = summed(rate, top, coef, tend, diff)
+    total, (coef, prepared) = summed(rate, top, coef, tend, diff, keep_coef)
     return tuple(
         call(
             functools.partial(last_kernel, total_rows), 0,

time: 53.1 us -> 57.2 us (1.077)
  waiting for transfers between devices: 8.01 us -> 13.7 us
  starting transfers between devices: 21.1 us -> 19.5 us
    ppermute x18 -> x14, starting transfers between devices: 21.1 us -> 9.19 us  [swap(): lax.ppermute(value, 'col', [(i, i ^ masks[i % 2]) for i in range(n) if ma...]
    ppermute x0 -> x4, starting transfers between devices: none -> 10.3 us  [fetch_half(): blocks.append(lax.ppermute(chip_rows, 'col', pairs))]
    ppermute x0 -> x4, waiting for transfers between devices: none -> 4.5 us  [fetch_half(): blocks.append(lax.ppermute(chip_rows, 'col', pairs))]
    ppermute x18 -> x14, waiting for transfers between devices: 8.01 us -> 9.18 us  [swap(): lax.ppermute(value, 'col', [(i, i ^ masks[i % 2]) for i in range(n) if ma...]
    pallas_call x13 -> x12, Pallas kernels: 21.6 us -> 21.6 us  [call(): pl.pallas_call(kernel, in_specs=[pl.BlockSpec(memory_space=pltpu.HBM if i...]
  transfers between devices with their start and end apart: 18 -> 18, of which waited for: 8 -> 9; matrix products, arithmetic and copies ran while one was open for 0% -> 0% of each run, Pallas kernels for 31% -> 31%
where the time goes in v7:
time: 57.2 us; the launch traced here: 57.1 us
  Pallas kernels  21.6 us (38%)
  starting transfers between devices  19.5 us (34%)
  waiting for transfers between devices  13.7 us (24%)
  between operations  1.66 us (3%)
  other arithmetic  0.59 us (1%)
    pallas_call x12, Pallas kernels, call(): pl.pallas_call(kernel, in_specs=[pl.BlockSpec(memory_space=pltpu.HBM if i...  21.6 us
    ppermute x4, starting transfers between devices, fetch_half(): blocks.append(lax.ppermute(chip_rows, 'col', pairs))  10.3 us
    ppermute x14, starting transfers between devices, swap(): lax.ppermute(value, 'col', [(i, i ^ masks[i % 2]) for i in range(n) if ma...  9.19 us
    ppermute x14, waiting for transfers between devices, swap(): lax.ppermute(value, 'col', [(i, i ^ masks[i % 2]) for i in range(n) if ma...  9.18 us
    ppermute x4, waiting for transfers between devices, fetch_half(): blocks.append(lax.ppermute(chip_rows, 'col', pairs))  4.5 us
  transfers between devices with their start and end apart: 18, of which 9 were waited for; matrix products, arithmetic and copies ran while one was open for 0% of the time, Pallas kernels for 31%

profile of v7, /device:TPU:0, one launch (start us, length us, event | category | flops | bytes accessed | tf_op | source)
XLA Modules:
  0.0 57.1 jit_solution(3664265383375271696)
XLA Ops:
  0.6 0.0 copy-start
  0.6 0.5 collective-permute-start
  1.2 1.0 %collective-permute-done = bf16[16,256]{1,0:T(8,128)(2,1)S(1)} collective-permute-done((bf16[16,256]{1,0:T(8,128)(2,1)}, bf16[16,256]{1,0:T(8,128)(2,1)S(1)}, u32[]{:S(2)}, u32[]{:S(2)}) %collective-permute-start) | collective-permute-done | bytes 8224 | tf_op jit(solution)/shard_map/ppermute | solution.py:537
  2.2 0.0 copy-done
  2.2 5.6 %collective-permute-start.1 = (bf16[32,256]{1,0:T(8,128)(2,1)S(1)}, bf16[32,256]{1,0:T(8,128)(2,1)S(1)}, u32[]{:S(2)}, u32[]{:S(2)}) collective-permute-start(bf16[32,256]{1,0:T(8,128)(2,1)S(1)} %maximum_select_fusion.2), channel_id=1, source_target_pairs={{9,0},{11,2},{13,4},{15,6},{0,9},{2,11},{4,13},{6,15},{25,16},{27,... | collective-permute-start | bytes 49160 | tf_op jit(solution)/shard_map/ppermute | solution.py:551
  8.5 1.3 %collective-permute-start.2 = (bf16[32,256]{1,0:T(8,128)(2,1)S(1)}, bf16[32,256]{1,0:T(8,128)(2,1)S(1)}, u32[]{:S(2)}, u32[]{:S(2)}) collective-permute-start(bf16[32,256]{1,0:T(8,128)(2,1)S(1)} %maximum_select_fusion.2), channel_id=1, source_target_pairs={{11,0},{3,1},{9,2},{1,3},{15,4},{7,5},{13,6},{5,7},{10,8},{2,9},{8... | collective-permute-start | bytes 49160 | tf_op jit(solution)/shard_map/ppermute | solution.py:551
  9.8 3.4 %collective-permute-start.3 = (bf16[32,256]{1,0:T(8,128)(2,1)S(1)}, bf16[32,256]{1,0:T(8,128)(2,1)S(1)}, u32[]{:S(2)}, u32[]{:S(2)}) collective-permute-start(bf16[32,256]{1,0:T(8,128)(2,1)S(1)} %maximum_select_fusion.2), channel_id=1, source_target_pairs={{13,0},{5,1},{15,2},{7,3},{9,4},{1,5},{11,6},{3,7},{12,8},{4,9},{1... | collective-permute-start | bytes 49160 | tf_op jit(solution)/shard_map/ppermute | solution.py:551
  13.2 0.0 collective-permute-start.4
  13.2 1.3 %shard_map.113 = (s32[2,12]{1,0:T(2,128)S(1)}, s32[8,12]{1,0:T(8,128)S(1)}, f32[1,12]{1,0:T(1,128)S(1)}, f32[1,8]{1,0:T(1,128)S(1)}, f32[512,256]{1,0:T(8,128)S(...) custom-call(s32[2,12]{1,0:T(2,128)} %bitcast.42, s32[8,12]{1,0:T(8,128)} %bitcast.24, ...), custom_call_target="tpu_custom_call" | custom-call | tf_op jit(solution)/shard_map/pallas_call | solution.py:519
  14.5 0.0 collective-permute-done.1
  14.5 0.0 collective-permute-done.2
  14.5 0.2 collective-permute-done.3
  14.8 4.3 %collective-permute-done.4 = bf16[32,256]{1,0:T(8,128)(2,1)S(1)} collective-permute-done((bf16[32,256]{1,0:T(8,128)(2,1)S(1)}, bf16[32,256]{1,0:T(8,128)(2,1)S(1)}, u32[]{:S(2)}, u32[]{:S(2)}) %collective-permute-start.4) | collective-permute-done | bytes 16416 | tf_op jit(solution)/shard_map/ppermute | solution.py:551
  19.0 0.1 collective-permute-start.5
  19.1 1.3 %shard_map.114 = (bf16[512,128]{1,0:T(8,128)(2,1)S(1)}, f32[128,256]{1,0:T(8,128)S(1)}, f32[8,256]{1,0:T(8,128)S(1)}) custom-call(s32[2,12]{1,0:T(2,128)S(1)} %get-tuple-element.122.pair_in_ref, s32[8,12]{1,0:T(8,128)S(1)} %get-tuple-element.123.stoich_in_ref, f32[1,12]{1,0:T(1,128)S(1)} %get-tuple-element.124.speed_in_ref, ...), custom_call_target="tpu_custom_call" | custom-call | tf_op jit(solution)/shard_map/pallas_call | solution.py:519
  20.4 0.0 collective-permute-done.5.refs_1_
  20.4 0.6 collective-permute-start.6
  21.0 1.3 %shard_map.115 = (bf16[512,128]{1,0:T(8,128)(2,1)S(1)}, f32[128,256]{1,0:T(8,128)S(1)}, f32[8,256]{1,0:T(8,128)S(1)}, bf16[256,256]{1,0:T(8,128)(2,1)S(1)}) custom-call(s32[2,12]{1,0:T(2,128)S(1)} %get-tuple-element.122.pair_in_ref, s32[8,12]{1,0:T(8,128)S(1)} %get-tuple-element.123.stoich_in_ref, f32[1,12]{1,0:T(1,128)S(1)} %get-tuple-element.124.speed_in_ref, ...), custom_call_target="tpu_custom_call" | custom-call | tf_op jit(solution)/shard_map/pallas_call | solution.py:519
  22.3 0.0 collective-permute-done.6
  22.4 0.6 collective-permute-start.7
  22.9 0.0 collective-permute-start.8
  22.9 3.0 %collective-permute-start.9 = (f16[136,256]{1,0:T(8,128)(2,1)S(1)}, f16[136,256]{1,0:T(8,128)(2,1)S(1)}, u32[]{:S(2)}, u32[]{:S(2)}) collective-permute-start(f16[136,256]{1,0:T(8,128)(2,1)S(1)} %pad_maximum_fusion.2), channel_id=1, source_target_pairs={{0,6},{1,7},{2,4},{3,5},{4,2},{5,3},{6,0},{7,1},{8,14},{9,15},{10,... | collective-permute-start | bytes 208904 | tf_op jit(solution)/shard_map/ppermute | solution.py:537
  25.9 3.2 %shard_map.116 = (bf16[256,256]{1,0:T(8,128)(2,1)S(1)}, bf16[256,256]{1,0:T(8,128)(2,1)S(1)}, f32[256,256]{1,0:T(8,128)S(1)}, f32[8,256]{1,0:T(8,128)S(1)}) custom-call(bf16[256,256]{1,0:T(8,128)(2,1)S(1)} %get-tuple-element.186.coef_ref), custom_call_target="tpu_custom_call" | custom-call | tf_op jit(solution)/shard_map/pallas_call | solution.py:519
  29.1 0.0 collective-permute-done.7
  29.1 0.0 collective-permute-done.8
  29.1 0.1 collective-permute-done.9
  29.3 0.1 multiply_convert_fusion.2
  29.4 0.1 collective-permute-start.10
  29.5 3.0 %shard_map.117 = (f32[256,256]{1,0:T(8,128)S(1)}, f32[512,256]{1,0:T(8,128)S(1)}) custom-call(f32[8,256]{1,0:T(8,128)S(1)} %get-tuple-element.160.gap_in_ref, bf16[256,256]{1,0:T(8,128)(2,1)S(1)} %get-tuple-element.161.high_ref, bf16[256,256]{1,0:T(8,128)(2,1)S(1)} %get-tuple-element.162.low_ref, f32[256,256]{1,0:T(8,128)S(1)} %get-tuple-element.163.inv_in_ref, ...), custom_call_target="tpu_custom_call" | custom-call | tf_op jit(solution)/shard_map/pallas_call | solution.py:519
  32.5 2.9 %collective-permute-done.10 = f16[136,256]{1,0:T(8,128)(2,1)S(1)} collective-permute-done((f16[136,256]{1,0:T(8,128)(2,1)S(1)}, f16[136,256]{1,0:T(8,128)(2,1)S(1)}, u32[]{:S(2)}, u32[]{:S(2)}) %collective-permute-start.10) | collective-permute-done | bytes 69664 | tf_op jit(solution)/shard_map/ppermute | solution.py:537
  35.5 0.1 collective-permute-start.11
  35.6 0.2 shard_map.118
  35.7 1.2 %collective-permute-done.11 = f32[128,256]{1,0:T(8,128)S(1)} collective-permute-done((f32[128,256]{1,0:T(8,128)S(1)}, f32[128,256]{1,0:T(8,128)S(1)}, u32[]{:S(2)}, u32[]{:S(2)}) %collective-permute-start.11) | collective-permute-done | bytes 131104 | tf_op jit(solution)/shard_map/ppermute | solution.py:537
  36.9 2.2 %shard_map.119 = (f32[512,256]{1,0:T(8,128)S(1)}, bf16[512,128]{1,0:T(8,128)(2,1)S(1)}, f32[128,256]{1,0:T(8,128)S(1)}, f32[8,256]{1,0:T(8,128)S(1)}, bf16[256,256]{1,0:T(8,128)(2,1)S(1)}) custom-call(s32[2,12]{1,0:T(2,128)S(1)} %get-tuple-element.122.pair_in_ref, s32[8,12]{1,0:T(8,128)S(1)} %get-tuple-element.123.stoich_in_ref, ...), custom_call_target="tpu_custom_call" | custom-call | tf_op jit(solution)/shard_map/pallas_call | solution.py:519
  39.2 0.2 collective-permute-start.12
  39.4 1.3 %shard_map.120 = (bf16[512,128]{1,0:T(8,128)(2,1)S(1)}, f32[128,256]{1,0:T(8,128)S(1)}, f32[8,256]{1,0:T(8,128)S(1)}) custom-call(s32[2,12]{1,0:T(2,128)S(1)} %get-tuple-element.122.pair_in_ref, s32[8,12]{1,0:T(8,128)S(1)} %get-tuple-element.123.stoich_in_ref, f32[1,12]{1,0:T(1,128)S(1)} %get-tuple-element.124.speed_in_ref, ...), custom_call_target="tpu_custom_call" | custom-call | tf_op jit(solution)/shard_map/pallas_call | solution.py:519
  40.6 0.0 collective-permute-done.12
  40.8 0.1 collective-permute-start.13
  40.8 1.7 %collective-permute-start.14 = (f16[136,256]{1,0:T(8,128)(2,1)S(1)}, f16[136,256]{1,0:T(8,128)(2,1)S(1)}, u32[]{:S(2)}, u32[]{:S(2)}) collective-permute-start(f16[136,256]{1,0:T(8,128)(2,1)S(1)} %pad_maximum_fusion.4), channel_id=1, source_target_pairs={{0,4},{1,5},{2,6},{3,7},{4,0},{5,1},{6,2},{7,3},{8,12},{9,13},{10,... | collective-permute-start | bytes 208904 | tf_op jit(solution)/shard_map/ppermute | solution.py:537
  42.5 1.8 %collective-permute-start.15 = (f16[136,256]{1,0:T(8,128)(2,1)S(1)}, f16[136,256]{1,0:T(8,128)(2,1)S(1)}, u32[]{:S(2)}, u32[]{:S(2)}) collective-permute-start(f16[136,256]{1,0:T(8,128)(2,1)S(1)} %pad_maximum_fusion.4), channel_id=1, source_target_pairs={{0,6},{1,7},{2,4},{3,5},{4,2},{5,3},{6,0},{7,1},{8,14},{9,15},{10,... | collective-permute-start | bytes 208904 | tf_op jit(solution)/shard_map/ppermute | solution.py:537
  44.3 3.2 %shard_map.121 = (bf16[256,256]{1,0:T(8,128)(2,1)S(1)}, bf16[256,256]{1,0:T(8,128)(2,1)S(1)}, f32[256,256]{1,0:T(8,128)S(1)}, f32[8,256]{1,0:T(8,128)S(1)}) custom-call(bf16[256,256]{1,0:T(8,128)(2,1)S(1)} %get-tuple-element.239.refs_0_.coef_ref), custom_call_target="tpu_custom_call" | custom-call | tf_op jit(solution)/shard_map/pallas_call | solution.py:519
  47.5 0.0 collective-permute-done.13
  47.5 0.0 collective-permute-done.14
  47.5 0.5 collective-permute-done.15
  48.1 0.1 multiply_convert_fusion
  48.2 0.5 collective-permute-start.16
  48.7 3.0 %shard_map.122 = (f32[256,256]{1,0:T(8,128)S(1)}, f32[512,256]{1,0:T(8,128)S(1)}) custom-call(f32[8,256]{1,0:T(8,128)S(1)} %get-tuple-element.213.gap_in_ref, bf16[256,256]{1,0:T(8,128)(2,1)S(1)} %get-tuple-element.214.high_ref, bf16[256,256]{1,0:T(8,128)(2,1)S(1)} %get-tuple-element.215.low_ref, f32[256,256]{1,0:T(8,128)S(1)} %get-tuple-element.216.inv_in_ref, ...), custom_call_target="tpu_custom_call" | custom-call | tf_op jit(solution)/shard_map/pallas_call | solution.py:519
  51.7 2.2 %collective-permute-done.16 = f16[136,256]{1,0:T(8,128)(2,1)S(1)} collective-permute-done((f16[136,256]{1,0:T(8,128)(2,1)S(1)}, f16[136,256]{1,0:T(8,128)(2,1)S(1)}, u32[]{:S(2)}, u32[]{:S(2)}) %collective-permute-start.16) | collective-permute-done | bytes 69664 | tf_op jit(solution)/shard_map/ppermute | solution.py:537
  54.0 0.1 collective-permute-start.17
  54.1 0.2 shard_map.123
  54.3 1.2 %collective-permute-done.17 = f32[128,256]{1,0:T(8,128)S(1)} collective-permute-done((f32[128,256]{1,0:T(8,128)S(1)}, f32[128,256]{1,0:T(8,128)S(1)}, u32[]{:S(2)}, u32[]{:S(2)}) %collective-permute-start.17) | collective-permute-done | bytes 131104 | tf_op jit(solution)/shard_map/ppermute | solution.py:537
  55.5 1.6 %shard_map.124 = (f32[512,256]{1,0:T(8,128)}, bf16[16,256]{1,0:T(8,128)(2,1)}) custom-call(f32[512,256]{1,0:T(8,128)S(1)} %get-tuple-element.233.base_ref, bf16[512,256]{1,0:T(8,128)(2,1)S(1)} %get-tuple-element.234.diff_high_ref, bf16[512,256]{1,0:T(8,128)(2,1)S(1)} %get-tuple-element.235.diff_low_ref, bf16[256,256]{1,0:T(8,128)(2,1)S(1)} %get-tuple-element.236.high_ref, ...), custom_call_target="tpu_custom_call" | custom-call | tf_op jit(solution)/shard_map/pallas_call | solution.py:519
  (34 shorter events, 0.5 us)
Async XLA Ops:
  0.6 1.6 %copy-start = (bf16[16,256]{1,0:T(8,128)(2,1)S(1)}, bf16[16,256]{1,0:T(8,128)(2,1)}, u32[]{:S(2)}) copy-start(bf16[16,256]{1,0:T(8,128)(2,1)} %param.11) | copy-start | bytes 24580
  0.6 1.6 %collective-permute-start = (bf16[16,256]{1,0:T(8,128)(2,1)}, bf16[16,256]{1,0:T(8,128)(2,1)S(1)}, u32[]{:S(2)}, u32[]{:S(2)}) collective-permute-start(bf16[16,256]{1,0:T(8,128)(2,1)} %param.11), channel_id=1, source_target_pairs={{0,1},{1,0},{2,3},{3,2},{4,5},{5,4},{6,7},{7,6},{8,9},{9,8},{10,11... | collective-permute-start | bytes 24584 | tf_op jit(solution)/shard_map/ppermute | solution.py:537
  2.2 12.3 %collective-permute-start.1 = (bf16[32,256]{1,0:T(8,128)(2,1)S(1)}, bf16[32,256]{1,0:T(8,128)(2,1)S(1)}, u32[]{:S(2)}, u32[]{:S(2)}) collective-permute-start(bf16[32,256]{1,0:T(8,128)(2,1)S(1)} %maximum_select_fusion.2), channel_id=1, source_target_pairs={{9,0},{11,2},{13,4},{15,6},{0,9},{2,11},{4,13},{6,15},{25,16},{27,... | collective-permute-start | bytes 49160 | tf_op jit(solution)/shard_map/ppermute | solution.py:551
  8.5 6.0 %collective-permute-start.2 = (bf16[32,256]{1,0:T(8,128)(2,1)S(1)}, bf16[32,256]{1,0:T(8,128)(2,1)S(1)}, u32[]{:S(2)}, u32[]{:S(2)}) collective-permute-start(bf16[32,256]{1,0:T(8,128)(2,1)S(1)} %maximum_select_fusion.2), channel_id=1, source_target_pairs={{11,0},{3,1},{9,2},{1,3},{15,4},{7,5},{13,6},{5,7},{10,8},{2,9},{8... | collective-permute-start | bytes 49160 | tf_op jit(solution)/shard_map/ppermute | solution.py:551
  9.8 5.0 %collective-permute-start.3 = (bf16[32,256]{1,0:T(8,128)(2,1)S(1)}, bf16[32,256]{1,0:T(8,128)(2,1)S(1)}, u32[]{:S(2)}, u32[]{:S(2)}) collective-permute-start(bf16[32,256]{1,0:T(8,128)(2,1)S(1)} %maximum_select_fusion.2), channel_id=1, source_target_pairs={{13,0},{5,1},{15,2},{7,3},{9,4},{1,5},{11,6},{3,7},{12,8},{4,9},{1... | collective-permute-start | bytes 49160 | tf_op jit(solution)/shard_map/ppermute | solution.py:551
  13.2 5.9 %collective-permute-start.4 = (bf16[32,256]{1,0:T(8,128)(2,1)S(1)}, bf16[32,256]{1,0:T(8,128)(2,1)S(1)}, u32[]{:S(2)}, u32[]{:S(2)}) collective-permute-start(bf16[32,256]{1,0:T(8,128)(2,1)S(1)} %maximum_select_fusion.2), channel_id=1, source_target_pairs={{15,0},{7,1},{13,2},{5,3},{11,4},{3,5},{9,6},{1,7},{14,8},{6,9},{1... | collective-permute-start | bytes 49160 | tf_op jit(solution)/shard_map/ppermute | solution.py:551
  19.0 1.4 %collective-permute-start.5 = (bf16[128,256]{1,0:T(8,128)(2,1)S(1)}, bf16[128,256]{1,0:T(8,128)(2,1)S(1)}, u32[]{:S(2)}, u32[]{:S(2)}) collective-permute-start(bf16[128,256]{1,0:T(8,128)(2,1)S(1)} %constant_dynamic-update-slice_fusion.coef_in_ref.refs_0_), channel_id=1, source_target_pairs={{0,1},{1,0},{2,3},{3,2},{4,5},{5,4},{6,7},{7,6},{8,9},{9,8},{10,11... | collective-permute-start | bytes 196616 | tf_op jit(solution)/shard_map/ppermute | solution.py:537
  20.4 1.8 %collective-permute-start.6 = (f32[136,256]{1,0:T(8,128)S(1)}, f32[136,256]{1,0:T(8,128)S(1)}, u32[]{:S(2)}, u32[]{:S(2)}) collective-permute-start(f32[136,256]{1,0:T(8,128)S(1)} %pad_maximum_fusion), channel_id=1, source_target_pairs={{0,1},{1,0},{2,3},{3,2},{4,5},{5,4},{6,7},{7,6},{8,9},{9,8},{10,11... | collective-permute-start | bytes 417800 | tf_op jit(solution)/shard_map/ppermute | solution.py:537
  22.4 6.7 %collective-permute-start.7 = (f16[136,256]{1,0:T(8,128)(2,1)S(1)}, f16[136,256]{1,0:T(8,128)(2,1)S(1)}, u32[]{:S(2)}, u32[]{:S(2)}) collective-permute-start(f16[136,256]{1,0:T(8,128)(2,1)S(1)} %pad_maximum_fusion.2), channel_id=1, source_target_pairs={{0,2},{1,3},{2,0},{3,1},{4,6},{5,7},{6,4},{7,5},{8,10},{9,11},{10,... | collective-permute-start | bytes 208904 | tf_op jit(solution)/shard_map/ppermute | solution.py:537
  22.9 6.2 %collective-permute-start.8 = (f16[136,256]{1,0:T(8,128)(2,1)S(1)}, f16[136,256]{1,0:T(8,128)(2,1)S(1)}, u32[]{:S(2)}, u32[]{:S(2)}) collective-permute-start(f16[136,256]{1,0:T(8,128)(2,1)S(1)} %pad_maximum_fusion.2), channel_id=1, source_target_pairs={{0,4},{1,5},{2,6},{3,7},{4,0},{5,1},{6,2},{7,3},{8,12},{9,13},{10,... | collective-permute-start | bytes 208904 | tf_op jit(solution)/shard_map/ppermute | solution.py:537
  22.9 6.3 %collective-permute-start.9 = (f16[136,256]{1,0:T(8,128)(2,1)S(1)}, f16[136,256]{1,0:T(8,128)(2,1)S(1)}, u32[]{:S(2)}, u32[]{:S(2)}) collective-permute-start(f16[136,256]{1,0:T(8,128)(2,1)S(1)} %pad_maximum_fusion.2), channel_id=1, source_target_pairs={{0,6},{1,7},{2,4},{3,5},{4,2},{5,3},{6,0},{7,1},{8,14},{9,15},{10,... | collective-permute-start | bytes 208904 | tf_op jit(solution)/shard_map/ppermute | solution.py:537
  29.4 6.0 %collective-permute-start.10 = (f16[136,256]{1,0:T(8,128)(2,1)S(1)}, f16[136,256]{1,0:T(8,128)(2,1)S(1)}, u32[]{:S(2)}, u32[]{:S(2)}) collective-permute-start(f16[136,256]{1,0:T(8,128)(2,1)S(1)} %pad_maximum_fusion.3), channel_id=1, source_target_pairs={{0,8},{1,9},{2,10},{3,11},{4,12},{5,13},{6,14},{7,15},{8,0},{9,1},... | collective-permute-start | bytes 208904 | tf_op jit(solution)/shard_map/ppermute | solution.py:537
  35.5 1.4 %collective-permute-start.11 = (f32[128,256]{1,0:T(8,128)S(1)}, f32[128,256]{1,0:T(8,128)S(1)}, u32[]{:S(2)}, u32[]{:S(2)}) collective-permute-start(f32[128,256]{1,0:T(8,128)S(1)} %multiply_add_fusion.1), channel_id=1, source_target_pairs={{0,1},{1,0},{2,3},{3,2},{4,5},{5,4},{6,7},{7,6},{8,9},{9,8},{10,11... | collective-permute-start | bytes 393224 | tf_op jit(solution)/shard_map/ppermute | solution.py:537
  39.2 1.5 %collective-permute-start.12 = (f32[136,256]{1,0:T(8,128)S(1)}, f32[136,256]{1,0:T(8,128)S(1)}, u32[]{:S(2)}, u32[]{:S(2)}) collective-permute-start(f32[136,256]{1,0:T(8,128)S(1)} %pad_maximum_fusion.1), channel_id=1, source_target_pairs={{0,1},{1,0},{2,3},{3,2},{4,5},{5,4},{6,7},{7,6},{8,9},{9,8},{10,11... | collective-permute-start | bytes 417800 | tf_op jit(solution)/shard_map/ppermute | solution.py:537
  40.8 6.8 %collective-permute-start.13 = (f16[136,256]{1,0:T(8,128)(2,1)S(1)}, f16[136,256]{1,0:T(8,128)(2,1)S(1)}, u32[]{:S(2)}, u32[]{:S(2)}) collective-permute-start(f16[136,256]{1,0:T(8,128)(2,1)S(1)} %pad_maximum_fusion.4), channel_id=1, source_target_pairs={{0,2},{1,3},{2,0},{3,1},{4,6},{5,7},{6,4},{7,5},{8,10},{9,11},{10,... | collective-permute-start | bytes 208904 | tf_op jit(solution)/shard_map/ppermute | solution.py:537
  40.8 6.7 %collective-permute-start.14 = (f16[136,256]{1,0:T(8,128)(2,1)S(1)}, f16[136,256]{1,0:T(8,128)(2,1)S(1)}, u32[]{:S(2)}, u32[]{:S(2)}) collective-permute-start(f16[136,256]{1,0:T(8,128)(2,1)S(1)} %pad_maximum_fusion.4), channel_id=1, source_target_pairs={{0,4},{1,5},{2,6},{3,7},{4,0},{5,1},{6,2},{7,3},{8,12},{9,13},{10,... | collective-permute-start | bytes 208904 | tf_op jit(solution)/shard_map/ppermute | solution.py:537
  42.5 5.5 %collective-permute-start.15 = (f16[136,256]{1,0:T(8,128)(2,1)S(1)}, f16[136,256]{1,0:T(8,128)(2,1)S(1)}, u32[]{:S(2)}, u32[]{:S(2)}) collective-permute-start(f16[136,256]{1,0:T(8,128)(2,1)S(1)} %pad_maximum_fusion.4), channel_id=1, source_target_pairs={{0,6},{1,7},{2,4},{3,5},{4,2},{5,3},{6,0},{7,1},{8,14},{9,15},{10,... | collective-permute-start | bytes 208904 | tf_op jit(solution)/shard_map/ppermute | solution.py:537
  48.2 5.8 %collective-permute-start.16 = (f16[136,256]{1,0:T(8,128)(2,1)S(1)}, f16[136,256]{1,0:T(8,128)(2,1)S(1)}, u32[]{:S(2)}, u32[]{:S(2)}) collective-permute-start(f16[136,256]{1,0:T(8,128)(2,1)S(1)} %pad_maximum_fusion.5), channel_id=1, source_target_pairs={{0,8},{1,9},{2,10},{3,11},{4,12},{5,13},{6,14},{7,15},{8,0},{9,1},... | collective-permute-start | bytes 208904 | tf_op jit(solution)/shard_map/ppermute | solution.py:537
  54.0 1.4 %collective-permute-start.17 = (f32[128,256]{1,0:T(8,128)S(1)}, f32[128,256]{1,0:T(8,128)S(1)}, u32[]{:S(2)}, u32[]{:S(2)}) collective-permute-start(f32[128,256]{1,0:T(8,128)S(1)} %multiply_add_fusion), channel_id=1, source_target_pairs={{0,1},{1,0},{2,3},{3,2},{4,5},{5,4},{6,7},{7,6},{8,9},{9,8},{10,11... | collective-permute-start | bytes 393224 | tf_op jit(solution)/shard_map/ppermute | solution.py:537

commit v8 on v6

--- a/solution.py
+++ b/solution.py
@@ -124,8 +124,8 @@
     columns,
     pair_hbm, stoich_hbm, speed_hbm, loss_hbm, table_hbm, level_face_hbm, idx_hbm, modes_hbm,
     counts_ref,
-    pair_ref, stoich_ref, speed_ref, loss_ref, modes_ref, emis_ref, face_ref, live_ref,
-    table_ref, level_face_ref, idx_ref, sems,
+    pair_ref, stoich_ref, speed_ref, loss_ref, diff_ref, emis_ref, face_ref, live_ref,
+    table_ref, level_face_ref, idx_ref, modes_ref, sems,
 ):
     later = fetch(
         (pair_hbm, stoich_hbm, speed_hbm, loss_hbm, modes_hbm),
@@ -152,9 +152,6 @@
         face_ref[part, :] = jnp.broadcast_to(face, (LEV, R))
         live_ref[part, :] = jnp.where(level < count, 1.0, 0.0)
     later()
-
-
-def diffuse_kernel(modes_ref, face_ref, diff_ref):
     diff_ref[...] = diffuse_rows(modes_ref[...], face_ref)
 
 
@@ -436,7 +433,7 @@
     def stage(modes):
         by_level = ((columns * LEV, R), F32)
         index = emis_idx.reshape(1, members)
-        *chem, modes, emis, face, live = call(
+        *chem, diff, emis, face, live = call(
             functools.partial(stage_kernel, columns), 8,
             [(value.shape, value.dtype) for value in tables]
             + [rows_f32, ((S, members), F32), by_level, by_level],
@@ -444,29 +441,25 @@
                 pltpu.SMEM((S, NEMIS), F32),
                 pltpu.VMEM(diffusivity.shape, F32),
                 pltpu.VMEM((1, members), jnp.int32),
+                pltpu.VMEM((rows, R), F32),
                 pltpu.SemaphoreType.DMA((8,)),
             ],
             *tables, emis_table.T, diffusivity, index, modes, counts.reshape(1, columns),
         )
-        return chem, modes, emis, face, live
-
-    def spread(modes, face):
-        return call(diffuse_kernel, 0, [rows_f32], [], modes, face)[0]
+        return chem, diff, emis, face, live
 
     if n == 16:
-        plan = ((1, 2), (4, 3), (5, 6), (0, 7))
+        plan = ((1, 1), (2, 3), (4, 6), (5, 7))
         other = swap(coeffs, n, (1, 1))
         side = lax.axis_index("col") & 1
         chip = jnp.where(
             side == 0, jnp.concatenate([coeffs, other], 0), jnp.concatenate([other, coeffs], 0)
         )
         fetched = [swap(chip, n, (2 * a, 2 * b)) for a, b in plan]
-        chem, modes, emis, face, live = stage(tied(mode_rows, chip))
-        fetched, modes = lax.optimization_barrier((fetched, modes))
+        chem, diff, emis, face, live = stage(tied(mode_rows, chip))
+        fetched, diff = lax.optimization_barrier((fetched, diff))
         mine_rows = jnp.concatenate(fetched, 0)
         theirs = swap(mine_rows, n, (1, 1))
-        diff = spread(tied(modes, mine_rows), face)
-        theirs, diff = lax.optimization_barrier((theirs, diff))
         gathered = (chip, mine_rows, theirs)
         tend, rate, top, coef = call(
             functools.partial(first_kernel, plan), 0,
@@ -475,8 +468,7 @@
         )
     else:
         coef = lax.all_to_all(jnp.tile(coeffs, (n, 1)), "col", 0, 0, tiled=True)
-        chem, modes, emis, face, live = stage(mode_rows)
-        diff = spread(modes, face)
+        chem, diff, emis, face, live = stage(mode_rows)
         tend, rate, top = call(
             functools.partial(first_kernel, ()), 0,
             [tend_out, half_out, top_out], react_tmp,

time: 53.1 us -> 52.1 us (0.981)
  starting transfers between devices: 21.1 us -> 20.1 us
    ppermute x18, starting transfers between devices: 21.1 us -> 20.1 us  [swap(): lax.ppermute(value, 'col', [(i, i ^ masks[i % 2]) for i in range(n) if ma...]
    pallas_call x13 -> x12, Pallas kernels: 21.6 us -> 21.6 us  [call(): pl.pallas_call(kernel, in_specs=[pl.BlockSpec(memory_space=pltpu.HBM if i...]
  transfers between devices with their start and end apart: 18 -> 18, of which waited for: 8 -> 10; matrix products, arithmetic and copies ran while one was open for 0% -> 0% of each run, Pallas kernels for 31% -> 32%
where the time goes in v8:
time: 52.1 us; the launch traced here: 51.9 us
  Pallas kernels  21.6 us (41%)
  starting transfers between devices  20.1 us (39%)
  waiting for transfers between devices  8.06 us (15%)
  between operations  1.6 us (3%)
  other arithmetic  0.58 us (1%)
    pallas_call x12, Pallas kernels, call(): pl.pallas_call(kernel, in_specs=[pl.BlockSpec(memory_space=pltpu.HBM if i...  21.6 us
    ppermute x18, starting transfers between devices, swap(): lax.ppermute(value, 'col', [(i, i ^ masks[i % 2]) for i in range(n) if ma...  20.1 us
    ppermute x18, waiting for transfers between devices, swap(): lax.ppermute(value, 'col', [(i, i ^ masks[i % 2]) for i in range(n) if ma...  8.06 us
  transfers between devices with their start and end apart: 18, of which 10 were waited for; matrix products, arithmetic and copies ran while one was open for 0% of the time, Pallas kernels for 32%

profile of v8, /device:TPU:0, one launch (start us, length us, event | category | flops | bytes accessed | tf_op | source)
XLA Modules:
  0.0 51.9 jit_solution(17063347653428585280)
XLA Ops:
  0.6 0.0 copy-start
  0.6 0.5 collective-permute-start
  1.2 1.0 %collective-permute-done = bf16[16,256]{1,0:T(8,128)(2,1)S(1)} collective-permute-done((bf16[16,256]{1,0:T(8,128)(2,1)}, bf16[16,256]{1,0:T(8,128)(2,1)S(1)}, u32[]{:S(2)}, u32[]{:S(2)}) %collective-permute-start) | collective-permute-done | bytes 8224 | tf_op jit(solution)/shard_map/ppermute | solution.py:342
  2.2 0.0 copy-done
  2.2 5.0 %collective-permute-start.4 = (bf16[32,256]{1,0:T(8,128)(2,1)S(1)}, bf16[32,256]{1,0:T(8,128)(2,1)S(1)}, u32[]{:S(2)}, u32[]{:S(2)}) collective-permute-start(bf16[32,256]{1,0:T(8,128)(2,1)S(1)} %maximum_select_fusion.2.allrefs_7_), channel_id=1, source_target_pairs={{0,10},{1,15},{2,8},{3,13},{4,14},{5,11},{6,12},{7,9},{8,2},{9,7},... | collective-permute-start | bytes 49160 | tf_op jit(solution)/shard_map/ppermute | solution.py:342
  7.2 0.3 collective-permute-start.3
  7.5 1.6 %collective-permute-start.2 = (bf16[32,256]{1,0:T(8,128)(2,1)S(1)}, bf16[32,256]{1,0:T(8,128)(2,1)S(1)}, u32[]{:S(2)}, u32[]{:S(2)}) collective-permute-start(bf16[32,256]{1,0:T(8,128)(2,1)S(1)} %maximum_select_fusion.2.allrefs_7_), channel_id=1, source_target_pairs={{0,4},{1,7},{2,6},{3,5},{4,0},{5,3},{6,2},{7,1},{8,12},{9,15},{10,... | collective-permute-start | bytes 49160 | tf_op jit(solution)/shard_map/ppermute | solution.py:342
  9.1 0.5 collective-permute-start.1
  10.2 1.3 %shard_map.113 = (s32[2,12]{1,0:T(2,128)S(1)}, s32[8,12]{1,0:T(8,128)S(1)}, f32[1,12]{1,0:T(1,128)S(1)}, f32[1,8]{1,0:T(1,128)S(1)}, f32[512,256]{1,0:T(8,128)S(...) custom-call(s32[2,12]{1,0:T(2,128)} %bitcast.42, s32[8,12]{1,0:T(8,128)} %bitcast.24, ...), custom_call_target="tpu_custom_call" | custom-call | tf_op jit(solution)/shard_map/pallas_call | solution.py:324
  11.6 0.0 collective-permute-done.4
  11.6 0.2 collective-permute-done.3
  11.8 0.0 collective-permute-done.2
  11.8 1.0 %collective-permute-done.1 = bf16[32,256]{1,0:T(8,128)(2,1)S(1)} collective-permute-done((bf16[32,256]{1,0:T(8,128)(2,1)S(1)}, bf16[32,256]{1,0:T(8,128)(2,1)S(1)}, u32[]{:S(2)}, u32[]{:S(2)}) %collective-permute-start.1) | collective-permute-done | bytes 16416 | tf_op jit(solution)/shard_map/ppermute | solution.py:342
  12.8 0.1 collective-permute-start.5
  12.9 1.2 %collective-permute-done.5.allrefs_9_ = bf16[128,256]{1,0:T(8,128)(2,1)S(1)} collective-permute-done((bf16[128,256]{1,0:T(8,128)(2,1)S(1)}, bf16[128,256]{1,0:T(8,128)(2,1)S(1)}, u32[]{:S(2)}, u32[]{:S(2)}) %collective-permute-start.5) | collective-permute-done | bytes 65568 | tf_op jit(solution)/shard_map/ppermute | solution.py:342
  14.2 1.3 %shard_map.114 = (bf16[512,128]{1,0:T(8,128)(2,1)S(1)}, f32[128,256]{1,0:T(8,128)S(1)}, f32[8,256]{1,0:T(8,128)S(1)}, bf16[256,256]{1,0:T(8,128)(2,1)S(1)}) custom-call(s32[2,12]{1,0:T(2,128)S(1)} %get-tuple-element.110.allrefs_0_.pair_in_ref, s32[8,12]{1,0:T(8,128)S(1)} %get-tuple-element.111.allrefs_1_.stoich_in_ref, ...), custom_call_target="tpu_custom_call" | custom-call | tf_op jit(solution)/shard_map/pallas_call | solution.py:324
  15.4 0.2 collective-permute-start.6
  15.7 1.2 %shard_map.115 = (bf16[512,128]{1,0:T(8,128)(2,1)S(1)}, f32[128,256]{1,0:T(8,128)S(1)}, f32[8,256]{1,0:T(8,128)S(1)}) custom-call(s32[2,12]{1,0:T(2,128)S(1)} %get-tuple-element.110.allrefs_0_.pair_in_ref, s32[8,12]{1,0:T(8,128)S(1)} %get-tuple-element.111.allrefs_1_.stoich_in_ref, f32[1,12]{1,0:T(1,128)S(1)} %get-tuple-element.112.allrefs_2_.speed_in_ref, ...), custom_call_target="tpu_custom_call" | custom-call | tf_op jit(solution)/shard_map/pallas_call | solution.py:324
  16.9 0.0 collective-permute-done.6
  17.0 0.8 %collective-permute-start.9 = (f16[136,256]{1,0:T(8,128)(2,1)S(1)}, f16[136,256]{1,0:T(8,128)(2,1)S(1)}, u32[]{:S(2)}, u32[]{:S(2)}) collective-permute-start(f16[136,256]{1,0:T(8,128)(2,1)S(1)} %pad_maximum_fusion.2), channel_id=1, source_target_pairs={{0,6},{1,7},{2,4},{3,5},{4,2},{5,3},{6,0},{7,1},{8,14},{9,15},{10,... | collective-permute-start | bytes 208904 | tf_op jit(solution)/shard_map/ppermute | solution.py:342
  17.8 1.3 %collective-permute-start.8 = (f16[136,256]{1,0:T(8,128)(2,1)S(1)}, f16[136,256]{1,0:T(8,128)(2,1)S(1)}, u32[]{:S(2)}, u32[]{:S(2)}) collective-permute-start(f16[136,256]{1,0:T(8,128)(2,1)S(1)} %pad_maximum_fusion.2), channel_id=1, source_target_pairs={{0,4},{1,5},{2,6},{3,7},{4,0},{5,1},{6,2},{7,3},{8,12},{9,13},{10,... | collective-permute-start | bytes 208904 | tf_op jit(solution)/shard_map/ppermute | solution.py:342
  19.1 1.5 %collective-permute-start.7 = (f16[136,256]{1,0:T(8,128)(2,1)S(1)}, f16[136,256]{1,0:T(8,128)(2,1)S(1)}, u32[]{:S(2)}, u32[]{:S(2)}) collective-permute-start(f16[136,256]{1,0:T(8,128)(2,1)S(1)} %pad_maximum_fusion.2), channel_id=1, source_target_pairs={{0,2},{1,3},{2,0},{3,1},{4,6},{5,7},{6,4},{7,5},{8,10},{9,11},{10,... | collective-permute-start | bytes 208904 | tf_op jit(solution)/shard_map/ppermute | solution.py:342
  20.6 3.2 %shard_map.116 = (bf16[256,256]{1,0:T(8,128)(2,1)S(1)}, bf16[256,256]{1,0:T(8,128)(2,1)S(1)}, f32[256,256]{1,0:T(8,128)S(1)}, f32[8,256]{1,0:T(8,128)S(1)}) custom-call(bf16[256,256]{1,0:T(8,128)(2,1)S(1)} %get-tuple-element.131.coef_ref), custom_call_target="tpu_custom_call" | custom-call | tf_op jit(solution)/shard_map/pallas_call | solution.py:324
  23.8 0.0 collective-permute-done.9
  23.8 0.0 collective-permute-done.8
  23.8 0.1 collective-permute-done.7
  24.0 0.1 multiply_convert_fusion.2
  24.1 2.7 %collective-permute-start.10 = (f16[136,256]{1,0:T(8,128)(2,1)S(1)}, f16[136,256]{1,0:T(8,128)(2,1)S(1)}, u32[]{:S(2)}, u32[]{:S(2)}) collective-permute-start(f16[136,256]{1,0:T(8,128)(2,1)S(1)} %pad_maximum_fusion.3), channel_id=1, source_target_pairs={{0,8},{1,9},{2,10},{3,11},{4,12},{5,13},{6,14},{7,15},{8,0},{9,1},... | collective-permute-start | bytes 208904 | tf_op jit(solution)/shard_map/ppermute | solution.py:342
  26.8 3.0 %shard_map.117 = (f32[256,256]{1,0:T(8,128)S(1)}, f32[512,256]{1,0:T(8,128)S(1)}) custom-call(f32[8,256]{1,0:T(8,128)S(1)} %get-tuple-element.144.gap_in_ref, bf16[256,256]{1,0:T(8,128)(2,1)S(1)} %get-tuple-element.145.high_ref, bf16[256,256]{1,0:T(8,128)(2,1)S(1)} %get-tuple-element.146.low_ref, f32[256,256]{1,0:T(8,128)S(1)} %get-tuple-element.147.inv_in_ref, ...), custom_call_target="tpu_custom_call" | custom-call | tf_op jit(solution)/shard_map/pallas_call | solution.py:324
  29.8 0.6 %collective-permute-done.10 = f16[136,256]{1,0:T(8,128)(2,1)S(1)} collective-permute-done((f16[136,256]{1,0:T(8,128)(2,1)S(1)}, f16[136,256]{1,0:T(8,128)(2,1)S(1)}, u32[]{:S(2)}, u32[]{:S(2)}) %collective-permute-start.10) | collective-permute-done | bytes 69664 | tf_op jit(solution)/shard_map/ppermute | solution.py:342
  30.4 0.1 collective-permute-start.11
  30.5 0.2 shard_map.118
  30.6 1.2 %collective-permute-done.11 = f32[128,256]{1,0:T(8,128)S(1)} collective-permute-done((f32[128,256]{1,0:T(8,128)S(1)}, f32[128,256]{1,0:T(8,128)S(1)}, u32[]{:S(2)}, u32[]{:S(2)}) %collective-permute-start.11) | collective-permute-done | bytes 131104 | tf_op jit(solution)/shard_map/ppermute | solution.py:342
  31.8 2.2 %shard_map.119 = (f32[512,256]{1,0:T(8,128)S(1)}, bf16[512,128]{1,0:T(8,128)(2,1)S(1)}, f32[128,256]{1,0:T(8,128)S(1)}, f32[8,256]{1,0:T(8,128)S(1)}, bf16[256,256]{1,0:T(8,128)(2,1)S(1)}) custom-call(s32[2,12]{1,0:T(2,128)S(1)} %get-tuple-element.110.allrefs_0_.pair_in_ref, s32[8,12]{1,0:T(8,128)S(1)} %get-tuple-element.111.allrefs_1_.stoich_in_ref, ...), custom_call_target="tpu_custom_call" | custom-call | tf_op jit(solution)/shard_map/pallas_call | solution.py:324
  34.1 0.2 collective-permute-start.12
  34.3 1.2 %shard_map.120 = (bf16[512,128]{1,0:T(8,128)(2,1)S(1)}, f32[128,256]{1,0:T(8,128)S(1)}, f32[8,256]{1,0:T(8,128)S(1)}) custom-call(s32[2,12]{1,0:T(2,128)S(1)} %get-tuple-element.110.allrefs_0_.pair_in_ref, s32[8,12]{1,0:T(8,128)S(1)} %get-tuple-element.111.allrefs_1_.stoich_in_ref, f32[1,12]{1,0:T(1,128)S(1)} %get-tuple-element.112.allrefs_2_.speed_in_ref, ...), custom_call_target="tpu_custom_call" | custom-call | tf_op jit(solution)/shard_map/pallas_call | solution.py:324
  35.5 0.0 collective-permute-done.12
  35.6 0.5 collective-permute-start.15
  36.2 1.8 %collective-permute-start.14 = (f16[136,256]{1,0:T(8,128)(2,1)S(1)}, f16[136,256]{1,0:T(8,128)(2,1)S(1)}, u32[]{:S(2)}, u32[]{:S(2)}) collective-permute-start(f16[136,256]{1,0:T(8,128)(2,1)S(1)} %pad_maximum_fusion.4), channel_id=1, source_target_pairs={{0,4},{1,5},{2,6},{3,7},{4,0},{5,1},{6,2},{7,3},{8,12},{9,13},{10,... | collective-permute-start | bytes 208904 | tf_op jit(solution)/shard_map/ppermute | solution.py:342
  37.9 1.3 %collective-permute-start.13 = (f16[136,256]{1,0:T(8,128)(2,1)S(1)}, f16[136,256]{1,0:T(8,128)(2,1)S(1)}, u32[]{:S(2)}, u32[]{:S(2)}) collective-permute-start(f16[136,256]{1,0:T(8,128)(2,1)S(1)} %pad_maximum_fusion.4), channel_id=1, source_target_pairs={{0,2},{1,3},{2,0},{3,1},{4,6},{5,7},{6,4},{7,5},{8,10},{9,11},{10,... | collective-permute-start | bytes 208904 | tf_op jit(solution)/shard_map/ppermute | solution.py:342
  39.2 3.2 %shard_map.121 = (bf16[256,256]{1,0:T(8,128)(2,1)S(1)}, bf16[256,256]{1,0:T(8,128)(2,1)S(1)}, f32[256,256]{1,0:T(8,128)S(1)}, f32[8,256]{1,0:T(8,128)S(1)}) custom-call(bf16[256,256]{1,0:T(8,128)(2,1)S(1)} %get-tuple-element.179.coef_ref), custom_call_target="tpu_custom_call" | custom-call | tf_op jit(solution)/shard_map/pallas_call | solution.py:324
  42.4 0.0 collective-permute-done.15
  42.4 0.0 collective-permute-done.14
  42.4 0.1 collective-permute-done.13
  42.6 0.1 multiply_convert_fusion
  42.7 1.8 %collective-permute-start.16 = (f16[136,256]{1,0:T(8,128)(2,1)S(1)}, f16[136,256]{1,0:T(8,128)(2,1)S(1)}, u32[]{:S(2)}, u32[]{:S(2)}) collective-permute-start(f16[136,256]{1,0:T(8,128)(2,1)S(1)} %pad_maximum_fusion.5), channel_id=1, source_target_pairs={{0,8},{1,9},{2,10},{3,11},{4,12},{5,13},{6,14},{7,15},{8,0},{9,1},... | collective-permute-start | bytes 208904 | tf_op jit(solution)/shard_map/ppermute | solution.py:342
  44.5 3.0 %shard_map.122 = (f32[256,256]{1,0:T(8,128)S(1)}, f32[512,256]{1,0:T(8,128)S(1)}) custom-call(f32[8,256]{1,0:T(8,128)S(1)} %get-tuple-element.192.gap_in_ref, bf16[256,256]{1,0:T(8,128)(2,1)S(1)} %get-tuple-element.193.high_ref, bf16[256,256]{1,0:T(8,128)(2,1)S(1)} %get-tuple-element.194.low_ref, f32[256,256]{1,0:T(8,128)S(1)} %get-tuple-element.195.inv_in_ref, ...), custom_call_target="tpu_custom_call" | custom-call | tf_op jit(solution)/shard_map/pallas_call | solution.py:324
  47.5 1.3 %collective-permute-done.16 = f16[136,256]{1,0:T(8,128)(2,1)S(1)} collective-permute-done((f16[136,256]{1,0:T(8,128)(2,1)S(1)}, f16[136,256]{1,0:T(8,128)(2,1)S(1)}, u32[]{:S(2)}, u32[]{:S(2)}) %collective-permute-start.16) | collective-permute-done | bytes 69664 | tf_op jit(solution)/shard_map/ppermute | solution.py:342
  48.9 0.1 collective-permute-start.17
  49.0 0.2 shard_map.123
  49.1 1.2 %collective-permute-done.17 = f32[128,256]{1,0:T(8,128)S(1)} collective-permute-done((f32[128,256]{1,0:T(8,128)S(1)}, f32[128,256]{1,0:T(8,128)S(1)}, u32[]{:S(2)}, u32[]{:S(2)}) %collective-permute-start.17) | collective-permute-done | bytes 131104 | tf_op jit(solution)/shard_map/ppermute | solution.py:342
  50.3 1.6 %shard_map.124 = (f32[512,256]{1,0:T(8,128)}, bf16[16,256]{1,0:T(8,128)(2,1)}) custom-call(f32[512,256]{1,0:T(8,128)S(1)} %get-tuple-element.210.base_ref, bf16[512,256]{1,0:T(8,128)(2,1)S(1)} %get-tuple-element.211.diff_high_ref, bf16[512,256]{1,0:T(8,128)(2,1)S(1)} %get-tuple-element.212.diff_low_ref, bf16[256,256]{1,0:T(8,128)(2,1)S(1)} %get-tuple-element.213.high_ref, ...), custom_call_target="tpu_custom_call" | custom-call | tf_op jit(solution)/shard_map/pallas_call | solution.py:324
  (33 shorter events, 0.5 us)
Async XLA Ops:
  0.6 1.6 %copy-start = (bf16[16,256]{1,0:T(8,128)(2,1)S(1)}, bf16[16,256]{1,0:T(8,128)(2,1)}, u32[]{:S(2)}) copy-start(bf16[16,256]{1,0:T(8,128)(2,1)} %param.11) | copy-start | bytes 24580
  0.6 1.6 %collective-permute-start = (bf16[16,256]{1,0:T(8,128)(2,1)}, bf16[16,256]{1,0:T(8,128)(2,1)S(1)}, u32[]{:S(2)}, u32[]{:S(2)}) collective-permute-start(bf16[16,256]{1,0:T(8,128)(2,1)} %param.11), channel_id=1, source_target_pairs={{0,1},{1,0},{2,3},{3,2},{4,5},{5,4},{6,7},{7,6},{8,9},{9,8},{10,11... | collective-permute-start | bytes 24584 | tf_op jit(solution)/shard_map/ppermute | solution.py:342
  2.2 9.4 %collective-permute-start.4 = (bf16[32,256]{1,0:T(8,128)(2,1)S(1)}, bf16[32,256]{1,0:T(8,128)(2,1)S(1)}, u32[]{:S(2)}, u32[]{:S(2)}) collective-permute-start(bf16[32,256]{1,0:T(8,128)(2,1)S(1)} %maximum_select_fusion.2.allrefs_7_), channel_id=1, source_target_pairs={{0,10},{1,15},{2,8},{3,13},{4,14},{5,11},{6,12},{7,9},{8,2},{9,7},... | collective-permute-start | bytes 49160 | tf_op jit(solution)/shard_map/ppermute | solution.py:342
  7.2 4.6 %collective-permute-start.3 = (bf16[32,256]{1,0:T(8,128)(2,1)S(1)}, bf16[32,256]{1,0:T(8,128)(2,1)S(1)}, u32[]{:S(2)}, u32[]{:S(2)}) collective-permute-start(bf16[32,256]{1,0:T(8,128)(2,1)S(1)} %maximum_select_fusion.2.allrefs_7_), channel_id=1, source_target_pairs={{0,8},{1,13},{2,10},{3,15},{4,12},{5,9},{6,14},{7,11},{8,0},{9,5},... | collective-permute-start | bytes 49160 | tf_op jit(solution)/shard_map/ppermute | solution.py:342
  7.5 4.3 %collective-permute-start.2 = (bf16[32,256]{1,0:T(8,128)(2,1)S(1)}, bf16[32,256]{1,0:T(8,128)(2,1)S(1)}, u32[]{:S(2)}, u32[]{:S(2)}) collective-permute-start(bf16[32,256]{1,0:T(8,128)(2,1)S(1)} %maximum_select_fusion.2.allrefs_7_), channel_id=1, source_target_pairs={{0,4},{1,7},{2,6},{3,5},{4,0},{5,3},{6,2},{7,1},{8,12},{9,15},{10,... | collective-permute-start | bytes 49160 | tf_op jit(solution)/shard_map/ppermute | solution.py:342
  9.1 3.7 %collective-permute-start.1 = (bf16[32,256]{1,0:T(8,128)(2,1)S(1)}, bf16[32,256]{1,0:T(8,128)(2,1)S(1)}, u32[]{:S(2)}, u32[]{:S(2)}) collective-permute-start(bf16[32,256]{1,0:T(8,128)(2,1)S(1)} %maximum_select_fusion.2.allrefs_7_), channel_id=1, source_target_pairs={{0,2},{1,3},{2,0},{3,1},{4,6},{5,7},{6,4},{7,5},{8,10},{9,11},{10,... | collective-permute-start | bytes 49160 | tf_op jit(solution)/shard_map/ppermute | solution.py:342
  12.8 1.3 %collective-permute-start.5 = (bf16[128,256]{1,0:T(8,128)(2,1)S(1)}, bf16[128,256]{1,0:T(8,128)(2,1)S(1)}, u32[]{:S(2)}, u32[]{:S(2)}) collective-permute-start(bf16[128,256]{1,0:T(8,128)(2,1)S(1)} %constant_dynamic-update-slice_fusion.allrefs_8_), channel_id=1, source_target_pairs={{0,1},{1,0},{2,3},{3,2},{4,5},{5,4},{6,7},{7,6},{8,9},{9,8},{10,11... | collective-permute-start | bytes 196616 | tf_op jit(solution)/shard_map/ppermute | solution.py:342
  15.4 1.5 %collective-permute-start.6 = (f32[136,256]{1,0:T(8,128)S(1)}, f32[136,256]{1,0:T(8,128)S(1)}, u32[]{:S(2)}, u32[]{:S(2)}) collective-permute-start(f32[136,256]{1,0:T(8,128)S(1)} %pad_maximum_fusion), channel_id=1, source_target_pairs={{0,1},{1,0},{2,3},{3,2},{4,5},{5,4},{6,7},{7,6},{8,9},{9,8},{10,11... | collective-permute-start | bytes 417800 | tf_op jit(solution)/shard_map/ppermute | solution.py:342
  17.0 6.7 %collective-permute-start.9 = (f16[136,256]{1,0:T(8,128)(2,1)S(1)}, f16[136,256]{1,0:T(8,128)(2,1)S(1)}, u32[]{:S(2)}, u32[]{:S(2)}) collective-permute-start(f16[136,256]{1,0:T(8,128)(2,1)S(1)} %pad_maximum_fusion.2), channel_id=1, source_target_pairs={{0,6},{1,7},{2,4},{3,5},{4,2},{5,3},{6,0},{7,1},{8,14},{9,15},{10,... | collective-permute-start | bytes 208904 | tf_op jit(solution)/shard_map/ppermute | solution.py:342
  17.8 6.0 %collective-permute-start.8 = (f16[136,256]{1,0:T(8,128)(2,1)S(1)}, f16[136,256]{1,0:T(8,128)(2,1)S(1)}, u32[]{:S(2)}, u32[]{:S(2)}) collective-permute-start(f16[136,256]{1,0:T(8,128)(2,1)S(1)} %pad_maximum_fusion.2), channel_id=1, source_target_pairs={{0,4},{1,5},{2,6},{3,7},{4,0},{5,1},{6,2},{7,3},{8,12},{9,13},{10,... | collective-permute-start | bytes 208904 | tf_op jit(solution)/shard_map/ppermute | solution.py:342
  19.1 4.9 %collective-permute-start.7 = (f16[136,256]{1,0:T(8,128)(2,1)S(1)}, f16[136,256]{1,0:T(8,128)(2,1)S(1)}, u32[]{:S(2)}, u32[]{:S(2)}) collective-permute-start(f16[136,256]{1,0:T(8,128)(2,1)S(1)} %pad_maximum_fusion.2), channel_id=1, source_target_pairs={{0,2},{1,3},{2,0},{3,1},{4,6},{5,7},{6,4},{7,5},{8,10},{9,11},{10,... | collective-permute-start | bytes 208904 | tf_op jit(solution)/shard_map/ppermute | solution.py:342
  24.1 6.3 %collective-permute-start.10 = (f16[136,256]{1,0:T(8,128)(2,1)S(1)}, f16[136,256]{1,0:T(8,128)(2,1)S(1)}, u32[]{:S(2)}, u32[]{:S(2)}) collective-permute-start(f16[136,256]{1,0:T(8,128)(2,1)S(1)} %pad_maximum_fusion.3), channel_id=1, source_target_pairs={{0,8},{1,9},{2,10},{3,11},{4,12},{5,13},{6,14},{7,15},{8,0},{9,1},... | collective-permute-start | bytes 208904 | tf_op jit(solution)/shard_map/ppermute | solution.py:342
  30.4 1.4 %collective-permute-start.11 = (f32[128,256]{1,0:T(8,128)S(1)}, f32[128,256]{1,0:T(8,128)S(1)}, u32[]{:S(2)}, u32[]{:S(2)}) collective-permute-start(f32[128,256]{1,0:T(8,128)S(1)} %multiply_add_fusion.1), channel_id=1, source_target_pairs={{0,1},{1,0},{2,3},{3,2},{4,5},{5,4},{6,7},{7,6},{8,9},{9,8},{10,11... | collective-permute-start | bytes 393224 | tf_op jit(solution)/shard_map/ppermute | solution.py:342
  34.1 1.5 %collective-permute-start.12 = (f32[136,256]{1,0:T(8,128)S(1)}, f32[136,256]{1,0:T(8,128)S(1)}, u32[]{:S(2)}, u32[]{:S(2)}) collective-permute-start(f32[136,256]{1,0:T(8,128)S(1)} %pad_maximum_fusion.1), channel_id=1, source_target_pairs={{0,1},{1,0},{2,3},{3,2},{4,5},{5,4},{6,7},{7,6},{8,9},{9,8},{10,11... | collective-permute-start | bytes 417800 | tf_op jit(solution)/shard_map/ppermute | solution.py:342
  35.6 6.8 %collective-permute-start.15 = (f16[136,256]{1,0:T(8,128)(2,1)S(1)}, f16[136,256]{1,0:T(8,128)(2,1)S(1)}, u32[]{:S(2)}, u32[]{:S(2)}) collective-permute-start(f16[136,256]{1,0:T(8,128)(2,1)S(1)} %pad_maximum_fusion.4), channel_id=1, source_target_pairs={{0,6},{1,7},{2,4},{3,5},{4,2},{5,3},{6,0},{7,1},{8,14},{9,15},{10,... | collective-permute-start | bytes 208904 | tf_op jit(solution)/shard_map/ppermute | solution.py:342
  36.2 6.3 %collective-permute-start.14 = (f16[136,256]{1,0:T(8,128)(2,1)S(1)}, f16[136,256]{1,0:T(8,128)(2,1)S(1)}, u32[]{:S(2)}, u32[]{:S(2)}) collective-permute-start(f16[136,256]{1,0:T(8,128)(2,1)S(1)} %pad_maximum_fusion.4), channel_id=1, source_target_pairs={{0,4},{1,5},{2,6},{3,7},{4,0},{5,1},{6,2},{7,3},{8,12},{9,13},{10,... | collective-permute-start | bytes 208904 | tf_op jit(solution)/shard_map/ppermute | solution.py:342
  37.9 4.6 %collective-permute-start.13 = (f16[136,256]{1,0:T(8,128)(2,1)S(1)}, f16[136,256]{1,0:T(8,128)(2,1)S(1)}, u32[]{:S(2)}, u32[]{:S(2)}) collective-permute-start(f16[136,256]{1,0:T(8,128)(2,1)S(1)} %pad_maximum_fusion.4), channel_id=1, source_target_pairs={{0,2},{1,3},{2,0},{3,1},{4,6},{5,7},{6,4},{7,5},{8,10},{9,11},{10,... | collective-permute-start | bytes 208904 | tf_op jit(solution)/shard_map/ppermute | solution.py:342
  42.7 6.1 %collective-permute-start.16 = (f16[136,256]{1,0:T(8,128)(2,1)S(1)}, f16[136,256]{1,0:T(8,128)(2,1)S(1)}, u32[]{:S(2)}, u32[]{:S(2)}) collective-permute-start(f16[136,256]{1,0:T(8,128)(2,1)S(1)} %pad_maximum_fusion.5), channel_id=1, source_target_pairs={{0,8},{1,9},{2,10},{3,11},{4,12},{5,13},{6,14},{7,15},{8,0},{9,1},... | collective-permute-start | bytes 208904 | tf_op jit(solution)/shard_map/ppermute | solution.py:342
  48.9 1.4 %collective-permute-start.17 = (f32[128,256]{1,0:T(8,128)S(1)}, f32[128,256]{1,0:T(8,128)S(1)}, u32[]{:S(2)}, u32[]{:S(2)}) collective-permute-start(f32[128,256]{1,0:T(8,128)S(1)} %multiply_add_fusion), channel_id=1, source_target_pairs={{0,1},{1,0},{2,3},{3,2},{4,5},{5,4},{6,7},{7,6},{8,9},{9,8},{10,11... | collective-permute-start | bytes 393224 | tf_op jit(solution)/shard_map/ppermute | solution.py:342

commit v9 on v8

--- a/solution.py
+++ b/solution.py
@@ -261,44 +261,45 @@
     ).astype(F32)
 
 
-def refine(eye, high_ref, low_ref, inv_ref, gap):
-    square = gap * gap
-    factor = 2.0 / (2.0 - square)
+def widen(room):
+    spread = room * (2.0 - room)
+    return 2.0 * spread / (1.0 + spread), 2.0 / (1.0 + spread)
+
+
+def refine(eye, high_ref, low_ref, inv_ref, room):
+    room, factor = widen(room)
     inv = inv_ref[...]
     halves = split(inv)
     rest = eye - mm3((high_ref[...], low_ref[...]), halves)
     inv_ref[...] = factor * (inv + mm3(halves, split(rest)))
-    return square / (2.0 - square)
-
-
-def inverse_start(ridge, steps, coef_ref, high_ref, low_ref, inv_ref, gap_ref):
+    return room
+
+
+def inverse_start(ridge, steps, coef_ref, high_ref, low_ref, inv_ref, room_ref):
     coef = coef_ref[...]
     eye = identity()
     gram = mm(coef, coef, TN) + ridge * eye
     top = jnp.max(jnp.sum(jnp.abs(gram), axis=0, keepdims=True))
     high_ref[...], low_ref[...] = split(gram)
     scale = 2.0 / (top + ridge)
-    gap = (top - ridge) / (top + ridge)
-    square = gap * gap
-    factor = 2.0 / (2.0 - square)
+    room, factor = widen(ridge * scale)
     inv_ref[...] = (factor * scale) * (2.0 * eye - scale * gram)
-    gap = lax.fori_loop(
-        0, steps, lambda i, gap: refine(eye, high_ref, low_ref, inv_ref, gap),
-        square / (2.0 - square),
-    )
-    gap_ref[...] = jnp.full(gap_ref.shape, gap, F32)
+    room = lax.fori_loop(
+        0, steps, lambda i, room: refine(eye, high_ref, low_ref, inv_ref, room), room
+    )
+    room_ref[...] = jnp.full(room_ref.shape, room, F32)
 
 
 def inverse_end(
-    gap_in_ref, high_ref, low_ref, inv_in_ref, coef_ref, give_ref, keep_ref,
+    room_in_ref, high_ref, low_ref, inv_in_ref, coef_ref, give_ref, keep_ref,
     solve_ref, pull_ref, inv_ref,
 ):
     eye = identity()
     inv_ref[...] = inv_in_ref[...]
     lax.while_loop(
-        lambda gap: gap > 1e-5,
-        lambda gap: refine(eye, high_ref, low_ref, inv_ref, gap),
-        jnp.max(gap_in_ref[...]),
+        lambda room: room < 1.0 - 1e-5,
+        lambda room: refine(eye, high_ref, low_ref, inv_ref, room),
+        jnp.max(room_in_ref[...]),
     )
     coef = coef_ref[...]
     high, low = split(inv_ref[...])

time: 52.1 us -> 52.1 us (level)
  no operation moved by 1% of the time
where the time goes in v9:
time: 52.1 us; the launch traced here: 51.9 us
  Pallas kernels  21.6 us (41%)
  starting transfers between devices  20.1 us (39%)
  waiting for transfers between devices  8.06 us (15%)
  between operations  1.6 us (3%)
  other arithmetic  0.58 us (1%)
    pallas_call x12, Pallas kernels, call(): pl.pallas_call(kernel, in_specs=[pl.BlockSpec(memory_space=pltpu.HBM if i...  21.6 us
    ppermute x18, starting transfers between devices, swap(): lax.ppermute(value, 'col', [(i, i ^ masks[i % 2]) for i in range(n) if ma...  20.1 us
    ppermute x18, waiting for transfers between devices, swap(): lax.ppermute(value, 'col', [(i, i ^ masks[i % 2]) for i in range(n) if ma...  8.06 us
  transfers between devices with their start and end apart: 18, of which 10 were waited for; matrix products, arithmetic and copies ran while one was open for 0% of the time, Pallas kernels for 32%

profile of v9, /device:TPU:0, one launch (start us, length us, event | category | flops | bytes accessed | tf_op | source)
XLA Modules:
  0.0 51.9 jit_solution(2309744746529418360)
XLA Ops:
  0.6 0.0 copy-start
  0.6 0.5 collective-permute-start
  1.2 1.0 %collective-permute-done = bf16[16,256]{1,0:T(8,128)(2,1)S(1)} collective-permute-done((bf16[16,256]{1,0:T(8,128)(2,1)}, bf16[16,256]{1,0:T(8,128)(2,1)S(1)}, u32[]{:S(2)}, u32[]{:S(2)}) %collective-permute-start) | collective-permute-done | bytes 8224 | tf_op jit(solution)/shard_map/ppermute | solution.py:343
  2.2 0.0 copy-done
  2.2 5.0 %collective-permute-start.4 = (bf16[32,256]{1,0:T(8,128)(2,1)S(1)}, bf16[32,256]{1,0:T(8,128)(2,1)S(1)}, u32[]{:S(2)}, u32[]{:S(2)}) collective-permute-start(bf16[32,256]{1,0:T(8,128)(2,1)S(1)} %maximum_select_fusion.2.allrefs_7_), channel_id=1, source_target_pairs={{0,10},{1,15},{2,8},{3,13},{4,14},{5,11},{6,12},{7,9},{8,2},{9,7},... | collective-permute-start | bytes 49160 | tf_op jit(solution)/shard_map/ppermute | solution.py:343
  7.2 0.3 collective-permute-start.3
  7.5 1.6 %collective-permute-start.2 = (bf16[32,256]{1,0:T(8,128)(2,1)S(1)}, bf16[32,256]{1,0:T(8,128)(2,1)S(1)}, u32[]{:S(2)}, u32[]{:S(2)}) collective-permute-start(bf16[32,256]{1,0:T(8,128)(2,1)S(1)} %maximum_select_fusion.2.allrefs_7_), channel_id=1, source_target_pairs={{0,4},{1,7},{2,6},{3,5},{4,0},{5,3},{6,2},{7,1},{8,12},{9,15},{10,... | collective-permute-start | bytes 49160 | tf_op jit(solution)/shard_map/ppermute | solution.py:343
  9.1 0.5 collective-permute-start.1
  10.2 1.3 %shard_map.113 = (s32[2,12]{1,0:T(2,128)S(1)}, s32[8,12]{1,0:T(8,128)S(1)}, f32[1,12]{1,0:T(1,128)S(1)}, f32[1,8]{1,0:T(1,128)S(1)}, f32[512,256]{1,0:T(8,128)S(...) custom-call(s32[2,12]{1,0:T(2,128)} %bitcast.42, s32[8,12]{1,0:T(8,128)} %bitcast.24, ...), custom_call_target="tpu_custom_call" | custom-call | tf_op jit(solution)/shard_map/pallas_call | solution.py:325
  11.6 0.0 collective-permute-done.4
  11.6 0.2 collective-permute-done.3
  11.8 0.0 collective-permute-done.2
  11.8 1.0 %collective-permute-done.1 = bf16[32,256]{1,0:T(8,128)(2,1)S(1)} collective-permute-done((bf16[32,256]{1,0:T(8,128)(2,1)S(1)}, bf16[32,256]{1,0:T(8,128)(2,1)S(1)}, u32[]{:S(2)}, u32[]{:S(2)}) %collective-permute-start.1) | collective-permute-done | bytes 16416 | tf_op jit(solution)/shard_map/ppermute | solution.py:343
  12.8 0.1 collective-permute-start.5
  12.9 1.2 %collective-permute-done.5.allrefs_9_ = bf16[128,256]{1,0:T(8,128)(2,1)S(1)} collective-permute-done((bf16[128,256]{1,0:T(8,128)(2,1)S(1)}, bf16[128,256]{1,0:T(8,128)(2,1)S(1)}, u32[]{:S(2)}, u32[]{:S(2)}) %collective-permute-start.5) | collective-permute-done | bytes 65568 | tf_op jit(solution)/shard_map/ppermute | solution.py:343
  14.2 1.3 %shard_map.114 = (bf16[512,128]{1,0:T(8,128)(2,1)S(1)}, f32[128,256]{1,0:T(8,128)S(1)}, f32[8,256]{1,0:T(8,128)S(1)}, bf16[256,256]{1,0:T(8,128)(2,1)S(1)}) custom-call(s32[2,12]{1,0:T(2,128)S(1)} %get-tuple-element.110.allrefs_0_.pair_in_ref, s32[8,12]{1,0:T(8,128)S(1)} %get-tuple-element.111.allrefs_1_.stoich_in_ref, ...), custom_call_target="tpu_custom_call" | custom-call | tf_op jit(solution)/shard_map/pallas_call | solution.py:325
  15.4 0.2 collective-permute-start.6
  15.7 1.2 %shard_map.115 = (bf16[512,128]{1,0:T(8,128)(2,1)S(1)}, f32[128,256]{1,0:T(8,128)S(1)}, f32[8,256]{1,0:T(8,128)S(1)}) custom-call(s32[2,12]{1,0:T(2,128)S(1)} %get-tuple-element.110.allrefs_0_.pair_in_ref, s32[8,12]{1,0:T(8,128)S(1)} %get-tuple-element.111.allrefs_1_.stoich_in_ref, f32[1,12]{1,0:T(1,128)S(1)} %get-tuple-element.112.allrefs_2_.speed_in_ref, ...), custom_call_target="tpu_custom_call" | custom-call | tf_op jit(solution)/shard_map/pallas_call | solution.py:325
  16.9 0.0 collective-permute-done.6
  17.0 0.8 %collective-permute-start.9 = (f16[136,256]{1,0:T(8,128)(2,1)S(1)}, f16[136,256]{1,0:T(8,128)(2,1)S(1)}, u32[]{:S(2)}, u32[]{:S(2)}) collective-permute-start(f16[136,256]{1,0:T(8,128)(2,1)S(1)} %pad_maximum_fusion.2), channel_id=1, source_target_pairs={{0,6},{1,7},{2,4},{3,5},{4,2},{5,3},{6,0},{7,1},{8,14},{9,15},{10,... | collective-permute-start | bytes 208904 | tf_op jit(solution)/shard_map/ppermute | solution.py:343
  17.8 1.3 %collective-permute-start.8 = (f16[136,256]{1,0:T(8,128)(2,1)S(1)}, f16[136,256]{1,0:T(8,128)(2,1)S(1)}, u32[]{:S(2)}, u32[]{:S(2)}) collective-permute-start(f16[136,256]{1,0:T(8,128)(2,1)S(1)} %pad_maximum_fusion.2), channel_id=1, source_target_pairs={{0,4},{1,5},{2,6},{3,7},{4,0},{5,1},{6,2},{7,3},{8,12},{9,13},{10,... | collective-permute-start | bytes 208904 | tf_op jit(solution)/shard_map/ppermute | solution.py:343
  19.1 1.5 %collective-permute-start.7 = (f16[136,256]{1,0:T(8,128)(2,1)S(1)}, f16[136,256]{1,0:T(8,128)(2,1)S(1)}, u32[]{:S(2)}, u32[]{:S(2)}) collective-permute-start(f16[136,256]{1,0:T(8,128)(2,1)S(1)} %pad_maximum_fusion.2), channel_id=1, source_target_pairs={{0,2},{1,3},{2,0},{3,1},{4,6},{5,7},{6,4},{7,5},{8,10},{9,11},{10,... | collective-permute-start | bytes 208904 | tf_op jit(solution)/shard_map/ppermute | solution.py:343
  20.6 3.2 %shard_map.116 = (bf16[256,256]{1,0:T(8,128)(2,1)S(1)}, bf16[256,256]{1,0:T(8,128)(2,1)S(1)}, f32[256,256]{1,0:T(8,128)S(1)}, f32[8,256]{1,0:T(8,128)S(1)}) custom-call(bf16[256,256]{1,0:T(8,128)(2,1)S(1)} %get-tuple-element.131.coef_ref), custom_call_target="tpu_custom_call" | custom-call | tf_op jit(solution)/shard_map/pallas_call | solution.py:325
  23.8 0.0 collective-permute-done.9
  23.8 0.0 collective-permute-done.8
  23.8 0.1 collective-permute-done.7
  24.0 0.1 multiply_convert_fusion.2
  24.1 2.7 %collective-permute-start.10 = (f16[136,256]{1,0:T(8,128)(2,1)S(1)}, f16[136,256]{1,0:T(8,128)(2,1)S(1)}, u32[]{:S(2)}, u32[]{:S(2)}) collective-permute-start(f16[136,256]{1,0:T(8,128)(2,1)S(1)} %pad_maximum_fusion.3), channel_id=1, source_target_pairs={{0,8},{1,9},{2,10},{3,11},{4,12},{5,13},{6,14},{7,15},{8,0},{9,1},... | collective-permute-start | bytes 208904 | tf_op jit(solution)/shard_map/ppermute | solution.py:343
  26.8 3.0 %shard_map.117 = (f32[256,256]{1,0:T(8,128)S(1)}, f32[512,256]{1,0:T(8,128)S(1)}) custom-call(f32[8,256]{1,0:T(8,128)S(1)} %get-tuple-element.144.room_in_ref, bf16[256,256]{1,0:T(8,128)(2,1)S(1)} %get-tuple-element.145.high_ref, bf16[256,256]{1,0:T(8,128)(2,1)S(1)} %get-tuple-element.146.low_ref, f32[256,256]{1,0:T(8,128)S(1)} %get-tuple-element.147.inv_in_ref, ...), custom_call_target="tpu_custom_call" | custom-call | tf_op jit(solution)/shard_map/pallas_call | solution.py:325
  29.8 0.6 %collective-permute-done.10 = f16[136,256]{1,0:T(8,128)(2,1)S(1)} collective-permute-done((f16[136,256]{1,0:T(8,128)(2,1)S(1)}, f16[136,256]{1,0:T(8,128)(2,1)S(1)}, u32[]{:S(2)}, u32[]{:S(2)}) %collective-permute-start.10) | collective-permute-done | bytes 69664 | tf_op jit(solution)/shard_map/ppermute | solution.py:343
  30.4 0.1 collective-permute-start.11
  30.5 0.2 shard_map.118
  30.6 1.2 %collective-permute-done.11 = f32[128,256]{1,0:T(8,128)S(1)} collective-permute-done((f32[128,256]{1,0:T(8,128)S(1)}, f32[128,256]{1,0:T(8,128)S(1)}, u32[]{:S(2)}, u32[]{:S(2)}) %collective-permute-start.11) | collective-permute-done | bytes 131104 | tf_op jit(solution)/shard_map/ppermute | solution.py:343
  31.8 2.2 %shard_map.119 = (f32[512,256]{1,0:T(8,128)S(1)}, bf16[512,128]{1,0:T(8,128)(2,1)S(1)}, f32[128,256]{1,0:T(8,128)S(1)}, f32[8,256]{1,0:T(8,128)S(1)}, bf16[256,256]{1,0:T(8,128)(2,1)S(1)}) custom-call(s32[2,12]{1,0:T(2,128)S(1)} %get-tuple-element.110.allrefs_0_.pair_in_ref, s32[8,12]{1,0:T(8,128)S(1)} %get-tuple-element.111.allrefs_1_.stoich_in_ref, ...), custom_call_target="tpu_custom_call" | custom-call | tf_op jit(solution)/shard_map/pallas_call | solution.py:325
  34.1 0.2 collective-permute-start.12
  34.3 1.2 %shard_map.120 = (bf16[512,128]{1,0:T(8,128)(2,1)S(1)}, f32[128,256]{1,0:T(8,128)S(1)}, f32[8,256]{1,0:T(8,128)S(1)}) custom-call(s32[2,12]{1,0:T(2,128)S(1)} %get-tuple-element.110.allrefs_0_.pair_in_ref, s32[8,12]{1,0:T(8,128)S(1)} %get-tuple-element.111.allrefs_1_.stoich_in_ref, f32[1,12]{1,0:T(1,128)S(1)} %get-tuple-element.112.allrefs_2_.speed_in_ref, ...), custom_call_target="tpu_custom_call" | custom-call | tf_op jit(solution)/shard_map/pallas_call | solution.py:325
  35.5 0.0 collective-permute-done.12
  35.6 0.5 collective-permute-start.15
  36.2 1.8 %collective-permute-start.14 = (f16[136,256]{1,0:T(8,128)(2,1)S(1)}, f16[136,256]{1,0:T(8,128)(2,1)S(1)}, u32[]{:S(2)}, u32[]{:S(2)}) collective-permute-start(f16[136,256]{1,0:T(8,128)(2,1)S(1)} %pad_maximum_fusion.4), channel_id=1, source_target_pairs={{0,4},{1,5},{2,6},{3,7},{4,0},{5,1},{6,2},{7,3},{8,12},{9,13},{10,... | collective-permute-start | bytes 208904 | tf_op jit(solution)/shard_map/ppermute | solution.py:343
  37.9 1.3 %collective-permute-start.13 = (f16[136,256]{1,0:T(8,128)(2,1)S(1)}, f16[136,256]{1,0:T(8,128)(2,1)S(1)}, u32[]{:S(2)}, u32[]{:S(2)}) collective-permute-start(f16[136,256]{1,0:T(8,128)(2,1)S(1)} %pad_maximum_fusion.4), channel_id=1, source_target_pairs={{0,2},{1,3},{2,0},{3,1},{4,6},{5,7},{6,4},{7,5},{8,10},{9,11},{10,... | collective-permute-start | bytes 208904 | tf_op jit(solution)/shard_map/ppermute | solution.py:343
  39.2 3.2 %shard_map.121 = (bf16[256,256]{1,0:T(8,128)(2,1)S(1)}, bf16[256,256]{1,0:T(8,128)(2,1)S(1)}, f32[256,256]{1,0:T(8,128)S(1)}, f32[8,256]{1,0:T(8,128)S(1)}) custom-call(bf16[256,256]{1,0:T(8,128)(2,1)S(1)} %get-tuple-element.179.coef_ref), custom_call_target="tpu_custom_call" | custom-call | tf_op jit(solution)/shard_map/pallas_call | solution.py:325
  42.4 0.0 collective-permute-done.15
  42.4 0.0 collective-permute-done.14
  42.4 0.1 collective-permute-done.13
  42.6 0.1 multiply_convert_fusion
  42.7 1.8 %collective-permute-start.16 = (f16[136,256]{1,0:T(8,128)(2,1)S(1)}, f16[136,256]{1,0:T(8,128)(2,1)S(1)}, u32[]{:S(2)}, u32[]{:S(2)}) collective-permute-start(f16[136,256]{1,0:T(8,128)(2,1)S(1)} %pad_maximum_fusion.5), channel_id=1, source_target_pairs={{0,8},{1,9},{2,10},{3,11},{4,12},{5,13},{6,14},{7,15},{8,0},{9,1},... | collective-permute-start | bytes 208904 | tf_op jit(solution)/shard_map/ppermute | solution.py:343
  44.5 3.0 %shard_map.122 = (f32[256,256]{1,0:T(8,128)S(1)}, f32[512,256]{1,0:T(8,128)S(1)}) custom-call(f32[8,256]{1,0:T(8,128)S(1)} %get-tuple-element.192.room_in_ref, bf16[256,256]{1,0:T(8,128)(2,1)S(1)} %get-tuple-element.193.high_ref, bf16[256,256]{1,0:T(8,128)(2,1)S(1)} %get-tuple-element.194.low_ref, f32[256,256]{1,0:T(8,128)S(1)} %get-tuple-element.195.inv_in_ref, ...), custom_call_target="tpu_custom_call" | custom-call | tf_op jit(solution)/shard_map/pallas_call | solution.py:325
  47.5 1.3 %collective-permute-done.16 = f16[136,256]{1,0:T(8,128)(2,1)S(1)} collective-permute-done((f16[136,256]{1,0:T(8,128)(2,1)S(1)}, f16[136,256]{1,0:T(8,128)(2,1)S(1)}, u32[]{:S(2)}, u32[]{:S(2)}) %collective-permute-start.16) | collective-permute-done | bytes 69664 | tf_op jit(solution)/shard_map/ppermute | solution.py:343
  48.9 0.1 collective-permute-start.17
  49.0 0.2 shard_map.123
  49.1 1.2 %collective-permute-done.17 = f32[128,256]{1,0:T(8,128)S(1)} collective-permute-done((f32[128,256]{1,0:T(8,128)S(1)}, f32[128,256]{1,0:T(8,128)S(1)}, u32[]{:S(2)}, u32[]{:S(2)}) %collective-permute-start.17) | collective-permute-done | bytes 131104 | tf_op jit(solution)/shard_map/ppermute | solution.py:343
  50.3 1.6 %shard_map.124 = (f32[512,256]{1,0:T(8,128)}, bf16[16,256]{1,0:T(8,128)(2,1)}) custom-call(f32[512,256]{1,0:T(8,128)S(1)} %get-tuple-element.210.base_ref, bf16[512,256]{1,0:T(8,128)(2,1)S(1)} %get-tuple-element.211.diff_high_ref, bf16[512,256]{1,0:T(8,128)(2,1)S(1)} %get-tuple-element.212.diff_low_ref, bf16[256,256]{1,0:T(8,128)(2,1)S(1)} %get-tuple-element.213.high_ref, ...), custom_call_target="tpu_custom_call" | custom-call | tf_op jit(solution)/shard_map/pallas_call | solution.py:325
  (33 shorter events, 0.5 us)
Async XLA Ops:
  0.6 1.6 %copy-start = (bf16[16,256]{1,0:T(8,128)(2,1)S(1)}, bf16[16,256]{1,0:T(8,128)(2,1)}, u32[]{:S(2)}) copy-start(bf16[16,256]{1,0:T(8,128)(2,1)} %param.11) | copy-start | bytes 24580
  0.6 1.6 %collective-permute-start = (bf16[16,256]{1,0:T(8,128)(2,1)}, bf16[16,256]{1,0:T(8,128)(2,1)S(1)}, u32[]{:S(2)}, u32[]{:S(2)}) collective-permute-start(bf16[16,256]{1,0:T(8,128)(2,1)} %param.11), channel_id=1, source_target_pairs={{0,1},{1,0},{2,3},{3,2},{4,5},{5,4},{6,7},{7,6},{8,9},{9,8},{10,11... | collective-permute-start | bytes 24584 | tf_op jit(solution)/shard_map/ppermute | solution.py:343
  2.2 9.4 %collective-permute-start.4 = (bf16[32,256]{1,0:T(8,128)(2,1)S(1)}, bf16[32,256]{1,0:T(8,128)(2,1)S(1)}, u32[]{:S(2)}, u32[]{:S(2)}) collective-permute-start(bf16[32,256]{1,0:T(8,128)(2,1)S(1)} %maximum_select_fusion.2.allrefs_7_), channel_id=1, source_target_pairs={{0,10},{1,15},{2,8},{3,13},{4,14},{5,11},{6,12},{7,9},{8,2},{9,7},... | collective-permute-start | bytes 49160 | tf_op jit(solution)/shard_map/ppermute | solution.py:343
  7.2 4.6 %collective-permute-start.3 = (bf16[32,256]{1,0:T(8,128)(2,1)S(1)}, bf16[32,256]{1,0:T(8,128)(2,1)S(1)}, u32[]{:S(2)}, u32[]{:S(2)}) collective-permute-start(bf16[32,256]{1,0:T(8,128)(2,1)S(1)} %maximum_select_fusion.2.allrefs_7_), channel_id=1, source_target_pairs={{0,8},{1,13},{2,10},{3,15},{4,12},{5,9},{6,14},{7,11},{8,0},{9,5},... | collective-permute-start | bytes 49160 | tf_op jit(solution)/shard_map/ppermute | solution.py:343
  7.5 4.3 %collective-permute-start.2 = (bf16[32,256]{1,0:T(8,128)(2,1)S(1)}, bf16[32,256]{1,0:T(8,128)(2,1)S(1)}, u32[]{:S(2)}, u32[]{:S(2)}) collective-permute-start(bf16[32,256]{1,0:T(8,128)(2,1)S(1)} %maximum_select_fusion.2.allrefs_7_), channel_id=1, source_target_pairs={{0,4},{1,7},{2,6},{3,5},{4,0},{5,3},{6,2},{7,1},{8,12},{9,15},{10,... | collective-permute-start | bytes 49160 | tf_op jit(solution)/shard_map/ppermute | solution.py:343
  9.1 3.7 %collective-permute-start.1 = (bf16[32,256]{1,0:T(8,128)(2,1)S(1)}, bf16[32,256]{1,0:T(8,128)(2,1)S(1)}, u32[]{:S(2)}, u32[]{:S(2)}) collective-permute-start(bf16[32,256]{1,0:T(8,128)(2,1)S(1)} %maximum_select_fusion.2.allrefs_7_), channel_id=1, source_target_pairs={{0,2},{1,3},{2,0},{3,1},{4,6},{5,7},{6,4},{7,5},{8,10},{9,11},{10,... | collective-permute-start | bytes 49160 | tf_op jit(solution)/shard_map/ppermute | solution.py:343
  12.8 1.3 %collective-permute-start.5 = (bf16[128,256]{1,0:T(8,128)(2,1)S(1)}, bf16[128,256]{1,0:T(8,128)(2,1)S(1)}, u32[]{:S(2)}, u32[]{:S(2)}) collective-permute-start(bf16[128,256]{1,0:T(8,128)(2,1)S(1)} %constant_dynamic-update-slice_fusion.allrefs_8_), channel_id=1, source_target_pairs={{0,1},{1,0},{2,3},{3,2},{4,5},{5,4},{6,7},{7,6},{8,9},{9,8},{10,11... | collective-permute-start | bytes 196616 | tf_op jit(solution)/shard_map/ppermute | solution.py:343
  15.4 1.5 %collective-permute-start.6 = (f32[136,256]{1,0:T(8,128)S(1)}, f32[136,256]{1,0:T(8,128)S(1)}, u32[]{:S(2)}, u32[]{:S(2)}) collective-permute-start(f32[136,256]{1,0:T(8,128)S(1)} %pad_maximum_fusion), channel_id=1, source_target_pairs={{0,1},{1,0},{2,3},{3,2},{4,5},{5,4},{6,7},{7,6},{8,9},{9,8},{10,11... | collective-permute-start | bytes 417800 | tf_op jit(solution)/shard_map/ppermute | solution.py:343
  17.0 6.7 %collective-permute-start.9 = (f16[136,256]{1,0:T(8,128)(2,1)S(1)}, f16[136,256]{1,0:T(8,128)(2,1)S(1)}, u32[]{:S(2)}, u32[]{:S(2)}) collective-permute-start(f16[136,256]{1,0:T(8,128)(2,1)S(1)} %pad_maximum_fusion.2), channel_id=1, source_target_pairs={{0,6},{1,7},{2,4},{3,5},{4,2},{5,3},{6,0},{7,1},{8,14},{9,15},{10,... | collective-permute-start | bytes 208904 | tf_op jit(solution)/shard_map/ppermute | solution.py:343
  17.8 6.0 %collective-permute-start.8 = (f16[136,256]{1,0:T(8,128)(2,1)S(1)}, f16[136,256]{1,0:T(8,128)(2,1)S(1)}, u32[]{:S(2)}, u32[]{:S(2)}) collective-permute-start(f16[136,256]{1,0:T(8,128)(2,1)S(1)} %pad_maximum_fusion.2), channel_id=1, source_target_pairs={{0,4},{1,5},{2,6},{3,7},{4,0},{5,1},{6,2},{7,3},{8,12},{9,13},{10,... | collective-permute-start | bytes 208904 | tf_op jit(solution)/shard_map/ppermute | solution.py:343
  19.1 4.9 %collective-permute-start.7 = (f16[136,256]{1,0:T(8,128)(2,1)S(1)}, f16[136,256]{1,0:T(8,128)(2,1)S(1)}, u32[]{:S(2)}, u32[]{:S(2)}) collective-permute-start(f16[136,256]{1,0:T(8,128)(2,1)S(1)} %pad_maximum_fusion.2), channel_id=1, source_target_pairs={{0,2},{1,3},{2,0},{3,1},{4,6},{5,7},{6,4},{7,5},{8,10},{9,11},{10,... | collective-permute-start | bytes 208904 | tf_op jit(solution)/shard_map/ppermute | solution.py:343
  24.1 6.3 %collective-permute-start.10 = (f16[136,256]{1,0:T(8,128)(2,1)S(1)}, f16[136,256]{1,0:T(8,128)(2,1)S(1)}, u32[]{:S(2)}, u32[]{:S(2)}) collective-permute-start(f16[136,256]{1,0:T(8,128)(2,1)S(1)} %pad_maximum_fusion.3), channel_id=1, source_target_pairs={{0,8},{1,9},{2,10},{3,11},{4,12},{5,13},{6,14},{7,15},{8,0},{9,1},... | collective-permute-start | bytes 208904 | tf_op jit(solution)/shard_map/ppermute | solution.py:343
  30.4 1.4 %collective-permute-start.11 = (f32[128,256]{1,0:T(8,128)S(1)}, f32[128,256]{1,0:T(8,128)S(1)}, u32[]{:S(2)}, u32[]{:S(2)}) collective-permute-start(f32[128,256]{1,0:T(8,128)S(1)} %multiply_add_fusion.1), channel_id=1, source_target_pairs={{0,1},{1,0},{2,3},{3,2},{4,5},{5,4},{6,7},{7,6},{8,9},{9,8},{10,11... | collective-permute-start | bytes 393224 | tf_op jit(solution)/shard_map/ppermute | solution.py:343
  34.1 1.5 %collective-permute-start.12 = (f32[136,256]{1,0:T(8,128)S(1)}, f32[136,256]{1,0:T(8,128)S(1)}, u32[]{:S(2)}, u32[]{:S(2)}) collective-permute-start(f32[136,256]{1,0:T(8,128)S(1)} %pad_maximum_fusion.1), channel_id=1, source_target_pairs={{0,1},{1,0},{2,3},{3,2},{4,5},{5,4},{6,7},{7,6},{8,9},{9,8},{10,11... | collective-permute-start | bytes 417800 | tf_op jit(solution)/shard_map/ppermute | solution.py:343
  35.6 6.8 %collective-permute-start.15 = (f16[136,256]{1,0:T(8,128)(2,1)S(1)}, f16[136,256]{1,0:T(8,128)(2,1)S(1)}, u32[]{:S(2)}, u32[]{:S(2)}) collective-permute-start(f16[136,256]{1,0:T(8,128)(2,1)S(1)} %pad_maximum_fusion.4), channel_id=1, source_target_pairs={{0,6},{1,7},{2,4},{3,5},{4,2},{5,3},{6,0},{7,1},{8,14},{9,15},{10,... | collective-permute-start | bytes 208904 | tf_op jit(solution)/shard_map/ppermute | solution.py:343
  36.2 6.3 %collective-permute-start.14 = (f16[136,256]{1,0:T(8,128)(2,1)S(1)}, f16[136,256]{1,0:T(8,128)(2,1)S(1)}, u32[]{:S(2)}, u32[]{:S(2)}) collective-permute-start(f16[136,256]{1,0:T(8,128)(2,1)S(1)} %pad_maximum_fusion.4), channel_id=1, source_target_pairs={{0,4},{1,5},{2,6},{3,7},{4,0},{5,1},{6,2},{7,3},{8,12},{9,13},{10,... | collective-permute-start | bytes 208904 | tf_op jit(solution)/shard_map/ppermute | solution.py:343
  37.9 4.6 %collective-permute-start.13 = (f16[136,256]{1,0:T(8,128)(2,1)S(1)}, f16[136,256]{1,0:T(8,128)(2,1)S(1)}, u32[]{:S(2)}, u32[]{:S(2)}) collective-permute-start(f16[136,256]{1,0:T(8,128)(2,1)S(1)} %pad_maximum_fusion.4), channel_id=1, source_target_pairs={{0,2},{1,3},{2,0},{3,1},{4,6},{5,7},{6,4},{7,5},{8,10},{9,11},{10,... | collective-permute-start | bytes 208904 | tf_op jit(solution)/shard_map/ppermute | solution.py:343
  42.7 6.1 %collective-permute-start.16 = (f16[136,256]{1,0:T(8,128)(2,1)S(1)}, f16[136,256]{1,0:T(8,128)(2,1)S(1)}, u32[]{:S(2)}, u32[]{:S(2)}) collective-permute-start(f16[136,256]{1,0:T(8,128)(2,1)S(1)} %pad_maximum_fusion.5), channel_id=1, source_target_pairs={{0,8},{1,9},{2,10},{3,11},{4,12},{5,13},{6,14},{7,15},{8,0},{9,1},... | collective-permute-start | bytes 208904 | tf_op jit(solution)/shard_map/ppermute | solution.py:343
  48.9 1.4 %collective-permute-start.17 = (f32[128,256]{1,0:T(8,128)S(1)}, f32[128,256]{1,0:T(8,128)S(1)}, u32[]{:S(2)}, u32[]{:S(2)}) collective-permute-start(f32[128,256]{1,0:T(8,128)S(1)} %multiply_add_fusion), channel_id=1, source_target_pairs={{0,1},{1,0},{2,3},{3,2},{4,5},{5,4},{6,7},{7,6},{8,9},{9,8},{10,11... | collective-permute-start | bytes 393224 | tf_op jit(solution)/shard_map/ppermute | solution.py:343
